TPU v7x, 32 devices: a whole 2x2x4 slice. The times are simulated.
32 devices in a mesh: seq: 8 (over z, y), dp: 4 (over x, core).
Axes of the slice: x: 2, y: 2, z: 4, core: 2. Of those that a mesh axis runs over, the one named last changes fastest.
Arguments:
- queries: bfloat16 [1024, 8192], P('seq', 'dp'), may hold values from -6 to 6
- keys: bfloat16 [1024, 8192], P('seq', 'dp'), may hold values from -0.59765625 to 0.59765625
- values: bfloat16 [1024, 8192], P('seq', 'dp'), may hold values from -6 to 6
- output_gradient: bfloat16 [1024, 8192], P('seq', 'dp'), may hold values from -6 to 6
- log_decay: float32 [64, 1024], P('dp', 'seq'), may hold values from -1 to 0, as said below
- gain: float32 [8192], P('dp'), may hold values from 0.1 to 1.9
Outputs:
- query_grad: bfloat16 [1024, 8192], P('seq', 'dp')
- key_grad: bfloat16 [1024, 8192], P('seq', 'dp')
- value_grad: bfloat16 [1024, 8192], P('seq', 'dp')
- gain_grad: float32 [8192], P('dp')
Inputs may be any that keep to these rules, and one draw needn't show every extreme that they name: `log_decay`: negative at every token and head.
All inputs are finite; a program needn't handle non-finite values.
Results may differ from a plain program's by a relative error of at most 0.005.
Values sent between devices are 32-bit elements; how exact they have to be, the bound alone decides.
No kernel may reach another device: no remote copies, remote signals or barrier semaphores. Data moves between devices by JAX's collectives and lax.ppermute only.
A program may use at most 128 MiB of HBM per device.

v0:
```python
import jax
import jax.numpy as jnp
from jax import lax
from jax.sharding import PartitionSpec as P

epsilon = 1e-05
highest = lax.Precision.HIGHEST


def entering(value, axis, join, neutral, backward):
    count, mine = (lax.axis_size(axis), lax.axis_index(axis))
    pieces = jax.tree.map(lambda part: lax.all_gather(part, axis), value)
    if backward:
        pieces = jax.tree.map(lambda part: part[::-1], pieces)
        mine = count - 1 - mine
    subtotal = jax.tree.map(
        lambda part, zero: jnp.full_like(part, 0) + jnp.asarray(zero, part.dtype), value, neutral
    )

    def turn(position, subtotal):
        longer = join(subtotal, jax.tree.map(lambda part: part[position], pieces))
        return jax.tree.map(lambda new, old: jnp.where(position < mine, new, old), longer, subtotal)

    return lax.fori_loop(0, count - 1, turn, subtotal)


def forward_combine(earlier, later):
    return (earlier[0] * later[0], later[0][:, None] * earlier[1] + later[1])


def backward_combine(earlier, later):
    return (earlier[0] * later[0], later[1] + later[0][:, None] * earlier[1])


def on_device(queries, keys, values, output_gradient, log_decay, gain):
    tok_count = queries.shape[0]
    width = queries.shape[1]
    heads = log_decay.shape[0]
    head_dim = width // heads
    full_width = width * lax.axis_size("dp")
    query_rows = queries.reshape(tok_count, heads, head_dim)
    key_rows = keys.reshape(tok_count, heads, head_dim)
    value_rows = values.reshape(tok_count, heads, head_dim)
    cumulative = jnp.cumsum(log_decay, axis=1)
    last = cumulative[:, -1]
    row_index = lax.broadcasted_iota(jnp.int32, (tok_count, tok_count), 0)
    col_index = lax.broadcasted_iota(jnp.int32, (tok_count, tok_count), 1)
    causal_mask = row_index >= col_index
    weights = jnp.where(
        causal_mask[None],
        jnp.exp(jnp.minimum(cumulative[:, :, None] - cumulative[:, None, :], 0.0)),
        0.0,
    )
    tail_t = jnp.exp(last[:, None] - cumulative).T[:, :, None]
    lead_t = jnp.exp(cumulative).T[:, :, None]
    total_decay = jnp.exp(last)
    key_f = key_rows.astype(jnp.float32)
    value_f = value_rows.astype(jnp.float32)
    query_f = query_rows.astype(jnp.float32)
    local_state = jnp.einsum("thd,the->hde", key_f * tail_t, value_f, precision=highest)
    local_state = local_state.reshape(heads, head_dim * head_dim)
    identity = (
        jnp.ones((heads,), jnp.float32),
        jnp.zeros((heads, head_dim * head_dim), jnp.float32),
    )
    incoming = entering((total_decay, local_state), "seq", forward_combine, identity, False)[1]
    incoming = incoming.reshape(heads, head_dim, head_dim)
    similarity_matrix = jnp.einsum(
        "thd,shd->hts", query_rows, key_rows, preferred_element_type=jnp.float32
    )
    mixed = (similarity_matrix * weights).astype(jnp.bfloat16)
    inner = jnp.einsum("hts,shd->thd", mixed, value_rows, preferred_element_type=jnp.float32)
    outer = jnp.einsum("thd,hde->the", query_f, incoming, precision=highest) * lead_t
    attn = (inner + outer).reshape(tok_count, width)
    grad_f = output_gradient.astype(jnp.float32)
    multiplied_entries = grad_f * gain
    square_sum, cross_sum = lax.psum(
        (jnp.sum(attn * attn, axis=-1), jnp.sum(multiplied_entries * attn, axis=-1)), "dp"
    )
    inv_rms = lax.rsqrt(square_sum / full_width + epsilon)[:, None]
    normed = attn * inv_rms
    cross_mean = inv_rms * (cross_sum / full_width)[:, None]
    d_attn = (inv_rms * (multiplied_entries - normed * cross_mean)).astype(jnp.bfloat16)
    gain_part = jnp.sum(grad_f * normed, axis=0)
    d_attn_rows = d_attn.reshape(tok_count, heads, head_dim)
    d_attn_f = d_attn_rows.astype(jnp.float32)
    local_back = jnp.einsum("thd,the->hde", query_f * lead_t, d_attn_f, precision=highest)
    local_back = local_back.reshape(heads, head_dim * head_dim)
    later = entering((total_decay, local_back), "seq", backward_combine, identity, True)[1]
    later = later.reshape(heads, head_dim, head_dim)
    dprod = jnp.einsum("thd,shd->hts", d_attn_rows, value_rows, preferred_element_type=jnp.float32)
    graded = (dprod * weights).astype(jnp.bfloat16)
    query_grad = jnp.einsum("hts,shd->thd", graded, key_rows, preferred_element_type=jnp.float32)
    query_grad = (
        query_grad + jnp.einsum("the,hde->thd", d_attn_f, incoming, precision=highest) * lead_t
    )
    key_grad = jnp.einsum("hts,thd->shd", graded, query_rows, preferred_element_type=jnp.float32)
    key_grad = key_grad + jnp.einsum("the,hde->thd", value_f, later, precision=highest) * tail_t
    value_grad = jnp.einsum("hts,thd->shd", mixed, d_attn_rows, preferred_element_type=jnp.float32)
    value_grad = value_grad + jnp.einsum("thd,hde->the", key_f, later, precision=highest) * tail_t
    gain_grad = lax.psum(gain_part, "seq")
    return (
        query_grad.reshape(tok_count, width).astype(jnp.bfloat16),
        key_grad.reshape(tok_count, width).astype(jnp.bfloat16),
        value_grad.reshape(tok_count, width).astype(jnp.bfloat16),
        gain_grad,
    )


def solution(mesh):
    return jax.shard_map(
        on_device,
        mesh=mesh,
        in_specs=(
            P("seq", "dp"),
            P("seq", "dp"),
            P("seq", "dp"),
            P("seq", "dp"),
            P("dp", "seq"),
            P("dp"),
        ),
        out_specs=(P("seq", "dp"), P("seq", "dp"), P("seq", "dp"), P("dp")),
        check_vma=False,
    )
```

profile of v0, /device:TPU:0, one launch (start us, length us, event | category | flops | bytes accessed | tf_op | source)
XLA Modules:
  0.0 335.3 jit_solution(1112312301518841867)
XLA Ops:
  14.0 23.7 %all-reduce = f32[128]{0:T(128)S(1)} all-reduce(f32[128]{0:T(128)S(1)} %dynamic-update-slice), channel_id=2, replica_groups=mesh['seq'=8,'dp'=4] {'seq'}, use_global_device_ids=true, to_apply=%add | all-reduce | flops 128 | bytes 1024
  40.6 98.8 %all-gather.4.cloned.1.call-done = f32[8,16,16384]{2,1,0:T(8,128)} async-done(((f32[1,16,16384]{2,1,0:T(8,128)}), f32[8,16,16384]{2,1,0:T(8,128)}) %all-gather.4.cloned.1.call-update) | async-done | bytes 8388624 | tf_op jit(solution)/shard_map/all_gather | solution.py:12
  139.3 11.1 %while.28 = (s32[]{:T(128)}, f32[16,16384]{1,0:T(8,128)S(1)}, s32[]{:T(128)}, f32[8,16]{1,0:T(8,128)S(1)}, f32[8,16,16384]{2,1,0:T(8,128)}, /*index=5*/s32[]{:T(128)}, s32[]{:T(128)}) while((s32[]{:T(128)}, f32[16,16384]{1,0:T(8,128)S(1)}, s32[]{:T(128)}, f32[8,16]{1,0:T(8,128)S(1)}, f32[8,16,16384]{2,1,0:T(8,128)}, ...), condition=%wide.region_2.3_spmd.clone, body=%wide.region_1.2_spmd.clone.sunk | while | flops 1048580 | bytes 3146025 | solution.py:24
  140.9 1.6 fusion.61
  142.5 1.6 fusion.61
  144.1 1.6 fusion.61
  145.7 1.6 fusion.61
  147.3 1.6 fusion.61
  148.9 1.6 fusion.61
  150.7 2.0 fusion.9
  152.7 2.5 multiply_reduce_fusion
  155.2 5.8 %psum.21 = f32[128]{0:T(128)S(1)} all-reduce(f32[128]{0:T(128)S(1)} %get-tuple-element.268), channel_id=1, replica_groups=mesh['seq'=8,'dp'=4] {'dp'}, use_global_device_ids=true, to_apply=%region_4.5 | all-reduce | flops 128 | bytes 1024 | tf_op jit(solution)/shard_map/psum | solution.py:77
  161.0 1.6 copy.60
  164.0 6.4 %psum.22 = f32[128]{0:T(128)S(1)} all-reduce(f32[128]{0:T(128)S(1)} %get-tuple-element.243), channel_id=1, replica_groups=mesh['seq'=8,'dp'=4] {'dp'}, use_global_device_ids=true, to_apply=%region_6.7 | all-reduce | flops 128 | bytes 1024 | tf_op jit(solution)/shard_map/psum | solution.py:77
  170.4 2.1 fusion.19
  173.8 3.5 %fusion.21 = f32[16,128,128]{2,1,0:T(8,128)} fusion(bf16[128,16,128]{0,2,1:T(8,128)(2,1)S(1)} %bitcast.130, bf16[128,16,128]{0,2,1:T(8,128)(2,1)} %bitcast.128, f32[128,16]{0,1:T(8,128)S(1)} %get-tuple-element.266), kind=kOutput, calls=%fused_computation.37 | convolution fusion | flops 403177472 | bytes 2105344 | tf_op jit(solution)/shard_map/thd,the->hde/dot_general | solution.py:87
  177.3 2.4 all_gather_reshape.7
  179.7 1.6 fusion.11
  181.4 1.8 fusion.8
  184.8 21.3 %psum.23 = f32[2048]{0:T(1024)} all-reduce(f32[2048]{0:T(1024)S(1)} %get-tuple-element.242), channel_id=1, replica_groups=mesh['seq'=8,'dp'=4] {'seq'}, use_global_device_ids=true, to_apply=%region_10.11 | all-reduce | flops 2048 | bytes 16384 | tf_op jit(solution)/shard_map/psum | solution.py:101
  206.1 96.6 %all-gather.6.cloned.1.call-done = f32[8,16,16384]{2,1,0:T(8,128)} async-done(((f32[1,16,16384]{2,1,0:T(8,128)}), f32[8,16,16384]{2,1,0:T(8,128)}) %all-gather.6.cloned.1.call-update) | async-done | bytes 8388624 | tf_op jit(solution)/shard_map/all_gather | solution.py:12
  302.7 7.4 %rev.6 = f32[8,16,16384]{2,1,0:T(8,128)} reverse(f32[8,16,16384]{2,1,0:T(8,128)} %all-gather.6.cloned.1.call-done), dimensions={0} | reverse | bytes 16777216 | tf_op jit(solution)/shard_map/rev | solution.py:14
  310.1 11.2 %while.29 = (s32[]{:T(128)}, f32[16,16384]{1,0:T(8,128)S(1)}, s32[]{:T(128)}, f32[8,16,16384]{2,1,0:T(8,128)}, f32[8,16]{1,0:T(8,128)S(1)}, /*index=5*/s32[]{:T(128)}, s32[]{:T(128)}) while((s32[]{:T(128)}, f32[16,16384]{1,0:T(8,128)S(1)}, s32[]{:T(128)}, f32[8,16,16384]{2,1,0:T(8,128)}, f32[8,16]{1,0:T(8,128)S(1)}, ...), condition=%wide.region_8.9_spmd.clone, body=%wide.region_7.8_spmd.clone.sunk | while | flops 1048580 | bytes 3146025 | solution.py:24
  310.1 1.6 fusion.62
  (69 shorter events, 31.4 us)
Async XLA Ops:
  7.2 2.7 copy-start
  7.2 132.1 %all-gather.4.cloned.1.call-start = ((), (), s32[]{:S(2)}) async-start(), calls=%async_computation | async-start | bytes 9437184 | tf_op jit(solution)/shard_map/all_gather | solution.py:12
  11.8 290.8 %all-gather.6.cloned.1.call-start = ((), (), s32[]{:S(2)}) async-start(), calls=%async_computation.1 | async-start | bytes 9437184 | tf_op jit(solution)/shard_map/all_gather | solution.py:12
  39.2 100.1 %copy-start.1 = (bf16[128,2048]{0,1:T(8,128)(2,1)}, bf16[128,2048]{0,1:T(8,128)(2,1)S(1)}, u32[]{:S(2)}) copy-start(bf16[128,2048]{0,1:T(8,128)(2,1)S(1)} %copy.52) | copy-start | bytes 1572868
  150.4 12.2 %copy-start.6 = (f32[2048]{0:T(1024)S(1)}, f32[2048]{0:T(1024)}, u32[]{:S(2)}) copy-start(f32[2048]{0:T(1024)} %param.15) | copy-start | bytes 24580
  173.8 5.9 %copy-start.3 = (bf16[128,2048]{0,1:T(8,128)(2,1)}, bf16[128,2048]{0,1:T(8,128)(2,1)S(1)}, u32[]{:S(2)}) copy-start(bf16[128,2048]{0,1:T(8,128)(2,1)S(1)} %copy.79) | copy-start | bytes 1572868
  181.4 2.4 copy-start.5
  310.1 13.6 %copy-start.4 = (bf16[128,2048]{0,1:T(8,128)(2,1)S(1)}, bf16[128,2048]{0,1:T(8,128)(2,1)}, u32[]{:S(2)}) copy-start(bf16[128,2048]{0,1:T(8,128)(2,1)} %copy-done.3) | copy-start | bytes 1572868
  321.3 4.8 %copy-start.2 = (bf16[128,2048]{0,1:T(8,128)(2,1)S(1)}, bf16[128,2048]{0,1:T(8,128)(2,1)}, u32[]{:S(2)}) copy-start(bf16[128,2048]{0,1:T(8,128)(2,1)} %copy-done.1) | copy-start | bytes 1572868
Sparse Core Ops, SparseCore 0:
  11.9 127.3 all-gather.3
  179.8 122.7 all-gather.5
where the time goes:
time: 337 us; the launch traced here: 335 us
  waiting for transfers between devices  195 us (58%)
  blocking collectives  57.3 us (17%)
  other arithmetic  26.4 us (8%)
  local copies, waits for them, and re-layouts  21.9 us (6%)
  matrix products  18.9 us (6%)
  between operations  15 us (4%)
    all_gather x2, waiting for transfers between devices, entering(): pieces = jax.tree.map(lambda part: lax.all_gather(part, axis), value)  195 us
    unnamed x1, blocking collectives  23.7 us
    select_n x14, other arithmetic, turn(): jnp.where(position < mine, new, old)  21.8 us
    psum x1, blocking collectives, on_device(): gain_grad = lax.psum(gain_part, 'seq')  21.3 us
    psum x2, blocking collectives, on_device(): lax.psum((jnp.sum(attn * attn, axis=-1), jnp.sum(multiplied_entries * att...  12.2 us
    unnamed x24, local copies, waits for them, and re-layouts  7.6 us
    rev x2, local copies, waits for them, and re-layouts, entering(): pieces = jax.tree.map(lambda part: part[::-1], pieces)  7.42 us
  transfers between devices with their start and end apart: 2, of which 2 were waited for; matrix products, arithmetic and copies ran while one was open for 3% of the time, Pallas kernels for 0%

commit v1 on v0

v1 whole, which is shorter than its diff:
```python
import functools

import jax
import jax.numpy as jnp
from jax import lax
from jax.experimental import pallas as pl
from jax.experimental.pallas import tpu as pltpu
from jax.sharding import PartitionSpec as P

epsilon = 1e-05
highest = lax.Precision.HIGHEST
f32 = jnp.float32
bf16 = jnp.bfloat16
VMEM = pl.BlockSpec(memory_space=pltpu.VMEM)
SMEM = pl.BlockSpec(memory_space=pltpu.SMEM)
GRANT = 24 * 2**20


def call(body, outs, flops, moved, name):
    def run(side, *arrays):
        return pl.pallas_call(
            body,
            out_shape=[jax.ShapeDtypeStruct(*o) for o in outs],
            in_specs=[SMEM] + [VMEM] * len(arrays),
            out_specs=[VMEM] * len(outs),
            compiler_params=pltpu.CompilerParams(vmem_limit_bytes=GRANT),
            cost_estimate=pl.CostEstimate(flops=flops, bytes_accessed=moved, transcendentals=0),
            name=name,
        )(side, *arrays)

    return run


def dot(a, b, ca, cb):
    return lax.dot_general(a, b, (((ca,), (cb,)), ((), ())), preferred_element_type=f32)


def split(x):
    hi = x.astype(bf16)
    return hi, (x - hi.astype(f32)).astype(bf16)


def column(table, side, half, j):
    return jnp.where(side == 0, table[:, j : j + 1], table[:, half + j : half + j + 1])


def lanes(side, half, j, dim):
    return pl.ds(pl.multiple_of((side * half + j) * dim, dim), dim)


def tables(ld):
    tok = ld.shape[1]
    row = lax.broadcasted_iota(jnp.int32, (tok, tok), 0)
    col = lax.broadcasted_iota(jnp.int32, (tok, tok), 1)
    lower = (row >= col).astype(f32)
    dims = (((1,), (1,)), ((), ()))
    cum_t = lax.dot_general(lower, ld, dims, precision=highest, preferred_element_type=f32)
    cum_r = lax.dot_general(ld, lower, dims, precision=highest, preferred_element_type=f32)
    return cum_t, cum_r


def state_into(outs, a_ref, b_of, factor, side, half, dim):
    j = 0
    for out in outs:
        for i in range(out.shape[0]):
            hi, lo = split(a_ref[:, lanes(side, half, j, dim)].astype(f32) * column(factor, side, half, j))
            b = b_of(j)
            out[i] = dot(hi, b, 0, 0) + dot(lo, b, 0, 0)
            j += 1


def first_states(half, dim, side_ref, k_ref, v_ref, ld_ref, cum_t_ref, cum_r_ref, total_ref, *outs):
    side = side_ref[0]
    cum_t, cum_r = tables(ld_ref[...])
    cum_t_ref[...] = cum_t
    cum_r_ref[...] = cum_r
    tok = cum_t.shape[0]
    total_ref[...] = jnp.broadcast_to(jnp.exp(cum_r[:, tok - 1 :]), total_ref.shape)
    tail = jnp.exp(cum_t[tok - 1 :, :] - cum_t)
    state_into(outs, k_ref, lambda j: v_ref[:, lanes(side, half, j, dim)], tail, side, half, dim)


def more_states(half, dim, side_ref, k_ref, v_ref, cum_t_ref, *outs):
    side = side_ref[0]
    cum_t = cum_t_ref[...]
    tail = jnp.exp(cum_t[cum_t.shape[0] - 1 :, :] - cum_t)
    state_into(outs, k_ref, lambda j: v_ref[:, lanes(side, half, j, dim)], tail, side, half, dim)


def weights_of(cum_t, cum_r, h):
    tok = cum_t.shape[0]
    row = lax.broadcasted_iota(jnp.int32, (tok, tok), 0)
    col = lax.broadcasted_iota(jnp.int32, (tok, tok), 1)
    gap = cum_t[:, h : h + 1] - cum_r[h : h + 1, :]
    return jnp.where(row >= col, jnp.exp(jnp.minimum(gap, 0.0)), 0.0)


def within(heads, dim, side_ref, q_ref, k_ref, v_ref, cum_t_ref, cum_r_ref, mixed_ref, inner_ref):
    cum_t, cum_r = cum_t_ref[...], cum_r_ref[...]
    for h in range(heads):
        at = slice(h * dim, (h + 1) * dim)
        scores = dot(q_ref[:, at], k_ref[:, at], 1, 1)
        mixed = (scores * weights_of(cum_t, cum_r, h)).astype(bf16)
        mixed_ref[h] = mixed
        inner_ref[:, at] = dot(mixed, v_ref[:, at], 1, 0)


def across(half, dim, start, count, have, last, side_ref, *refs):
    side = side_ref[0]
    q_ref, inner_ref, g_ref, gain_ref, cum_t_ref = refs[:5]
    before = refs[5 : 5 + have]
    states = refs[5 + have : -2]
    attn_ref, sums_ref = refs[-2:]
    lead = jnp.exp(cum_t_ref[...])
    squares = cross = jnp.zeros((lead.shape[0], dim), f32)
    j = start
    for ref in states:
        for i in range(ref.shape[0]):
            at = lanes(side, half, j, dim)
            hi, lo = split(ref[i])
            q = q_ref[:, at]
            outer = (dot(q, hi, 1, 0) + dot(q, lo, 1, 0)) * column(lead, side, half, j)
            attn = inner_ref[:, at] + outer
            attn_ref[:, (j - start) * dim : (j - start + 1) * dim] = attn
            scaled = g_ref[:, at].astype(f32) * gain_ref[:, at]
            squares += attn * attn
            cross += scaled * attn
            j += 1
    for ref in before:
        squares += ref[0]
        cross += ref[1]
    if last:
        sums_ref[0:1, :] = jnp.sum(squares.T, axis=0, keepdims=True)
        sums_ref[1:2, :] = jnp.sum(cross.T, axis=0, keepdims=True)
        sums_ref[2:, :] = jnp.zeros((sums_ref.shape[0] - 2, sums_ref.shape[1]), f32)
    else:
        sums_ref[0] = squares
        sums_ref[1] = cross


def gradient(half, dim, full_width, n_sums, n_attn, side_ref, *refs):
    side = side_ref[0]
    q_ref, g_ref, gain_ref, cum_t_ref = refs[:4]
    sums = refs[4 : 4 + n_sums]
    attns = refs[4 + n_sums : 4 + n_sums + n_attn]
    d_ref, gain_part_ref = refs[4 + n_sums + n_attn :][:2]
    outs = refs[4 + n_sums + n_attn + 2 :]
    total = sums[0][...]
    for ref in sums[1:]:
        total = total + ref[...]
    inv_row = lax.rsqrt(total[0:1] / full_width + epsilon)
    mean_row = inv_row * (total[1:2] / full_width)
    tok = inv_row.shape[1]
    inv = jnp.broadcast_to(inv_row, (tok, tok)).T
    mean = jnp.broadcast_to(mean_row, (tok, tok)).T
    lead = jnp.exp(cum_t_ref[...])
    kept = {}
    j = 0
    for ref in attns:
        for i in range(ref.shape[1] // dim):
            at = lanes(side, half, j, dim)
            normed = ref[:, i * dim : (i + 1) * dim] * inv
            g = g_ref[:, at].astype(f32)
            d = (inv * (g * gain_ref[:, at] - normed * mean)).astype(bf16)
            d_ref[:, j * dim : (j + 1) * dim] = d
            gain_part_ref[j : j + 1, :] = jnp.sum(g * normed, axis=0, keepdims=True)
            kept[j] = d
            j += 1
    state_into(outs, q_ref, lambda j: kept[j], lead, side, half, dim)


def local_grads(half, dim, chunks, side_ref, *refs):
    side = side_ref[0]
    q_ref, k_ref, v_ref, cum_t_ref, cum_r_ref, mixed_ref, d_own_ref, d_give_ref = refs[:8]
    states = refs[8 : 8 + 2 * chunks]
    qg_ref, kg_ref, vg_ref = refs[8 + 2 * chunks :]
    cum_t = cum_t_ref[...]
    lead = jnp.exp(cum_t)
    tok = cum_t.shape[0]
    row = lax.broadcasted_iota(jnp.int32, (tok, tok), 0)
    col = lax.broadcasted_iota(jnp.int32, (tok, tok), 1)
    for s, (d_ref, group) in enumerate(((d_own_ref, states[:chunks]), (d_give_ref, states[chunks:]))):
        which = side if s == 0 else 1 - side
        j = 0
        for ref in group:
            for i in range(ref.shape[0]):
                at = lanes(which, half, j, dim)
                h = which * half + j
                d = d_ref[:, j * dim : (j + 1) * dim]
                cum_col = column(cum_t, which, half, j)
                gap = cum_col - cum_r_ref[pl.ds(h, 1), :]
                weights = jnp.where(row >= col, jnp.exp(jnp.minimum(gap, 0.0)), 0.0)
                graded = (dot(d, v_ref[:, at], 1, 1) * weights).astype(bf16)
                hi, lo = split(ref[i])
                outer = (dot(d, hi, 1, 1) + dot(d, lo, 1, 1)) * column(lead, which, half, j)
                qg_ref[:, at] = (dot(graded, k_ref[:, at], 1, 0) + outer).astype(bf16)
                kg_ref[:, at] = dot(graded, q_ref[:, at], 0, 0)
                vg_ref[:, at] = dot(mixed_ref[h], d, 0, 0)
                j += 1


def final_grads(half, dim, chunks, side_ref, *refs):
    side = side_ref[0]
    k_ref, v_ref, cum_t_ref, kg_ref, vg_ref = refs[:5]
    states = refs[5 : 5 + 2 * chunks]
    key_ref, value_ref = refs[5 + 2 * chunks :]
    cum_t = cum_t_ref[...]
    tail = jnp.exp(cum_t[cum_t.shape[0] - 1 :, :] - cum_t)
    for s, group in enumerate((states[:chunks], states[chunks:])):
        which = side if s == 0 else 1 - side
        j = 0
        for ref in group:
            for i in range(ref.shape[0]):
                at = lanes(which, half, j, dim)
                tail_col = column(tail, which, half, j)
                hi, lo = split(ref[i])
                v, k = v_ref[:, at], k_ref[:, at]
                key_ref[:, at] = (kg_ref[:, at] + (dot(v, hi, 1, 1) + dot(v, lo, 1, 1)) * tail_col).astype(bf16)
                value_ref[:, at] = (vg_ref[:, at] + (dot(k, hi, 1, 0) + dot(k, lo, 1, 0)) * tail_col).astype(bf16)
                j += 1


def carried(mine, theirs, total_mine, total_theirs, place, n_seq, n_dp, reverse):
    pairs = n_seq // 2
    block = n_seq - 1 - place if reverse else place
    first = block % 2 == 0
    pair = block // 2
    swap = [(i, i ^ 1) for i in range(n_seq)]

    def hop(a):
        b = a + 1
        lo, hi = (pairs - 1 - a, pairs - 1 - b) if reverse else (a, b)
        perm = []
        for s in range(n_seq):
            for d in range(n_dp):
                if s // 2 == lo:
                    to = (s + 2 * (hi - lo)) * n_dp + d
                elif s // 2 == hi:
                    to = (s - 2 * (hi - lo)) * n_dp + d
                else:
                    to = s * n_dp + (d ^ 1)
                perm.append((s * n_dp + d, to))
        return perm

    received = [lax.ppermute(x, "seq", swap) for x in theirs]
    kept, sent = [], []
    at = 0
    cuts = []
    for x in mine:
        n = x.shape[0]
        cuts.append((total_mine[at : at + n, None, :], total_theirs[at : at + n, None, :]))
        at += n
    sums = [
        jnp.where(first, their_decay, 1.0) * x + jnp.where(first, 1.0, my_decay) * r
        for x, r, (my_decay, their_decay) in zip(mine, received, cuts)
    ]
    both = [a * b for a, b in cuts]
    inward = [None] * len(mine)
    outward = sums
    for a in range(pairs - 1):
        got = [lax.ppermute(x, ("seq", "dp"), hop(a)) for x in outward]
        here = pair == a + 1
        inward = [
            jnp.where(here, g, 0.0 if e is None else e) for g, e in zip(got, inward)
        ]
        outward = [s + d * g for s, d, g in zip(sums, both, got)]
    for x, r, e, (my_decay, their_decay) in zip(mine, received, inward, cuts):
        if e is None:
            e = jnp.zeros_like(x)
        through = jnp.where(first, my_decay, their_decay) * e + jnp.where(first, x, r)
        kept.append(jnp.where(first, e, through))
        sent.append(jnp.where(first, through, e))
    return kept, [lax.ppermute(x, "seq", swap) for x in sent]


def on_device(n_seq, n_dp, queries, keys, values, output_gradient, log_decay, gain):
    tok, width = queries.shape
    heads = log_decay.shape[0]
    dim = width // heads
    half = heads // 2
    chunks = min(4, half)
    sizes = [half // chunks + (1 if i < half % chunks else 0) for i in range(chunks)]
    full_width = width * n_dp
    place = lax.axis_index("seq")
    own = (place % 2).astype(jnp.int32)
    own_side = own.reshape(1)
    give_side = (1 - own).reshape(1)
    gain_row = gain.reshape(1, width)
    pair_flops = 2 * tok * dim * dim
    state = [((n, dim, dim), f32) for n in sizes]
    row_bytes = tok * half * dim

    cum_t, cum_r, total, *give = call(
        functools.partial(first_states, half, dim),
        [((tok, heads), f32), ((heads, tok), f32), ((heads, dim), f32)] + state,
        2 * half * pair_flops, 8 * row_bytes, "first_states",
    )(give_side, keys, values, log_decay)
    swap = [(i, i ^ 1) for i in range(n_seq)]
    other = lax.ppermute(total, "seq", swap)
    own_states = call(
        functools.partial(more_states, half, dim), state, 2 * half * pair_flops, 8 * row_bytes, "more_states"
    )(own_side, keys, values, cum_t)
    mixed, inner = call(
        functools.partial(within, heads, dim),
        [((heads, tok, tok), bf16), ((tok, width), f32)],
        2 * heads * pair_flops, 12 * row_bytes, "within",
    )(own_side, queries, keys, values, cum_t, cum_r)

    upper = own == 1
    total_mine = jnp.where(upper, total[half:], total[:half])
    total_theirs = jnp.where(upper, other[half:], other[:half])
    in_own, in_give = carried(own_states, give, total_mine, total_theirs, place, n_seq, n_dp, False)

    def outer(side, states, start, before, last, name):
        count = sum(x.shape[0] for x in states)
        return call(
            functools.partial(across, half, dim, start, count, len(before), last),
            [((tok, count * dim), f32), ((8, tok), f32) if last else ((2, tok, dim), f32)],
            2 * count * pair_flops, 14 * tok * count * dim, name,
        )(side, queries, inner, output_gradient, gain_row, cum_t, *before, *states)

    attn_own, part = outer(own_side, in_own, 0, [], False, "across_own")
    early = sum(sizes[:-1])
    if early:
        attn_early, more = outer(give_side, in_give[:-1], 0, [part], False, "across_early")
        attn_late, sums = outer(give_side, in_give[-1:], early, [more], True, "across_late")
        attn_give = [attn_early, attn_late]
    else:
        attn_late, sums = outer(give_side, in_give, 0, [part], True, "across_late")
        attn_give = [attn_late]

    if n_dp <= 4:
        all_sums = [sums] + [
            lax.ppermute(sums, "dp", [(i, i ^ m) for i in range(n_dp)]) for m in range(1, n_dp)
        ]
    else:
        all_sums = [lax.psum(sums, "dp")]

    def grads(side, attns, name):
        return call(
            functools.partial(gradient, half, dim, full_width, len(all_sums), len(attns)),
            [((tok, half * dim), bf16), ((half, dim), f32)] + state,
            2 * half * pair_flops, 14 * row_bytes, name,
        )(side, queries, output_gradient, gain_row, cum_t, *all_sums, *attns)

    d_give, gain_give, *back_give = grads(give_side, attn_give, "gradient_give")
    d_own, gain_own, *back_own = grads(own_side, [attn_own], "gradient_own")
    query_grad, key_part, value_part = call(
        functools.partial(local_grads, half, dim, chunks),
        [((tok, width), bf16), ((tok, width), f32), ((tok, width), f32)],
        6 * heads * pair_flops, 40 * row_bytes, "local_grads",
    )(own_side, queries, keys, values, cum_t, cum_r, mixed, d_own, d_give, *in_own, *in_give)

    late_own, late_give = carried(back_own, back_give, total_mine, total_theirs, place, n_seq, n_dp, True)

    gain_grad = jnp.concatenate(
        [jnp.where(upper, gain_give, gain_own), jnp.where(upper, gain_own, gain_give)], axis=0
    )
    step = 1
    while step < n_seq:
        gain_grad = gain_grad + lax.ppermute(gain_grad, "seq", [(i, i ^ step) for i in range(n_seq)])
        step *= 2

    key_grad, value_grad = call(
        functools.partial(final_grads, half, dim, chunks),
        [((tok, width), bf16), ((tok, width), bf16)],
        4 * heads * pair_flops, 32 * row_bytes, "final_grads",
    )(own_side, keys, values, cum_t, key_part, value_part, *late_own, *late_give)
    return query_grad, key_grad, value_grad, gain_grad.reshape(width)


def solution(mesh):
    return jax.shard_map(
        functools.partial(on_device, mesh.shape["seq"], mesh.shape["dp"]),
        mesh=mesh,
        in_specs=(P("seq", "dp"), P("seq", "dp"), P("seq", "dp"), P("seq", "dp"), P("dp", "seq"), P("dp")),
        out_specs=(P("seq", "dp"), P("seq", "dp"), P("seq", "dp"), P("dp")),
        check_vma=False,
    )
```

time: 337 us -> 115 us (0.34)
  waiting for transfers between devices: 195 us -> 29.2 us
  blocking collectives: 57.3 us -> 0 us
  starting transfers between devices: 0.08 us -> 51.9 us
  other arithmetic: 26.4 us -> 4.2 us
  matrix products: 18.9 us -> 0 us
  between operations: 15 us -> 1.06 us
  Pallas kernels: 0 us -> 12.6 us
  local copies, waits for them, and re-layouts: 21.9 us -> 14.1 us
    all_gather x2 -> x0, waiting for transfers between devices: 195 us -> none  [entering(): pieces = jax.tree.map(lambda part: lax.all_gather(part, axis), value)]
    ppermute x0 -> x47, starting transfers between devices: none -> 51.9 us  [the longest x24 21.4 us: carried(): got = [lax.ppermute(x, ('seq', 'dp'), hop(a)) for x in outward]]
    psum x3 -> x0, blocking collectives: 33.5 us -> none  [the longest x1 21.3 us: on_device(): gain_grad = lax.psum(gain_part, 'seq')]
    ppermute x0 -> x47, waiting for transfers between devices: none -> 29.2 us  [the longest x8 11 us: carried(): return (kept, [lax.ppermute(x, 'seq', swap) for x in sent])]
    unnamed x1 -> x0, blocking collectives: 23.7 us -> none
    select_n x14 -> x23, other arithmetic: 21.8 us -> 1.3 us  [the longest x2 0.62 us: carried(): jnp.where(first, their_decay, 1.0) * x + jnp.where(first, 1.0, my_decay) * r]
    dot_general x12 -> x0, matrix products: 18.9 us -> none  [the longest x1 3.47 us: on_device(): jnp.einsum('thd,the->hde', query_f * lead_t, d_attn_f, precision=highest)]
    pallas_call x0 -> x10, Pallas kernels: none -> 12.6 us  [run(): pl.pallas_call(body, out_shape=[jax.ShapeDtypeStruct(*o) for o in outs],...]
  transfers between devices with their start and end apart: 2 -> 47, of which waited for: 2 -> 17; matrix products, arithmetic and copies ran while one was open for 3% -> 4% of each run, Pallas kernels for 0% -> 7%
where the time goes in v1:
time: 115 us; the launch traced here: 113 us
  starting transfers between devices  51.9 us (45%)
  waiting for transfers between devices  29.2 us (25%)
  local copies, waits for them, and re-layouts  14.1 us (12%)
  Pallas kernels  12.6 us (11%)
  other arithmetic  4.2 us (4%)
    ppermute x24, starting transfers between devices, carried(): got = [lax.ppermute(x, ('seq', 'dp'), hop(a)) for x in outward]  21.4 us
    unnamed x56, local copies, waits for them, and re-layouts  14.1 us
    pallas_call x10, Pallas kernels, run(): pl.pallas_call(body, out_shape=[jax.ShapeDtypeStruct(*o) for o in outs],...  12.6 us
    ppermute x8, waiting for transfers between devices, carried(): return (kept, [lax.ppermute(x, 'seq', swap) for x in sent])  11 us
    ppermute x8, starting transfers between devices, carried(): return (kept, [lax.ppermute(x, 'seq', swap) for x in sent])  10.7 us
    ppermute x8, starting transfers between devices, carried(): received = [lax.ppermute(x, 'seq', swap) for x in theirs]  8.1 us
    ppermute x24, waiting for transfers between devices, carried(): got = [lax.ppermute(x, ('seq', 'dp'), hop(a)) for x in outward]  8.02 us
    ppermute x3, starting transfers between devices, on_device(): lax.ppermute(gain_grad, 'seq', [(i, i ^ step) for i in range(n_seq)])  6.8 us
  transfers between devices with their start and end apart: 47, of which 17 were waited for; matrix products, arithmetic and copies ran while one was open for 4% of the time, Pallas kernels for 7%

profile of v1, /device:TPU:0, one launch (start us, length us, event | category | flops | bytes accessed | tf_op | source)
XLA Modules:
  0.0 113.0 jit_solution(17660405190979465543)
XLA Ops:
  4.3 3.1 %collective-permute-start = (f32[16,128]{1,0:T(8,128)S(1)}, f32[16,128]{1,0:T(8,128)S(1)}, u32[]{:S(2)}, u32[]{:S(2)}) collective-permute-start(f32[16,128]{1,0:T(8,128)S(1)} %get-tuple-element.44), channel_id=1, source_target_pairs={{0,4},{4,0},{8,12},{12,8},{16,20},{20,16},{24,28},{28,24},{1,5},{5... | collective-permute-start | bytes 24584 | tf_op jit(solution)/shard_map/ppermute | solution.py:299
  7.4 1.9 %collective-permute-start.5 = (f32[2,128,128]{2,1,0:T(8,128)S(1)}, f32[2,128,128]{2,1,0:T(8,128)S(1)}, u32[]{:S(2)}, u32[]{:S(2)}) collective-permute-start(f32[2,128,128]{2,1,0:T(8,128)S(1)} %get-tuple-element.48), channel_id=1, source_target_pairs={{0,4},{4,0},{8,12},{12,8},{16,20},{20,16},{24,28},{28,24},{1,5},{5... | collective-permute-start | bytes 393224 | tf_op jit(solution)/shard_map/ppermute | solution.py:245
  9.5 1.9 %collective-permute-start.13 = (f32[2,128,128]{2,1,0:T(8,128)S(1)}, f32[2,128,128]{2,1,0:T(8,128)}, u32[]{:S(2)}, u32[]{:S(2)}) collective-permute-start(f32[2,128,128]{2,1,0:T(8,128)S(1)} %get-tuple-element.52), channel_id=1, source_target_pairs={{0,4},{4,0},{8,12},{12,8},{16,20},{20,16},{24,28},{28,24},{1,5},{5... | collective-permute-start | bytes 393224 | tf_op jit(solution)/shard_map/ppermute | solution.py:245
  12.5 2.6 %within.1 = (bf16[16,128,128]{2,1,0:T(8,128)(2,1)S(1)}, f32[128,2048]{1,0:T(8,128)S(1)}) custom-call(s32[1]{0:T(128)} %bitcast.side_ref, bf16[128,2048]{1,0:T(8,128)(2,1)S(1)} %copy-done, bf16[128,2048]{1,0:T(8,128)(2,1)S(1)} %copy-done.2, bf16[128,2048]{1,0:T(8,128)(2,1)S(1)} %copy-done.4, ...), custom_call_target="tpu_custom_call" | custom-call | flops 134217728 | bytes 1572864 | tf_op jit(solution)/shard_map/within/pallas_call | solution.py:21
  17.2 3.6 %collective-permute-done.13 = f32[2,128,128]{2,1,0:T(8,128)} collective-permute-done((f32[2,128,128]{2,1,0:T(8,128)S(1)}, f32[2,128,128]{2,1,0:T(8,128)}, u32[]{:S(2)}, u32[]{:S(2)}) %collective-permute-start.13) | collective-permute-done | bytes 131104 | tf_op jit(solution)/shard_map/ppermute | solution.py:245
  21.8 1.6 %collective-permute-start.14 = (f32[2,128,128]{2,1,0:T(8,128)S(1)}, f32[2,128,128]{2,1,0:T(8,128)S(1)}, u32[]{:S(2)}, u32[]{:S(2)}) collective-permute-start(f32[2,128,128]{2,1,0:T(8,128)S(1)} %multiply_add_fusion.14), channel_id=1, source_target_pairs={{0,8},{1,9},{2,10},{3,11},{4,12},{5,13},{6,14},{7,15},{8,0},{9,1},... | collective-permute-start | bytes 393224 | tf_op jit(solution)/shard_map/ppermute | solution.py:261
  24.9 1.6 %collective-permute-start.6 = (f32[2,128,128]{2,1,0:T(8,128)S(1)}, f32[2,128,128]{2,1,0:T(8,128)S(1)}, u32[]{:S(2)}, u32[]{:S(2)}) collective-permute-start(f32[2,128,128]{2,1,0:T(8,128)S(1)} %multiply_add_fusion.20), channel_id=1, source_target_pairs={{0,8},{1,9},{2,10},{3,11},{4,12},{5,13},{6,14},{7,15},{8,0},{9,1},... | collective-permute-start | bytes 393224 | tf_op jit(solution)/shard_map/ppermute | solution.py:261
  28.3 2.7 %collective-permute-done.10 = f32[2,128,128]{2,1,0:T(8,128)S(1)} collective-permute-done((f32[2,128,128]{2,1,0:T(8,128)S(1)}, f32[2,128,128]{2,1,0:T(8,128)S(1)}, u32[]{:S(2)}, u32[]{:S(2)}) %collective-permute-start.10) | collective-permute-done | bytes 131104 | tf_op jit(solution)/shard_map/ppermute | solution.py:261
  31.1 2.7 %collective-permute-done.6 = f32[2,128,128]{2,1,0:T(8,128)S(1)} collective-permute-done((f32[2,128,128]{2,1,0:T(8,128)S(1)}, f32[2,128,128]{2,1,0:T(8,128)S(1)}, u32[]{:S(2)}, u32[]{:S(2)}) %collective-permute-start.6) | collective-permute-done | bytes 131104 | tf_op jit(solution)/shard_map/ppermute | solution.py:261
  38.4 1.6 %collective-permute-start.19 = (f32[2,128,128]{2,1,0:T(8,128)S(1)}, f32[2,128,128]{2,1,0:T(8,128)S(1)}, u32[]{:S(2)}, u32[]{:S(2)}) collective-permute-start(f32[2,128,128]{2,1,0:T(8,128)S(1)} %get-tuple-element.86), channel_id=1, source_target_pairs={{0,4},{4,0},{8,12},{12,8},{16,20},{20,16},{24,28},{28,24},{1,5},{5... | collective-permute-start | bytes 393224 | tf_op jit(solution)/shard_map/ppermute | solution.py:273
  40.7 1.6 %collective-permute-start.17 = (f32[2,128,128]{2,1,0:T(8,128)S(1)}, f32[2,128,128]{2,1,0:T(8,128)S(1)}, u32[]{:S(2)}, u32[]{:S(2)}) collective-permute-start(f32[2,128,128]{2,1,0:T(8,128)S(1)} %get-tuple-element.90), channel_id=1, source_target_pairs={{0,4},{4,0},{8,12},{12,8},{16,20},{20,16},{24,28},{28,24},{1,5},{5... | collective-permute-start | bytes 393224 | tf_op jit(solution)/shard_map/ppermute | solution.py:273
  44.4 1.8 %collective-permute-done.19.refs_8_.refs_14_ = f32[2,128,128]{2,1,0:T(8,128)S(1)} collective-permute-done((f32[2,128,128]{2,1,0:T(8,128)S(1)}, f32[2,128,128]{2,1,0:T(8,128)S(1)}, u32[]{:S(2)}, u32[]{:S(2)}) %collective-permute-start.19) | collective-permute-done | bytes 131104 | tf_op jit(solution)/shard_map/ppermute | solution.py:273
  46.2 2.8 %collective-permute-done.18.refs_7_.refs_13_ = f32[2,128,128]{2,1,0:T(8,128)S(1)} collective-permute-done((f32[2,128,128]{2,1,0:T(8,128)S(1)}, f32[2,128,128]{2,1,0:T(8,128)S(1)}, u32[]{:S(2)}, u32[]{:S(2)}) %collective-permute-start.18) | collective-permute-done | bytes 131104 | tf_op jit(solution)/shard_map/ppermute | solution.py:273
  49.0 2.2 %collective-permute-done.17.refs_6_.refs_12_ = f32[2,128,128]{2,1,0:T(8,128)S(1)} collective-permute-done((f32[2,128,128]{2,1,0:T(8,128)S(1)}, f32[2,128,128]{2,1,0:T(8,128)S(1)}, u32[]{:S(2)}, u32[]{:S(2)}) %collective-permute-start.17) | collective-permute-done | bytes 131104 | tf_op jit(solution)/shard_map/ppermute | solution.py:273
  63.3 2.2 %collective-permute-done.44 = f32[16,128]{1,0:T(8,128)S(1)} collective-permute-done((f32[16,128]{1,0:T(8,128)S(1)}, f32[16,128]{1,0:T(8,128)S(1)}, u32[]{:S(2)}, u32[]{:S(2)}) %collective-permute-start.44) | collective-permute-done | bytes 8224 | tf_op jit(solution)/shard_map/ppermute | solution.py:361
  65.5 5.3 %collective-permute-start.45 = (f32[16,128]{1,0:T(8,128)S(1)}, f32[16,128]{1,0:T(8,128)S(1)}, u32[]{:S(2)}, u32[]{:S(2)}) collective-permute-start(f32[16,128]{1,0:T(8,128)S(1)} %fusion.16), channel_id=1, source_target_pairs={{0,8},{4,12},{8,0},{12,4},{16,24},{20,28},{24,16},{28,20},{1,9},{5... | collective-permute-start | bytes 24584 | tf_op jit(solution)/shard_map/ppermute | solution.py:361
  70.8 1.5 %collective-permute-start.24 = (f32[2,128,128]{2,1,0:T(8,128)}, f32[2,128,128]{2,1,0:T(8,128)S(1)}, u32[]{:S(2)}, u32[]{:S(2)}) collective-permute-start(f32[2,128,128]{2,1,0:T(8,128)} %copy-done.17), channel_id=1, source_target_pairs={{0,4},{4,0},{8,12},{12,8},{16,20},{20,16},{24,28},{28,24},{1,5},{5... | collective-permute-start | bytes 393224 | tf_op jit(solution)/shard_map/ppermute | solution.py:245
  72.8 1.5 %collective-permute-start.32 = (f32[2,128,128]{2,1,0:T(8,128)}, f32[2,128,128]{2,1,0:T(8,128)S(1)}, u32[]{:S(2)}, u32[]{:S(2)}) collective-permute-start(f32[2,128,128]{2,1,0:T(8,128)} %copy-done.19), channel_id=1, source_target_pairs={{0,4},{4,0},{8,12},{12,8},{16,20},{20,16},{24,28},{28,24},{1,5},{5... | collective-permute-start | bytes 393224 | tf_op jit(solution)/shard_map/ppermute | solution.py:245
  76.9 3.6 %local_grads.1 = (bf16[128,2048]{1,0:T(8,128)(2,1)}, f32[128,2048]{1,0:T(8,128)S(1)}, f32[128,2048]{1,0:T(8,128)S(1)}) custom-call(s32[1]{0:T(128)} %bitcast.side_ref, bf16[128,2048]{1,0:T(8,128)(2,1)S(1)} %copy-done, bf16[128,2048]{1,0:T(8,128)(2,1)S(1)} %copy-done.2, bf16[128,2048]{1,0:T(8,128)(2,1)S(1)} %copy-done.5, ...), custom_call_target="tpu_custom_call" | custom-call | flops 402653184 | bytes 5242880 | tf_op jit(solution)/shard_map/local_grads/pallas_call | solution.py:21
  81.1 2.0 %collective-permute-done.36 = f32[2,128,128]{2,1,0:T(8,128)S(1)} collective-permute-done((f32[2,128,128]{2,1,0:T(8,128)}, f32[2,128,128]{2,1,0:T(8,128)S(1)}, u32[]{:S(2)}, u32[]{:S(2)}) %collective-permute-start.36) | collective-permute-done | bytes 131104 | tf_op jit(solution)/shard_map/ppermute | solution.py:245
  88.0 8.5 %collective-permute-start.39 = (f32[2,128,128]{2,1,0:T(8,128)S(1)}, f32[2,128,128]{2,1,0:T(8,128)S(1)}, u32[]{:S(2)}, u32[]{:S(2)}) collective-permute-start(f32[2,128,128]{2,1,0:T(8,128)S(1)} %multiply_add_fusion), channel_id=1, source_target_pairs={{0,8},{1,9},{2,10},{3,11},{4,12},{5,13},{6,14},{7,15},{8,0},{9,1},... | collective-permute-start | bytes 393224 | tf_op jit(solution)/shard_map/ppermute | solution.py:261
  96.4 1.6 %collective-permute-start.35 = (f32[2,128,128]{2,1,0:T(8,128)S(1)}, f32[2,128,128]{2,1,0:T(8,128)S(1)}, u32[]{:S(2)}, u32[]{:S(2)}) collective-permute-start(f32[2,128,128]{2,1,0:T(8,128)S(1)} %multiply_add_fusion.3), channel_id=1, source_target_pairs={{0,8},{1,9},{2,10},{3,11},{4,12},{5,13},{6,14},{7,15},{8,0},{9,1},... | collective-permute-start | bytes 393224 | tf_op jit(solution)/shard_map/ppermute | solution.py:261
  100.9 1.6 %collective-permute-start.43 = (f32[2,128,128]{2,1,0:T(8,128)S(1)}, f32[2,128,128]{2,1,0:T(8,128)S(1)}, u32[]{:S(2)}, u32[]{:S(2)}) collective-permute-start(f32[2,128,128]{2,1,0:T(8,128)S(1)} %get-tuple-element.76), channel_id=1, source_target_pairs={{0,4},{4,0},{8,12},{12,8},{16,20},{20,16},{24,28},{28,24},{1,5},{5... | collective-permute-start | bytes 393224 | tf_op jit(solution)/shard_map/ppermute | solution.py:273
  110.9 2.1 %final_grads.1 = (bf16[128,2048]{1,0:T(8,128)(2,1)}, bf16[128,2048]{1,0:T(8,128)(2,1)}) custom-call(s32[1]{0:T(128)} %bitcast.side_ref, bf16[128,2048]{1,0:T(8,128)(2,1)S(1)} %copy-done.2, bf16[128,2048]{1,0:T(8,128)(2,1)S(1)} %copy-done.5, f32[128,16]{1,0:T(8,128)S(1)} %get-tuple-element.40.cum_t_ref.refs_4_.refs_3_.refs_2_, ...), custom_call_target="tpu_custom_call" | custom-call | flops 268435456 | bytes 4194304 | tf_op jit(solution)/shard_map/final_grads/pallas_call | solution.py:21
  (187 shorter events, 50.1 us)
Async XLA Ops:
  4.3 12.3 %collective-permute-start = (f32[16,128]{1,0:T(8,128)S(1)}, f32[16,128]{1,0:T(8,128)S(1)}, u32[]{:S(2)}, u32[]{:S(2)}) collective-permute-start(f32[16,128]{1,0:T(8,128)S(1)} %get-tuple-element.44), channel_id=1, source_target_pairs={{0,4},{4,0},{8,12},{12,8},{16,20},{20,16},{24,28},{28,24},{1,5},{5... | collective-permute-start | bytes 24584 | tf_op jit(solution)/shard_map/ppermute | solution.py:299
  7.4 19.2 %collective-permute-start.1 = (f32[2,128,128]{2,1,0:T(8,128)S(1)}, f32[2,128,128]{2,1,0:T(8,128)S(1)}, u32[]{:S(2)}, u32[]{:S(2)}) collective-permute-start(f32[2,128,128]{2,1,0:T(8,128)S(1)} %get-tuple-element.46), channel_id=1, source_target_pairs={{0,4},{4,0},{8,12},{12,8},{16,20},{20,16},{24,28},{28,24},{1,5},{5... | collective-permute-start | bytes 393224 | tf_op jit(solution)/shard_map/ppermute | solution.py:245
  7.4 17.4 %collective-permute-start.5 = (f32[2,128,128]{2,1,0:T(8,128)S(1)}, f32[2,128,128]{2,1,0:T(8,128)S(1)}, u32[]{:S(2)}, u32[]{:S(2)}) collective-permute-start(f32[2,128,128]{2,1,0:T(8,128)S(1)} %get-tuple-element.48), channel_id=1, source_target_pairs={{0,4},{4,0},{8,12},{12,8},{16,20},{20,16},{24,28},{28,24},{1,5},{5... | collective-permute-start | bytes 393224 | tf_op jit(solution)/shard_map/ppermute | solution.py:245
  9.4 14.0 %collective-permute-start.9 = (f32[2,128,128]{2,1,0:T(8,128)S(1)}, f32[2,128,128]{2,1,0:T(8,128)}, u32[]{:S(2)}, u32[]{:S(2)}) collective-permute-start(f32[2,128,128]{2,1,0:T(8,128)S(1)} %get-tuple-element.50), channel_id=1, source_target_pairs={{0,4},{4,0},{8,12},{12,8},{16,20},{20,16},{24,28},{28,24},{1,5},{5... | collective-permute-start | bytes 393224 | tf_op jit(solution)/shard_map/ppermute | solution.py:245
  9.5 11.4 %collective-permute-start.13 = (f32[2,128,128]{2,1,0:T(8,128)S(1)}, f32[2,128,128]{2,1,0:T(8,128)}, u32[]{:S(2)}, u32[]{:S(2)}) collective-permute-start(f32[2,128,128]{2,1,0:T(8,128)S(1)} %get-tuple-element.52), channel_id=1, source_target_pairs={{0,4},{4,0},{8,12},{12,8},{16,20},{20,16},{24,28},{28,24},{1,5},{5... | collective-permute-start | bytes 393224 | tf_op jit(solution)/shard_map/ppermute | solution.py:245
  21.8 6.4 %collective-permute-start.14 = (f32[2,128,128]{2,1,0:T(8,128)S(1)}, f32[2,128,128]{2,1,0:T(8,128)S(1)}, u32[]{:S(2)}, u32[]{:S(2)}) collective-permute-start(f32[2,128,128]{2,1,0:T(8,128)S(1)} %multiply_add_fusion.14), channel_id=1, source_target_pairs={{0,8},{1,9},{2,10},{3,11},{4,12},{5,13},{6,14},{7,15},{8,0},{9,1},... | collective-permute-start | bytes 393224 | tf_op jit(solution)/shard_map/ppermute | solution.py:261
  24.3 6.7 %collective-permute-start.10 = (f32[2,128,128]{2,1,0:T(8,128)S(1)}, f32[2,128,128]{2,1,0:T(8,128)S(1)}, u32[]{:S(2)}, u32[]{:S(2)}) collective-permute-start(f32[2,128,128]{2,1,0:T(8,128)S(1)} %multiply_add_fusion.17), channel_id=1, source_target_pairs={{0,8},{1,9},{2,10},{3,11},{4,12},{5,13},{6,14},{7,15},{8,0},{9,1},... | collective-permute-start | bytes 393224 | tf_op jit(solution)/shard_map/ppermute | solution.py:261
  24.9 8.9 %collective-permute-start.6 = (f32[2,128,128]{2,1,0:T(8,128)S(1)}, f32[2,128,128]{2,1,0:T(8,128)S(1)}, u32[]{:S(2)}, u32[]{:S(2)}) collective-permute-start(f32[2,128,128]{2,1,0:T(8,128)S(1)} %multiply_add_fusion.20), channel_id=1, source_target_pairs={{0,8},{1,9},{2,10},{3,11},{4,12},{5,13},{6,14},{7,15},{8,0},{9,1},... | collective-permute-start | bytes 393224 | tf_op jit(solution)/shard_map/ppermute | solution.py:261
  26.5 8.7 %collective-permute-start.2 = (f32[2,128,128]{2,1,0:T(8,128)S(1)}, f32[2,128,128]{2,1,0:T(8,128)S(1)}, u32[]{:S(2)}, u32[]{:S(2)}) collective-permute-start(f32[2,128,128]{2,1,0:T(8,128)S(1)} %multiply_add_fusion.23), channel_id=1, source_target_pairs={{0,8},{1,9},{2,10},{3,11},{4,12},{5,13},{6,14},{7,15},{8,0},{9,1},... | collective-permute-start | bytes 393224 | tf_op jit(solution)/shard_map/ppermute | solution.py:261
  28.2 7.1 %collective-permute-start.15 = (f32[2,128,128]{2,1,0:T(8,128)S(1)}, f32[2,128,128]{2,1,0:T(8,128)S(1)}, u32[]{:S(2)}, u32[]{:S(2)}) collective-permute-start(f32[2,128,128]{2,1,0:T(8,128)S(1)} %multiply_add_fusion.13), channel_id=1, source_target_pairs={{0,1},{1,0},{2,3},{3,2},{4,5},{5,4},{6,7},{7,6},{8,16},{9,17},{10,... | collective-permute-start | bytes 393224 | tf_op jit(solution)/shard_map/ppermute | solution.py:261
  37.0 14.9 %collective-permute-start.20 = (f32[2,128,128]{2,1,0:T(8,128)S(1)}, f32[2,128,128]{2,1,0:T(8,128)S(1)}, u32[]{:S(2)}, u32[]{:S(2)}) collective-permute-start(f32[2,128,128]{2,1,0:T(8,128)S(1)} %get-tuple-element.84), channel_id=1, source_target_pairs={{0,4},{4,0},{8,12},{12,8},{16,20},{20,16},{24,28},{28,24},{1,5},{5... | collective-permute-start | bytes 393224 | tf_op jit(solution)/shard_map/ppermute | solution.py:273
  38.4 7.8 %collective-permute-start.19 = (f32[2,128,128]{2,1,0:T(8,128)S(1)}, f32[2,128,128]{2,1,0:T(8,128)S(1)}, u32[]{:S(2)}, u32[]{:S(2)}) collective-permute-start(f32[2,128,128]{2,1,0:T(8,128)S(1)} %get-tuple-element.86), channel_id=1, source_target_pairs={{0,4},{4,0},{8,12},{12,8},{16,20},{20,16},{24,28},{28,24},{1,5},{5... | collective-permute-start | bytes 393224 | tf_op jit(solution)/shard_map/ppermute | solution.py:273
  40.1 8.9 %collective-permute-start.18 = (f32[2,128,128]{2,1,0:T(8,128)S(1)}, f32[2,128,128]{2,1,0:T(8,128)S(1)}, u32[]{:S(2)}, u32[]{:S(2)}) collective-permute-start(f32[2,128,128]{2,1,0:T(8,128)S(1)} %get-tuple-element.88), channel_id=1, source_target_pairs={{0,4},{4,0},{8,12},{12,8},{16,20},{20,16},{24,28},{28,24},{1,5},{5... | collective-permute-start | bytes 393224 | tf_op jit(solution)/shard_map/ppermute | solution.py:273
  40.7 10.5 %collective-permute-start.17 = (f32[2,128,128]{2,1,0:T(8,128)S(1)}, f32[2,128,128]{2,1,0:T(8,128)S(1)}, u32[]{:S(2)}, u32[]{:S(2)}) collective-permute-start(f32[2,128,128]{2,1,0:T(8,128)S(1)} %get-tuple-element.90), channel_id=1, source_target_pairs={{0,4},{4,0},{8,12},{12,8},{16,20},{20,16},{24,28},{28,24},{1,5},{5... | collective-permute-start | bytes 393224 | tf_op jit(solution)/shard_map/ppermute | solution.py:273
  65.5 9.4 %collective-permute-start.45 = (f32[16,128]{1,0:T(8,128)S(1)}, f32[16,128]{1,0:T(8,128)S(1)}, u32[]{:S(2)}, u32[]{:S(2)}) collective-permute-start(f32[16,128]{1,0:T(8,128)S(1)} %fusion.16), channel_id=1, source_target_pairs={{0,8},{4,12},{8,0},{12,4},{16,24},{20,28},{24,16},{28,20},{1,9},{5... | collective-permute-start | bytes 24584 | tf_op jit(solution)/shard_map/ppermute | solution.py:361
  70.8 15.2 %collective-permute-start.24 = (f32[2,128,128]{2,1,0:T(8,128)}, f32[2,128,128]{2,1,0:T(8,128)S(1)}, u32[]{:S(2)}, u32[]{:S(2)}) collective-permute-start(f32[2,128,128]{2,1,0:T(8,128)} %copy-done.17), channel_id=1, source_target_pairs={{0,4},{4,0},{8,12},{12,8},{16,20},{20,16},{24,28},{28,24},{1,5},{5... | collective-permute-start | bytes 393224 | tf_op jit(solution)/shard_map/ppermute | solution.py:245
  72.3 12.9 %collective-permute-start.28 = (f32[2,128,128]{2,1,0:T(8,128)}, f32[2,128,128]{2,1,0:T(8,128)S(1)}, u32[]{:S(2)}, u32[]{:S(2)}) collective-permute-start(f32[2,128,128]{2,1,0:T(8,128)} %copy-done.18), channel_id=1, source_target_pairs={{0,4},{4,0},{8,12},{12,8},{16,20},{20,16},{24,28},{28,24},{1,5},{5... | collective-permute-start | bytes 393224 | tf_op jit(solution)/shard_map/ppermute | solution.py:245
  72.8 11.1 %collective-permute-start.32 = (f32[2,128,128]{2,1,0:T(8,128)}, f32[2,128,128]{2,1,0:T(8,128)S(1)}, u32[]{:S(2)}, u32[]{:S(2)}) collective-permute-start(f32[2,128,128]{2,1,0:T(8,128)} %copy-done.19), channel_id=1, source_target_pairs={{0,4},{4,0},{8,12},{12,8},{16,20},{20,16},{24,28},{28,24},{1,5},{5... | collective-permute-start | bytes 393224 | tf_op jit(solution)/shard_map/ppermute | solution.py:245
  74.3 8.8 %collective-permute-start.36 = (f32[2,128,128]{2,1,0:T(8,128)}, f32[2,128,128]{2,1,0:T(8,128)S(1)}, u32[]{:S(2)}, u32[]{:S(2)}) collective-permute-start(f32[2,128,128]{2,1,0:T(8,128)} %copy-done.20), channel_id=1, source_target_pairs={{0,4},{4,0},{8,12},{12,8},{16,20},{20,16},{24,28},{28,24},{1,5},{5... | collective-permute-start | bytes 393224 | tf_op jit(solution)/shard_map/ppermute | solution.py:245
  86.6 9.8 %collective-permute-start.34 = (f32[2,128,128]{2,1,0:T(8,128)S(1)}, f32[2,128,128]{2,1,0:T(8,128)S(1)}, u32[]{:S(2)}, u32[]{:S(2)}) collective-permute-start(f32[2,128,128]{2,1,0:T(8,128)S(1)} %multiply_add_fusion.4), channel_id=1, source_target_pairs={{0,1},{1,0},{2,3},{3,2},{4,5},{5,4},{6,7},{7,6},{8,16},{9,17},{10,... | collective-permute-start | bytes 393224 | tf_op jit(solution)/shard_map/ppermute | solution.py:261
  87.3 10.8 %collective-permute-start.30 = (f32[2,128,128]{2,1,0:T(8,128)S(1)}, f32[2,128,128]{2,1,0:T(8,128)S(1)}, u32[]{:S(2)}, u32[]{:S(2)}) collective-permute-start(f32[2,128,128]{2,1,0:T(8,128)S(1)} %multiply_add_fusion.7), channel_id=1, source_target_pairs={{0,1},{1,0},{2,3},{3,2},{4,5},{5,4},{6,7},{7,6},{8,16},{9,17},{10,... | collective-permute-start | bytes 393224 | tf_op jit(solution)/shard_map/ppermute | solution.py:261
  87.5 12.0 %collective-permute-start.26 = (f32[2,128,128]{2,1,0:T(8,128)S(1)}, f32[2,128,128]{2,1,0:T(8,128)S(1)}, u32[]{:S(2)}, u32[]{:S(2)}) collective-permute-start(f32[2,128,128]{2,1,0:T(8,128)S(1)} %multiply_add_fusion.10), channel_id=1, source_target_pairs={{0,1},{1,0},{2,3},{3,2},{4,5},{5,4},{6,7},{7,6},{8,16},{9,17},{10,... | collective-permute-start | bytes 393224 | tf_op jit(solution)/shard_map/ppermute | solution.py:261
  88.0 12.9 %collective-permute-start.39 = (f32[2,128,128]{2,1,0:T(8,128)S(1)}, f32[2,128,128]{2,1,0:T(8,128)S(1)}, u32[]{:S(2)}, u32[]{:S(2)}) collective-permute-start(f32[2,128,128]{2,1,0:T(8,128)S(1)} %multiply_add_fusion), channel_id=1, source_target_pairs={{0,8},{1,9},{2,10},{3,11},{4,12},{5,13},{6,14},{7,15},{8,0},{9,1},... | collective-permute-start | bytes 393224 | tf_op jit(solution)/shard_map/ppermute | solution.py:261
  96.4 6.1 %collective-permute-start.35 = (f32[2,128,128]{2,1,0:T(8,128)S(1)}, f32[2,128,128]{2,1,0:T(8,128)S(1)}, u32[]{:S(2)}, u32[]{:S(2)}) collective-permute-start(f32[2,128,128]{2,1,0:T(8,128)S(1)} %multiply_add_fusion.3), channel_id=1, source_target_pairs={{0,8},{1,9},{2,10},{3,11},{4,12},{5,13},{6,14},{7,15},{8,0},{9,1},... | collective-permute-start | bytes 393224 | tf_op jit(solution)/shard_map/ppermute | solution.py:261
  (51 other events, 173.2 us)

commit v2 on v1

--- a/solution.py
+++ b/solution.py
@@ -6,6 +6,7 @@
 from jax.experimental import pallas as pl
 from jax.experimental.pallas import tpu as pltpu
 from jax.sharding import PartitionSpec as P
+
 
 epsilon = 1e-05
 highest = lax.Precision.HIGHEST
@@ -16,8 +17,8 @@
 GRANT = 24 * 2**20
 
 
-def call(body, outs, flops, moved, name):
-    def run(side, *arrays):
+def call(body, outs, flops, moved):
+    def run(place, *arrays):
         return pl.pallas_call(
             body,
             out_shape=[jax.ShapeDtypeStruct(*o) for o in outs],
@@ -25,8 +26,7 @@
             out_specs=[VMEM] * len(outs),
             compiler_params=pltpu.CompilerParams(vmem_limit_bytes=GRANT),
             cost_estimate=pl.CostEstimate(flops=flops, bytes_accessed=moved, transcendentals=0),
-            name=name,
-        )(side, *arrays)
+        )(place, *arrays)
 
     return run
 
@@ -42,6 +42,21 @@
 
 def column(table, side, half, j):
     return jnp.where(side == 0, table[:, j : j + 1], table[:, half + j : half + j + 1])
+
+
+def side_of(place_ref, give):
+    own = place_ref[0] & 1
+    return 1 - own if give else own
+
+
+def flags_of(place, pairs, shape):
+    row = lax.broadcasted_iota(jnp.int32, shape, 0)
+    odd, pair = place & 1, place >> 1
+    forward = (row >= 3) & (row < 2 + pairs) & (row - 2 == pair)
+    reverse = (row >= 2 + pairs) & (row < 1 + 2 * pairs) & (row - 1 - pairs == pairs - 1 - pair)
+    even = jnp.full(shape, odd, jnp.int32) == 0
+    on = ((row == 0) & ~even) | ((row == 1) & even) | ((row == 2) & ~even) | forward | reverse
+    return on.astype(f32)
 
 
 def lanes(side, half, j, dim):
@@ -69,8 +84,9 @@
             j += 1
 
 
-def first_states(half, dim, side_ref, k_ref, v_ref, ld_ref, cum_t_ref, cum_r_ref, total_ref, *outs):
-    side = side_ref[0]
+def first_states(half, dim, pairs, place_ref, k_ref, v_ref, ld_ref, cum_t_ref, cum_r_ref, total_ref, flags_ref, *outs):
+    side = side_of(place_ref, True)
+    flags_ref[...] = flags_of(place_ref[0], pairs, flags_ref.shape)
     cum_t, cum_r = tables(ld_ref[...])
     cum_t_ref[...] = cum_t
     cum_r_ref[...] = cum_r
@@ -80,8 +96,8 @@
     state_into(outs, k_ref, lambda j: v_ref[:, lanes(side, half, j, dim)], tail, side, half, dim)
 
 
-def more_states(half, dim, side_ref, k_ref, v_ref, cum_t_ref, *outs):
-    side = side_ref[0]
+def more_states(half, dim, place_ref, k_ref, v_ref, cum_t_ref, *outs):
+    side = side_of(place_ref, False)
     cum_t = cum_t_ref[...]
     tail = jnp.exp(cum_t[cum_t.shape[0] - 1 :, :] - cum_t)
     state_into(outs, k_ref, lambda j: v_ref[:, lanes(side, half, j, dim)], tail, side, half, dim)
@@ -95,7 +111,7 @@
     return jnp.where(row >= col, jnp.exp(jnp.minimum(gap, 0.0)), 0.0)
 
 
-def within(heads, dim, side_ref, q_ref, k_ref, v_ref, cum_t_ref, cum_r_ref, mixed_ref, inner_ref):
+def within(heads, dim, place_ref, q_ref, k_ref, v_ref, cum_t_ref, cum_r_ref, mixed_ref, inner_ref):
     cum_t, cum_r = cum_t_ref[...], cum_r_ref[...]
     for h in range(heads):
         at = slice(h * dim, (h + 1) * dim)
@@ -105,8 +121,8 @@
         inner_ref[:, at] = dot(mixed, v_ref[:, at], 1, 0)
 
 
-def across(half, dim, start, count, have, last, side_ref, *refs):
-    side = side_ref[0]
+def across(half, dim, give, start, have, last, place_ref, *refs):
+    side = side_of(place_ref, give)
     q_ref, inner_ref, g_ref, gain_ref, cum_t_ref = refs[:5]
     before = refs[5 : 5 + have]
     states = refs[5 + have : -2]
@@ -138,8 +154,8 @@
         sums_ref[1] = cross
 
 
-def gradient(half, dim, full_width, n_sums, n_attn, side_ref, *refs):
-    side = side_ref[0]
+def gradient(half, dim, give, full_width, n_sums, n_attn, place_ref, *refs):
+    side = side_of(place_ref, give)
     q_ref, g_ref, gain_ref, cum_t_ref = refs[:4]
     sums = refs[4 : 4 + n_sums]
     attns = refs[4 + n_sums : 4 + n_sums + n_attn]
@@ -169,8 +185,8 @@
     state_into(outs, q_ref, lambda j: kept[j], lead, side, half, dim)
 
 
-def local_grads(half, dim, chunks, side_ref, *refs):
-    side = side_ref[0]
+def local_grads(half, dim, chunks, place_ref, *refs):
+    side = side_of(place_ref, False)
     q_ref, k_ref, v_ref, cum_t_ref, cum_r_ref, mixed_ref, d_own_ref, d_give_ref = refs[:8]
     states = refs[8 : 8 + 2 * chunks]
     qg_ref, kg_ref, vg_ref = refs[8 + 2 * chunks :]
@@ -199,8 +215,8 @@
                 j += 1
 
 
-def final_grads(half, dim, chunks, side_ref, *refs):
-    side = side_ref[0]
+def final_grads(half, dim, chunks, place_ref, *refs):
+    side = side_of(place_ref, False)
     k_ref, v_ref, cum_t_ref, kg_ref, vg_ref = refs[:5]
     states = refs[5 : 5 + 2 * chunks]
     key_ref, value_ref = refs[5 + 2 * chunks :]
@@ -220,11 +236,10 @@
                 j += 1
 
 
-def carried(mine, theirs, total_mine, total_theirs, place, n_seq, n_dp, reverse):
+def carried(mine, theirs, total_mine, total_theirs, flags, n_seq, n_dp, reverse):
     pairs = n_seq // 2
-    block = n_seq - 1 - place if reverse else place
-    first = block % 2 == 0
-    pair = block // 2
+    first = flags[2 if reverse else 1]
+    base = 2 + pairs if reverse else 3
     swap = [(i, i ^ 1) for i in range(n_seq)]
 
     def hop(a):
@@ -251,7 +266,7 @@
         cuts.append((total_mine[at : at + n, None, :], total_theirs[at : at + n, None, :]))
         at += n
     sums = [
-        jnp.where(first, their_decay, 1.0) * x + jnp.where(first, 1.0, my_decay) * r
+        jnp.where(first > 0.5, their_decay, 1.0) * x + jnp.where(first > 0.5, 1.0, my_decay) * r
         for x, r, (my_decay, their_decay) in zip(mine, received, cuts)
     ]
     both = [a * b for a, b in cuts]
@@ -259,18 +274,24 @@
     outward = sums
     for a in range(pairs - 1):
         got = [lax.ppermute(x, ("seq", "dp"), hop(a)) for x in outward]
-        here = pair == a + 1
+        here = flags[base + a]
         inward = [
-            jnp.where(here, g, 0.0 if e is None else e) for g, e in zip(got, inward)
+            jnp.where(here > 0.5, g, 0.0 if e is None else e) for g, e in zip(got, inward)
         ]
         outward = [s + d * g for s, d, g in zip(sums, both, got)]
     for x, r, e, (my_decay, their_decay) in zip(mine, received, inward, cuts):
         if e is None:
             e = jnp.zeros_like(x)
-        through = jnp.where(first, my_decay, their_decay) * e + jnp.where(first, x, r)
-        kept.append(jnp.where(first, e, through))
-        sent.append(jnp.where(first, through, e))
+        if sent:
+            x, sent[-1] = lax.optimization_barrier((x, sent[-1]))
+        through = jnp.where(first > 0.5, my_decay, their_decay) * e + jnp.where(first > 0.5, x, r)
+        kept.append(jnp.where(first > 0.5, e, through))
+        sent.append(jnp.where(first > 0.5, through, e))
     return kept, [lax.ppermute(x, "seq", swap) for x in sent]
+
+
+def chunk_count(heads):
+    return min(4, heads // 2)
 
 
 def on_device(n_seq, n_dp, queries, keys, values, output_gradient, log_decay, gain):
@@ -278,55 +299,55 @@
     heads = log_decay.shape[0]
     dim = width // heads
     half = heads // 2
-    chunks = min(4, half)
+    chunks = chunk_count(heads)
     sizes = [half // chunks + (1 if i < half % chunks else 0) for i in range(chunks)]
     full_width = width * n_dp
     place = lax.axis_index("seq")
-    own = (place % 2).astype(jnp.int32)
-    own_side = own.reshape(1)
-    give_side = (1 - own).reshape(1)
+    pairs = n_seq // 2
+    place = place.astype(jnp.int32).reshape(1)
+    rows = -(-(1 + 2 * pairs) // 8) * 8
     gain_row = gain.reshape(1, width)
     pair_flops = 2 * tok * dim * dim
     state = [((n, dim, dim), f32) for n in sizes]
     row_bytes = tok * half * dim
 
-    cum_t, cum_r, total, *give = call(
-        functools.partial(first_states, half, dim),
-        [((tok, heads), f32), ((heads, tok), f32), ((heads, dim), f32)] + state,
-        2 * half * pair_flops, 8 * row_bytes, "first_states",
-    )(give_side, keys, values, log_decay)
+    cum_t, cum_r, total, flags, *give = call(
+        functools.partial(first_states, half, dim, pairs),
+        [((tok, heads), f32), ((heads, tok), f32), ((heads, dim), f32), ((rows, dim), f32)] + state,
+        2 * half * pair_flops, 8 * row_bytes,
+    )(place, keys, values, log_decay)
     swap = [(i, i ^ 1) for i in range(n_seq)]
     other = lax.ppermute(total, "seq", swap)
     own_states = call(
-        functools.partial(more_states, half, dim), state, 2 * half * pair_flops, 8 * row_bytes, "more_states"
-    )(own_side, keys, values, cum_t)
+        functools.partial(more_states, half, dim), state, 2 * half * pair_flops, 8 * row_bytes
+    )(place, keys, values, cum_t)
     mixed, inner = call(
         functools.partial(within, heads, dim),
         [((heads, tok, tok), bf16), ((tok, width), f32)],
-        2 * heads * pair_flops, 12 * row_bytes, "within",
-    )(own_side, queries, keys, values, cum_t, cum_r)
-
-    upper = own == 1
+        2 * heads * pair_flops, 12 * row_bytes,
+    )(place, queries, keys, values, cum_t, cum_r)
+
+    upper = flags[0] > 0.5
     total_mine = jnp.where(upper, total[half:], total[:half])
     total_theirs = jnp.where(upper, other[half:], other[:half])
-    in_own, in_give = carried(own_states, give, total_mine, total_theirs, place, n_seq, n_dp, False)
-
-    def outer(side, states, start, before, last, name):
+    in_own, in_give = carried(own_states, give, total_mine, total_theirs, flags, n_seq, n_dp, False)
+
+    def outer(is_give, states, start, before, last):
         count = sum(x.shape[0] for x in states)
         return call(
-            functools.partial(across, half, dim, start, count, len(before), last),
+            functools.partial(across, half, dim, is_give, start, len(before), last),
             [((tok, count * dim), f32), ((8, tok), f32) if last else ((2, tok, dim), f32)],
-            2 * count * pair_flops, 14 * tok * count * dim, name,
-        )(side, queries, inner, output_gradient, gain_row, cum_t, *before, *states)
-
-    attn_own, part = outer(own_side, in_own, 0, [], False, "across_own")
+            2 * count * pair_flops, 14 * tok * count * dim,
+        )(place, queries, inner, output_gradient, gain_row, cum_t, *before, *states)
+
+    attn_own, part = outer(False, in_own, 0, [], False)
     early = sum(sizes[:-1])
     if early:
-        attn_early, more = outer(give_side, in_give[:-1], 0, [part], False, "across_early")
-        attn_late, sums = outer(give_side, in_give[-1:], early, [more], True, "across_late")
+        attn_early, more = outer(True, in_give[:-1], 0, [part], False)
+        attn_late, sums = outer(True, in_give[-1:], early, [more], True)
         attn_give = [attn_early, attn_late]
     else:
-        attn_late, sums = outer(give_side, in_give, 0, [part], True, "across_late")
+        attn_late, sums = outer(True, in_give, 0, [part], True)
         attn_give = [attn_late]
 
     if n_dp <= 4:
@@ -336,22 +357,22 @@
     else:
         all_sums = [lax.psum(sums, "dp")]
 
-    def grads(side, attns, name):
+    def grads(is_give, attns):
         return call(
-            functools.partial(gradient, half, dim, full_width, len(all_sums), len(attns)),
+            functools.partial(gradient, half, dim, is_give, full_width, len(all_sums), len(attns)),
             [((tok, half * dim), bf16), ((half, dim), f32)] + state,
-            2 * half * pair_flops, 14 * row_bytes, name,
-        )(side, queries, output_gradient, gain_row, cum_t, *all_sums, *attns)
-
-    d_give, gain_give, *back_give = grads(give_side, attn_give, "gradient_give")
-    d_own, gain_own, *back_own = grads(own_side, [attn_own], "gradient_own")
+            2 * half * pair_flops, 14 * row_bytes,
+        )(place, queries, output_gradient, gain_row, cum_t, *all_sums, *attns)
+
+    d_give, gain_give, *back_give = grads(True, attn_give)
+    d_own, gain_own, *back_own = grads(False, [attn_own])
     query_grad, key_part, value_part = call(
         functools.partial(local_grads, half, dim, chunks),
         [((tok, width), bf16), ((tok, width), f32), ((tok, width), f32)],
-        6 * heads * pair_flops, 40 * row_bytes, "local_grads",
-    )(own_side, queries, keys, values, cum_t, cum_r, mixed, d_own, d_give, *in_own, *in_give)
-
-    late_own, late_give = carried(back_own, back_give, total_mine, total_theirs, place, n_seq, n_dp, True)
+        6 * heads * pair_flops, 40 * row_bytes,
+    )(place, queries, keys, values, cum_t, cum_r, mixed, d_own, d_give, *in_own, *in_give)
+
+    late_own, late_give = carried(back_own, back_give, total_mine, total_theirs, flags, n_seq, n_dp, True)
 
     gain_grad = jnp.concatenate(
         [jnp.where(upper, gain_give, gain_own), jnp.where(upper, gain_own, gain_give)], axis=0
@@ -364,14 +385,19 @@
     key_grad, value_grad = call(
         functools.partial(final_grads, half, dim, chunks),
         [((tok, width), bf16), ((tok, width), bf16)],
-        4 * heads * pair_flops, 32 * row_bytes, "final_grads",
-    )(own_side, keys, values, cum_t, key_part, value_part, *late_own, *late_give)
+        4 * heads * pair_flops, 32 * row_bytes,
+    )(place, keys, values, cum_t, key_part, value_part, *late_own, *late_give)
     return query_grad, key_grad, value_grad, gain_grad.reshape(width)
 
 
 def solution(mesh):
+    n_seq, n_dp = mesh.shape["seq"], mesh.shape["dp"]
+
+    def body(*args):
+        return on_device(n_seq, n_dp, *args)
+
     return jax.shard_map(
-        functools.partial(on_device, mesh.shape["seq"], mesh.shape["dp"]),
+        body,
         mesh=mesh,
         in_specs=(P("seq", "dp"), P("seq", "dp"), P("seq", "dp"), P("seq", "dp"), P("dp", "seq"), P("dp")),
         out_specs=(P("seq", "dp"), P("seq", "dp"), P("seq", "dp"), P("dp")),

time: 115 us -> 110 us (0.957); the launches traced: 113 us -> 109 us
  local copies, waits for them, and re-layouts: 14.1 us -> 3.71 us
  waiting for transfers between devices: 29.2 us -> 38.6 us
  other arithmetic: 4.2 us -> 1.77 us
    unnamed x56 -> x16, local copies, waits for them, and re-layouts: 14.1 us -> 3.71 us
    ppermute x24, waiting for transfers between devices: 8.02 us -> 12 us  [carried(): got = [lax.ppermute(x, ('seq', 'dp'), hop(a)) for x in outward]]
    ppermute x8, starting transfers between devices: 10.7 us -> 7.46 us  [carried(): return (kept, [lax.ppermute(x, 'seq', swap) for x in sent])]
    ppermute x8, waiting for transfers between devices: 11 us -> 14.2 us  [carried(): return (kept, [lax.ppermute(x, 'seq', swap) for x in sent])]
    ppermute x24, starting transfers between devices: 21.4 us -> 23.4 us  [carried(): got = [lax.ppermute(x, ('seq', 'dp'), hop(a)) for x in outward]]
    add x8, other arithmetic: 1.96 us -> 0.17 us  [carried(): jnp.where(first > 0.5, their_decay, 1.0) * x]
    ppermute x8, waiting for transfers between devices: 5.65 us -> 7.1 us  [carried(): received = [lax.ppermute(x, 'seq', swap) for x in theirs]]
  transfers between devices with their start and end apart: 47 -> 47, of which waited for: 17 -> 19; matrix products, arithmetic and copies ran while one was open for 4% -> 2% of each run, Pallas kernels for 7% -> 7%
where the time goes in v2:
time: 110 us; the launch traced here: 109 us
  starting transfers between devices  51.8 us (47%)
  waiting for transfers between devices  38.6 us (35%)
  Pallas kernels  12.6 us (11%)
  local copies, waits for them, and re-layouts  3.71 us (3%)
  other arithmetic  1.77 us (2%)
    ppermute x24, starting transfers between devices, carried(): got = [lax.ppermute(x, ('seq', 'dp'), hop(a)) for x in outward]  23.4 us
    ppermute x8, waiting for transfers between devices, carried(): return (kept, [lax.ppermute(x, 'seq', swap) for x in sent])  14.2 us
    pallas_call x10, Pallas kernels, run(): pl.pallas_call(body, out_shape=[jax.ShapeDtypeStruct(*o) for o in outs],...  12.6 us
    ppermute x24, waiting for transfers between devices, carried(): got = [lax.ppermute(x, ('seq', 'dp'), hop(a)) for x in outward]  12 us
    ppermute x8, starting transfers between devices, carried(): received = [lax.ppermute(x, 'seq', swap) for x in theirs]  8.1 us
    ppermute x3, starting transfers between devices, on_device(): lax.ppermute(gain_grad, 'seq', [(i, i ^ step) for i in range(n_seq)])  7.84 us
    ppermute x8, starting transfers between devices, carried(): return (kept, [lax.ppermute(x, 'seq', swap) for x in sent])  7.46 us
    ppermute x8, waiting for transfers between devices, carried(): received = [lax.ppermute(x, 'seq', swap) for x in theirs]  7.1 us
  transfers between devices with their start and end apart: 47, of which 19 were waited for; matrix products, arithmetic and copies ran while one was open for 2% of the time, Pallas kernels for 7%

profile of v2, /device:TPU:0, one launch (start us, length us, event | category | flops | bytes accessed | tf_op | source)
XLA Modules:
  0.0 109.5 jit_solution(12166868609478627110)
XLA Ops:
  4.3 3.1 %collective-permute-start = (f32[16,128]{1,0:T(8,128)S(1)}, f32[16,128]{1,0:T(8,128)S(1)}, u32[]{:S(2)}, u32[]{:S(2)}) collective-permute-start(f32[16,128]{1,0:T(8,128)S(1)} %get-tuple-element.58), channel_id=1, source_target_pairs={{0,4},{4,0},{8,12},{12,8},{16,20},{20,16},{24,28},{28,24},{1,5},{5... | collective-permute-start | bytes 24584 | tf_op jit(solution)/shard_map/ppermute | solution.py:320
  7.4 1.9 %collective-permute-start.5 = (f32[2,128,128]{2,1,0:T(8,128)S(1)}, f32[2,128,128]{2,1,0:T(8,128)S(1)}, u32[]{:S(2)}, u32[]{:S(2)}) collective-permute-start(f32[2,128,128]{2,1,0:T(8,128)S(1)} %get-tuple-element.62), channel_id=1, source_target_pairs={{0,4},{4,0},{8,12},{12,8},{16,20},{20,16},{24,28},{28,24},{1,5},{5... | collective-permute-start | bytes 393224 | tf_op jit(solution)/shard_map/ppermute | solution.py:260
  9.4 1.9 %collective-permute-start.13 = (f32[2,128,128]{2,1,0:T(8,128)S(1)}, f32[2,128,128]{2,1,0:T(8,128)S(1)}, u32[]{:S(2)}, u32[]{:S(2)}) collective-permute-start(f32[2,128,128]{2,1,0:T(8,128)S(1)} %get-tuple-element.68), channel_id=1, source_target_pairs={{0,4},{4,0},{8,12},{12,8},{16,20},{20,16},{24,28},{28,24},{1,5},{5... | collective-permute-start | bytes 393224 | tf_op jit(solution)/shard_map/ppermute | solution.py:260
  11.4 2.6 %shard_map.94 = (bf16[16,128,128]{2,1,0:T(8,128)(2,1)S(1)}, f32[128,2048]{1,0:T(8,128)S(1)}) custom-call(s32[1]{0:T(128)} %bitcast.place_ref, bf16[128,2048]{1,0:T(8,128)(2,1)S(1)} %copy-done, bf16[128,2048]{1,0:T(8,128)(2,1)S(1)} %copy-done.1, bf16[128,2048]{1,0:T(8,128)(2,1)S(1)} %copy-done.3, ...), custom_call_target="tpu_custom_call" | custom-call | flops 134217728 | bytes 1572864 | tf_op jit(solution)/shard_map/pallas_call | solution.py:22
  14.8 1.6 %collective-permute-start.2 = (f32[2,128,128]{2,1,0:T(8,128)S(1)}, f32[2,128,128]{2,1,0:T(8,128)S(1)}, u32[]{:S(2)}, u32[]{:S(2)}) collective-permute-start(f32[2,128,128]{2,1,0:T(8,128)S(1)} %multiply_add_fusion.23), channel_id=1, source_target_pairs={{0,8},{1,9},{2,10},{3,11},{4,12},{5,13},{6,14},{7,15},{8,0},{9,1},... | collective-permute-start | bytes 393224 | tf_op jit(solution)/shard_map/ppermute | solution.py:276
  16.5 4.3 %collective-permute-done.13 = f32[2,128,128]{2,1,0:T(8,128)S(1)} collective-permute-done((f32[2,128,128]{2,1,0:T(8,128)S(1)}, f32[2,128,128]{2,1,0:T(8,128)S(1)}, u32[]{:S(2)}, u32[]{:S(2)}) %collective-permute-start.13) | collective-permute-done | bytes 131104 | tf_op jit(solution)/shard_map/ppermute | solution.py:260
  20.7 1.6 %collective-permute-start.14 = (f32[2,128,128]{2,1,0:T(8,128)S(1)}, f32[2,128,128]{2,1,0:T(8,128)S(1)}, u32[]{:S(2)}, u32[]{:S(2)}) collective-permute-start(f32[2,128,128]{2,1,0:T(8,128)S(1)} %multiply_add_fusion.14), channel_id=1, source_target_pairs={{0,8},{1,9},{2,10},{3,11},{4,12},{5,13},{6,14},{7,15},{8,0},{9,1},... | collective-permute-start | bytes 393224 | tf_op jit(solution)/shard_map/ppermute | solution.py:276
  23.0 1.6 %collective-permute-start.6 = (f32[2,128,128]{2,1,0:T(8,128)S(1)}, f32[2,128,128]{2,1,0:T(8,128)S(1)}, u32[]{:S(2)}, u32[]{:S(2)}) collective-permute-start(f32[2,128,128]{2,1,0:T(8,128)S(1)} %multiply_add_fusion.20), channel_id=1, source_target_pairs={{0,8},{1,9},{2,10},{3,11},{4,12},{5,13},{6,14},{7,15},{8,0},{9,1},... | collective-permute-start | bytes 393224 | tf_op jit(solution)/shard_map/ppermute | solution.py:276
  24.7 2.5 %collective-permute-done.14 = f32[2,128,128]{2,1,0:T(8,128)S(1)} collective-permute-done((f32[2,128,128]{2,1,0:T(8,128)S(1)}, f32[2,128,128]{2,1,0:T(8,128)S(1)}, u32[]{:S(2)}, u32[]{:S(2)}) %collective-permute-start.14) | collective-permute-done | bytes 131104 | tf_op jit(solution)/shard_map/ppermute | solution.py:276
  27.3 1.8 %collective-permute-done.10 = f32[2,128,128]{2,1,0:T(8,128)S(1)} collective-permute-done((f32[2,128,128]{2,1,0:T(8,128)S(1)}, f32[2,128,128]{2,1,0:T(8,128)S(1)}, u32[]{:S(2)}, u32[]{:S(2)}) %collective-permute-start.10) | collective-permute-done | bytes 131104 | tf_op jit(solution)/shard_map/ppermute | solution.py:276
  38.7 5.6 %collective-permute-done.19.refs_8_.refs_14_ = f32[2,128,128]{2,1,0:T(8,128)S(1)} collective-permute-done((f32[2,128,128]{2,1,0:T(8,128)S(1)}, f32[2,128,128]{2,1,0:T(8,128)S(1)}, u32[]{:S(2)}, u32[]{:S(2)}) %collective-permute-start.19) | collective-permute-done | bytes 131104 | tf_op jit(solution)/shard_map/ppermute | solution.py:290
  44.3 2.2 %collective-permute-done.18.refs_7_.refs_13_ = f32[2,128,128]{2,1,0:T(8,128)S(1)} collective-permute-done((f32[2,128,128]{2,1,0:T(8,128)S(1)}, f32[2,128,128]{2,1,0:T(8,128)S(1)}, u32[]{:S(2)}, u32[]{:S(2)}) %collective-permute-start.18) | collective-permute-done | bytes 131104 | tf_op jit(solution)/shard_map/ppermute | solution.py:290
  53.9 3.0 %collective-permute-done.44 = f32[16,128]{1,0:T(8,128)S(1)} collective-permute-done((f32[16,128]{1,0:T(8,128)S(1)}, f32[16,128]{1,0:T(8,128)S(1)}, u32[]{:S(2)}, u32[]{:S(2)}) %collective-permute-start.44) | collective-permute-done | bytes 8224 | tf_op jit(solution)/shard_map/ppermute | solution.py:382
  56.9 6.2 %collective-permute-start.45 = (f32[16,128]{1,0:T(8,128)S(1)}, f32[16,128]{1,0:T(8,128)S(1)}, u32[]{:S(2)}, u32[]{:S(2)}) collective-permute-start(f32[16,128]{1,0:T(8,128)S(1)} %fusion.16), channel_id=1, source_target_pairs={{0,8},{4,12},{8,0},{12,4},{16,24},{20,28},{24,16},{28,20},{1,9},{5... | collective-permute-start | bytes 24584 | tf_op jit(solution)/shard_map/ppermute | solution.py:382
  63.7 1.4 %collective-permute-start.28 = (f32[2,128,128]{2,1,0:T(8,128)S(1)}, f32[2,128,128]{2,1,0:T(8,128)S(1)}, u32[]{:S(2)}, u32[]{:S(2)}) collective-permute-start(f32[2,128,128]{2,1,0:T(8,128)S(1)} %get-tuple-element.87), channel_id=1, source_target_pairs={{0,4},{4,0},{8,12},{12,8},{16,20},{20,16},{24,28},{28,24},{1,5},{5... | collective-permute-start | bytes 393224 | tf_op jit(solution)/shard_map/ppermute | solution.py:260
  65.7 1.4 %collective-permute-start.36 = (f32[2,128,128]{2,1,0:T(8,128)S(1)}, f32[2,128,128]{2,1,0:T(8,128)S(1)}, u32[]{:S(2)}, u32[]{:S(2)}) collective-permute-start(f32[2,128,128]{2,1,0:T(8,128)S(1)} %get-tuple-element.93), channel_id=1, source_target_pairs={{0,4},{4,0},{8,12},{12,8},{16,20},{20,16},{24,28},{28,24},{1,5},{5... | collective-permute-start | bytes 393224 | tf_op jit(solution)/shard_map/ppermute | solution.py:260
  68.1 3.6 %shard_map.101 = (bf16[128,2048]{1,0:T(8,128)(2,1)}, f32[128,2048]{1,0:T(8,128)S(1)}, f32[128,2048]{1,0:T(8,128)S(1)}) custom-call(s32[1]{0:T(128)} %bitcast.place_ref, bf16[128,2048]{1,0:T(8,128)(2,1)S(1)} %copy-done, bf16[128,2048]{1,0:T(8,128)(2,1)S(1)} %copy-done.2, bf16[128,2048]{1,0:T(8,128)(2,1)S(1)} %copy-done.4, ...), custom_call_target="tpu_custom_call" | custom-call | flops 402653184 | bytes 5242880 | tf_op jit(solution)/shard_map/pallas_call | solution.py:22
  72.4 2.8 %collective-permute-done.36 = f32[2,128,128]{2,1,0:T(8,128)S(1)} collective-permute-done((f32[2,128,128]{2,1,0:T(8,128)S(1)}, f32[2,128,128]{2,1,0:T(8,128)S(1)}, u32[]{:S(2)}, u32[]{:S(2)}) %collective-permute-start.36) | collective-permute-done | bytes 131104 | tf_op jit(solution)/shard_map/ppermute | solution.py:260
  77.6 10.5 %collective-permute-start.27 = (f32[2,128,128]{2,1,0:T(8,128)S(1)}, f32[2,128,128]{2,1,0:T(8,128)S(1)}, u32[]{:S(2)}, u32[]{:S(2)}) collective-permute-start(f32[2,128,128]{2,1,0:T(8,128)S(1)} %multiply_add_fusion.9), channel_id=1, source_target_pairs={{0,8},{1,9},{2,10},{3,11},{4,12},{5,13},{6,14},{7,15},{8,0},{9,1},... | collective-permute-start | bytes 393224 | tf_op jit(solution)/shard_map/ppermute | solution.py:276
  88.3 2.1 %collective-permute-start.35 = (f32[2,128,128]{2,1,0:T(8,128)S(1)}, f32[2,128,128]{2,1,0:T(8,128)S(1)}, u32[]{:S(2)}, u32[]{:S(2)}) collective-permute-start(f32[2,128,128]{2,1,0:T(8,128)S(1)} %multiply_add_fusion.3), channel_id=1, source_target_pairs={{0,8},{1,9},{2,10},{3,11},{4,12},{5,13},{6,14},{7,15},{8,0},{9,1},... | collective-permute-start | bytes 393224 | tf_op jit(solution)/shard_map/ppermute | solution.py:276
  90.4 1.4 %collective-permute-start.31 = (f32[2,128,128]{2,1,0:T(8,128)S(1)}, f32[2,128,128]{2,1,0:T(8,128)S(1)}, u32[]{:S(2)}, u32[]{:S(2)}) collective-permute-start(f32[2,128,128]{2,1,0:T(8,128)S(1)} %multiply_add_fusion.6), channel_id=1, source_target_pairs={{0,8},{1,9},{2,10},{3,11},{4,12},{5,13},{6,14},{7,15},{8,0},{9,1},... | collective-permute-start | bytes 393224 | tf_op jit(solution)/shard_map/ppermute | solution.py:276
  93.3 5.1 %collective-permute-done.31 = f32[2,128,128]{2,1,0:T(8,128)S(1)} collective-permute-done((f32[2,128,128]{2,1,0:T(8,128)S(1)}, f32[2,128,128]{2,1,0:T(8,128)S(1)}, u32[]{:S(2)}, u32[]{:S(2)}) %collective-permute-start.31) | collective-permute-done | bytes 131104 | tf_op jit(solution)/shard_map/ppermute | solution.py:276
  101.6 2.9 %collective-permute-done.43.refs_12_ = f32[2,128,128]{2,1,0:T(8,128)S(1)} collective-permute-done((f32[2,128,128]{2,1,0:T(8,128)S(1)}, f32[2,128,128]{2,1,0:T(8,128)S(1)}, u32[]{:S(2)}, u32[]{:S(2)}) %collective-permute-start.43) | collective-permute-done | bytes 131104 | tf_op jit(solution)/shard_map/ppermute | solution.py:290
  107.3 2.1 %shard_map.102 = (bf16[128,2048]{1,0:T(8,128)(2,1)}, bf16[128,2048]{1,0:T(8,128)(2,1)}) custom-call(s32[1]{0:T(128)} %bitcast.place_ref, bf16[128,2048]{1,0:T(8,128)(2,1)S(1)} %copy-done.2, bf16[128,2048]{1,0:T(8,128)(2,1)S(1)} %copy-done.4, f32[128,16]{1,0:T(8,128)S(1)} %get-tuple-element.53.cum_t_ref.refs_4_.refs_3_.refs_2_, ...), custom_call_target="tpu_custom_call" | custom-call | flops 268435456 | bytes 4194304 | tf_op jit(solution)/shard_map/pallas_call | solution.py:22
  (140 shorter events, 34.9 us)
Async XLA Ops:
  4.3 10.4 %collective-permute-start = (f32[16,128]{1,0:T(8,128)S(1)}, f32[16,128]{1,0:T(8,128)S(1)}, u32[]{:S(2)}, u32[]{:S(2)}) collective-permute-start(f32[16,128]{1,0:T(8,128)S(1)} %get-tuple-element.58), channel_id=1, source_target_pairs={{0,4},{4,0},{8,12},{12,8},{16,20},{20,16},{24,28},{28,24},{1,5},{5... | collective-permute-start | bytes 24584 | tf_op jit(solution)/shard_map/ppermute | solution.py:320
  7.3 7.4 %collective-permute-start.1 = (f32[2,128,128]{2,1,0:T(8,128)S(1)}, f32[2,128,128]{2,1,0:T(8,128)S(1)}, u32[]{:S(2)}, u32[]{:S(2)}) collective-permute-start(f32[2,128,128]{2,1,0:T(8,128)S(1)} %get-tuple-element.60), channel_id=1, source_target_pairs={{0,4},{4,0},{8,12},{12,8},{16,20},{20,16},{24,28},{28,24},{1,5},{5... | collective-permute-start | bytes 393224 | tf_op jit(solution)/shard_map/ppermute | solution.py:260
  7.4 15.5 %collective-permute-start.5 = (f32[2,128,128]{2,1,0:T(8,128)S(1)}, f32[2,128,128]{2,1,0:T(8,128)S(1)}, u32[]{:S(2)}, u32[]{:S(2)}) collective-permute-start(f32[2,128,128]{2,1,0:T(8,128)S(1)} %get-tuple-element.62), channel_id=1, source_target_pairs={{0,4},{4,0},{8,12},{12,8},{16,20},{20,16},{24,28},{28,24},{1,5},{5... | collective-permute-start | bytes 393224 | tf_op jit(solution)/shard_map/ppermute | solution.py:260
  9.4 13.0 %collective-permute-start.9 = (f32[2,128,128]{2,1,0:T(8,128)S(1)}, f32[2,128,128]{2,1,0:T(8,128)S(1)}, u32[]{:S(2)}, u32[]{:S(2)}) collective-permute-start(f32[2,128,128]{2,1,0:T(8,128)S(1)} %get-tuple-element.65), channel_id=1, source_target_pairs={{0,4},{4,0},{8,12},{12,8},{16,20},{20,16},{24,28},{28,24},{1,5},{5... | collective-permute-start | bytes 393224 | tf_op jit(solution)/shard_map/ppermute | solution.py:260
  9.4 11.3 %collective-permute-start.13 = (f32[2,128,128]{2,1,0:T(8,128)S(1)}, f32[2,128,128]{2,1,0:T(8,128)S(1)}, u32[]{:S(2)}, u32[]{:S(2)}) collective-permute-start(f32[2,128,128]{2,1,0:T(8,128)S(1)} %get-tuple-element.68), channel_id=1, source_target_pairs={{0,4},{4,0},{8,12},{12,8},{16,20},{20,16},{24,28},{28,24},{1,5},{5... | collective-permute-start | bytes 393224 | tf_op jit(solution)/shard_map/ppermute | solution.py:260
  14.8 9.8 %collective-permute-start.2 = (f32[2,128,128]{2,1,0:T(8,128)S(1)}, f32[2,128,128]{2,1,0:T(8,128)S(1)}, u32[]{:S(2)}, u32[]{:S(2)}) collective-permute-start(f32[2,128,128]{2,1,0:T(8,128)S(1)} %multiply_add_fusion.23), channel_id=1, source_target_pairs={{0,8},{1,9},{2,10},{3,11},{4,12},{5,13},{6,14},{7,15},{8,0},{9,1},... | collective-permute-start | bytes 393224 | tf_op jit(solution)/shard_map/ppermute | solution.py:276
  22.4 6.7 %collective-permute-start.10 = (f32[2,128,128]{2,1,0:T(8,128)S(1)}, f32[2,128,128]{2,1,0:T(8,128)S(1)}, u32[]{:S(2)}, u32[]{:S(2)}) collective-permute-start(f32[2,128,128]{2,1,0:T(8,128)S(1)} %multiply_add_fusion.17), channel_id=1, source_target_pairs={{0,8},{1,9},{2,10},{3,11},{4,12},{5,13},{6,14},{7,15},{8,0},{9,1},... | collective-permute-start | bytes 393224 | tf_op jit(solution)/shard_map/ppermute | solution.py:276
  23.0 7.6 %collective-permute-start.6 = (f32[2,128,128]{2,1,0:T(8,128)S(1)}, f32[2,128,128]{2,1,0:T(8,128)S(1)}, u32[]{:S(2)}, u32[]{:S(2)}) collective-permute-start(f32[2,128,128]{2,1,0:T(8,128)S(1)} %multiply_add_fusion.20), channel_id=1, source_target_pairs={{0,8},{1,9},{2,10},{3,11},{4,12},{5,13},{6,14},{7,15},{8,0},{9,1},... | collective-permute-start | bytes 393224 | tf_op jit(solution)/shard_map/ppermute | solution.py:276
  33.6 13.3 %collective-permute-start.20 = (f32[2,128,128]{2,1,0:T(8,128)S(1)}, f32[2,128,128]{2,1,0:T(8,128)S(1)}, u32[]{:S(2)}, u32[]{:S(2)}) collective-permute-start(f32[2,128,128]{2,1,0:T(8,128)S(1)} %get-tuple-element.110), channel_id=1, source_target_pairs={{0,4},{4,0},{8,12},{12,8},{16,20},{20,16},{24,28},{28,24},{1,5},{5... | collective-permute-start | bytes 393224 | tf_op jit(solution)/shard_map/ppermute | solution.py:290
  34.6 9.7 %collective-permute-start.19 = (f32[2,128,128]{2,1,0:T(8,128)S(1)}, f32[2,128,128]{2,1,0:T(8,128)S(1)}, u32[]{:S(2)}, u32[]{:S(2)}) collective-permute-start(f32[2,128,128]{2,1,0:T(8,128)S(1)} %get-tuple-element.73), channel_id=1, source_target_pairs={{0,4},{4,0},{8,12},{12,8},{16,20},{20,16},{24,28},{28,24},{1,5},{5... | collective-permute-start | bytes 393224 | tf_op jit(solution)/shard_map/ppermute | solution.py:290
  35.7 10.8 %collective-permute-start.18 = (f32[2,128,128]{2,1,0:T(8,128)S(1)}, f32[2,128,128]{2,1,0:T(8,128)S(1)}, u32[]{:S(2)}, u32[]{:S(2)}) collective-permute-start(f32[2,128,128]{2,1,0:T(8,128)S(1)} %get-tuple-element.72), channel_id=1, source_target_pairs={{0,4},{4,0},{8,12},{12,8},{16,20},{20,16},{24,28},{28,24},{1,5},{5... | collective-permute-start | bytes 393224 | tf_op jit(solution)/shard_map/ppermute | solution.py:290
  56.9 10.2 %collective-permute-start.45 = (f32[16,128]{1,0:T(8,128)S(1)}, f32[16,128]{1,0:T(8,128)S(1)}, u32[]{:S(2)}, u32[]{:S(2)}) collective-permute-start(f32[16,128]{1,0:T(8,128)S(1)} %fusion.16), channel_id=1, source_target_pairs={{0,8},{4,12},{8,0},{12,4},{16,24},{20,28},{24,16},{28,20},{1,9},{5... | collective-permute-start | bytes 24584 | tf_op jit(solution)/shard_map/ppermute | solution.py:382
  63.1 9.2 %collective-permute-start.24 = (f32[2,128,128]{2,1,0:T(8,128)S(1)}, f32[2,128,128]{2,1,0:T(8,128)S(1)}, u32[]{:S(2)}, u32[]{:S(2)}) collective-permute-start(f32[2,128,128]{2,1,0:T(8,128)S(1)} %get-tuple-element.85), channel_id=1, source_target_pairs={{0,4},{4,0},{8,12},{12,8},{16,20},{20,16},{24,28},{28,24},{1,5},{5... | collective-permute-start | bytes 393224 | tf_op jit(solution)/shard_map/ppermute | solution.py:260
  63.7 12.2 %collective-permute-start.28 = (f32[2,128,128]{2,1,0:T(8,128)S(1)}, f32[2,128,128]{2,1,0:T(8,128)S(1)}, u32[]{:S(2)}, u32[]{:S(2)}) collective-permute-start(f32[2,128,128]{2,1,0:T(8,128)S(1)} %get-tuple-element.87), channel_id=1, source_target_pairs={{0,4},{4,0},{8,12},{12,8},{16,20},{20,16},{24,28},{28,24},{1,5},{5... | collective-permute-start | bytes 393224 | tf_op jit(solution)/shard_map/ppermute | solution.py:260
  65.1 10.2 %collective-permute-start.32 = (f32[2,128,128]{2,1,0:T(8,128)S(1)}, f32[2,128,128]{2,1,0:T(8,128)S(1)}, u32[]{:S(2)}, u32[]{:S(2)}) collective-permute-start(f32[2,128,128]{2,1,0:T(8,128)S(1)} %get-tuple-element.90), channel_id=1, source_target_pairs={{0,4},{4,0},{8,12},{12,8},{16,20},{20,16},{24,28},{28,24},{1,5},{5... | collective-permute-start | bytes 393224 | tf_op jit(solution)/shard_map/ppermute | solution.py:260
  65.7 9.5 %collective-permute-start.36 = (f32[2,128,128]{2,1,0:T(8,128)S(1)}, f32[2,128,128]{2,1,0:T(8,128)S(1)}, u32[]{:S(2)}, u32[]{:S(2)}) collective-permute-start(f32[2,128,128]{2,1,0:T(8,128)S(1)} %get-tuple-element.93), channel_id=1, source_target_pairs={{0,4},{4,0},{8,12},{12,8},{16,20},{20,16},{24,28},{28,24},{1,5},{5... | collective-permute-start | bytes 393224 | tf_op jit(solution)/shard_map/ppermute | solution.py:260
  76.7 11.5 %collective-permute-start.38 = (f32[2,128,128]{2,1,0:T(8,128)S(1)}, f32[2,128,128]{2,1,0:T(8,128)S(1)}, u32[]{:S(2)}, u32[]{:S(2)}) collective-permute-start(f32[2,128,128]{2,1,0:T(8,128)S(1)} %multiply_add_fusion.1), channel_id=1, source_target_pairs={{0,1},{1,0},{2,3},{3,2},{4,5},{5,4},{6,7},{7,6},{8,16},{9,17},{10,... | collective-permute-start | bytes 393224 | tf_op jit(solution)/shard_map/ppermute | solution.py:276
  76.9 11.4 %collective-permute-start.34 = (f32[2,128,128]{2,1,0:T(8,128)S(1)}, f32[2,128,128]{2,1,0:T(8,128)S(1)}, u32[]{:S(2)}, u32[]{:S(2)}) collective-permute-start(f32[2,128,128]{2,1,0:T(8,128)S(1)} %multiply_add_fusion.4), channel_id=1, source_target_pairs={{0,1},{1,0},{2,3},{3,2},{4,5},{5,4},{6,7},{7,6},{8,16},{9,17},{10,... | collective-permute-start | bytes 393224 | tf_op jit(solution)/shard_map/ppermute | solution.py:276
  77.4 13.0 %collective-permute-start.30 = (f32[2,128,128]{2,1,0:T(8,128)S(1)}, f32[2,128,128]{2,1,0:T(8,128)S(1)}, u32[]{:S(2)}, u32[]{:S(2)}) collective-permute-start(f32[2,128,128]{2,1,0:T(8,128)S(1)} %multiply_add_fusion.7), channel_id=1, source_target_pairs={{0,1},{1,0},{2,3},{3,2},{4,5},{5,4},{6,7},{7,6},{8,16},{9,17},{10,... | collective-permute-start | bytes 393224 | tf_op jit(solution)/shard_map/ppermute | solution.py:276
  77.6 14.9 %collective-permute-start.27 = (f32[2,128,128]{2,1,0:T(8,128)S(1)}, f32[2,128,128]{2,1,0:T(8,128)S(1)}, u32[]{:S(2)}, u32[]{:S(2)}) collective-permute-start(f32[2,128,128]{2,1,0:T(8,128)S(1)} %multiply_add_fusion.9), channel_id=1, source_target_pairs={{0,8},{1,9},{2,10},{3,11},{4,12},{5,13},{6,14},{7,15},{8,0},{9,1},... | collective-permute-start | bytes 393224 | tf_op jit(solution)/shard_map/ppermute | solution.py:276
  88.2 10.4 %collective-permute-start.39 = (f32[2,128,128]{2,1,0:T(8,128)S(1)}, f32[2,128,128]{2,1,0:T(8,128)S(1)}, u32[]{:S(2)}, u32[]{:S(2)}) collective-permute-start(f32[2,128,128]{2,1,0:T(8,128)S(1)} %multiply_add_fusion), channel_id=1, source_target_pairs={{0,8},{1,9},{2,10},{3,11},{4,12},{5,13},{6,14},{7,15},{8,0},{9,1},... | collective-permute-start | bytes 393224 | tf_op jit(solution)/shard_map/ppermute | solution.py:276
  88.3 10.2 %collective-permute-start.35 = (f32[2,128,128]{2,1,0:T(8,128)S(1)}, f32[2,128,128]{2,1,0:T(8,128)S(1)}, u32[]{:S(2)}, u32[]{:S(2)}) collective-permute-start(f32[2,128,128]{2,1,0:T(8,128)S(1)} %multiply_add_fusion.3), channel_id=1, source_target_pairs={{0,8},{1,9},{2,10},{3,11},{4,12},{5,13},{6,14},{7,15},{8,0},{9,1},... | collective-permute-start | bytes 393224 | tf_op jit(solution)/shard_map/ppermute | solution.py:276
  90.4 8.1 %collective-permute-start.31 = (f32[2,128,128]{2,1,0:T(8,128)S(1)}, f32[2,128,128]{2,1,0:T(8,128)S(1)}, u32[]{:S(2)}, u32[]{:S(2)}) collective-permute-start(f32[2,128,128]{2,1,0:T(8,128)S(1)} %multiply_add_fusion.6), channel_id=1, source_target_pairs={{0,8},{1,9},{2,10},{3,11},{4,12},{5,13},{6,14},{7,15},{8,0},{9,1},... | collective-permute-start | bytes 393224 | tf_op jit(solution)/shard_map/ppermute | solution.py:276
  92.5 9.1 %collective-permute-start.40 = (f32[2,128,128]{2,1,0:T(8,128)S(1)}, f32[2,128,128]{2,1,0:T(8,128)S(1)}, u32[]{:S(2)}, u32[]{:S(2)}) collective-permute-start(f32[2,128,128]{2,1,0:T(8,128)S(1)} %get-tuple-element.95), channel_id=1, source_target_pairs={{0,4},{4,0},{8,12},{12,8},{16,20},{20,16},{24,28},{28,24},{1,5},{5... | collective-permute-start | bytes 393224 | tf_op jit(solution)/shard_map/ppermute | solution.py:290
  (31 other events, 124.4 us)

commit v3 on v2

--- a/solution.py
+++ b/solution.py
@@ -14,16 +14,20 @@
 bf16 = jnp.bfloat16
 VMEM = pl.BlockSpec(memory_space=pltpu.VMEM)
 SMEM = pl.BlockSpec(memory_space=pltpu.SMEM)
+HBM = pl.BlockSpec(memory_space=pltpu.HBM)
 GRANT = 24 * 2**20
 
 
-def call(body, outs, flops, moved):
+def call(body, outs, flops, moved, in_hbm=(), outs_in_hbm=False, scratch=(), aliases=None):
     def run(place, *arrays):
+        arrays = [pltpu.with_memory_space_constraint(x, pltpu.HBM) if i in in_hbm and not aliases else x for i, x in enumerate(arrays)]
         return pl.pallas_call(
             body,
             out_shape=[jax.ShapeDtypeStruct(*o) for o in outs],
-            in_specs=[SMEM] + [VMEM] * len(arrays),
-            out_specs=[VMEM] * len(outs),
+            in_specs=[SMEM] + [HBM if i in in_hbm else VMEM for i in range(len(arrays))],
+            out_specs=[HBM if outs_in_hbm else VMEM] * len(outs),
+            scratch_shapes=list(scratch),
+            input_output_aliases=aliases or {},
             compiler_params=pltpu.CompilerParams(vmem_limit_bytes=GRANT),
             cost_estimate=pl.CostEstimate(flops=flops, bytes_accessed=moved, transcendentals=0),
         )(place, *arrays)
@@ -74,33 +78,60 @@
     return cum_t, cum_r
 
 
-def state_into(outs, a_ref, b_of, factor, side, half, dim):
-    j = 0
+def state_into(outs, a_of, b_of, factor, side, half, start=0):
+    j = start
     for out in outs:
         for i in range(out.shape[0]):
-            hi, lo = split(a_ref[:, lanes(side, half, j, dim)].astype(f32) * column(factor, side, half, j))
+            hi, lo = split(a_of(j).astype(f32) * column(factor, side, half, j))
             b = b_of(j)
             out[i] = dot(hi, b, 0, 0) + dot(lo, b, 0, 0)
             j += 1
 
 
-def first_states(half, dim, pairs, place_ref, k_ref, v_ref, ld_ref, cum_t_ref, cum_r_ref, total_ref, flags_ref, *outs):
+def first_states(half, dim, pairs, place_ref, k_ref, v_ref, ld_ref, cum_t_ref, cum_r_ref, total_ref, flags_ref, *refs):
+    outs, (k_buf, v_buf, ld_buf, sems) = refs[:-4], refs[-4:]
     side = side_of(place_ref, True)
+    copies = [pltpu.make_async_copy(ld_ref, ld_buf, sems.at[0])]
+    at = 0
+    for c, out in enumerate(outs):
+        size = out.shape[0] * dim
+        source = pl.ds(pl.multiple_of((side * half) * dim + at, dim), size)
+        for n, (ref, buf) in enumerate(((k_ref, k_buf), (v_ref, v_buf))):
+            copies.append(pltpu.make_async_copy(ref.at[:, source], buf.at[:, at : at + size], sems.at[1 + 2 * c + n]))
+        at += size
+    for copy in copies:
+        copy.start()
     flags_ref[...] = flags_of(place_ref[0], pairs, flags_ref.shape)
-    cum_t, cum_r = tables(ld_ref[...])
+    copies[0].wait()
+    cum_t, cum_r = tables(ld_buf[...])
     cum_t_ref[...] = cum_t
     cum_r_ref[...] = cum_r
     tok = cum_t.shape[0]
     total_ref[...] = jnp.broadcast_to(jnp.exp(cum_r[:, tok - 1 :]), total_ref.shape)
     tail = jnp.exp(cum_t[tok - 1 :, :] - cum_t)
-    state_into(outs, k_ref, lambda j: v_ref[:, lanes(side, half, j, dim)], tail, side, half, dim)
+    start = 0
+    for c, out in enumerate(outs):
+        copies[1 + 2 * c].wait()
+        copies[2 + 2 * c].wait()
+        state_into(
+            [out],
+            lambda j: k_buf[:, j * dim : (j + 1) * dim],
+            lambda j: v_buf[:, j * dim : (j + 1) * dim],
+            tail, side, half, start,
+        )
+        start += out.shape[0]
 
 
 def more_states(half, dim, place_ref, k_ref, v_ref, cum_t_ref, *outs):
     side = side_of(place_ref, False)
     cum_t = cum_t_ref[...]
     tail = jnp.exp(cum_t[cum_t.shape[0] - 1 :, :] - cum_t)
-    state_into(outs, k_ref, lambda j: v_ref[:, lanes(side, half, j, dim)], tail, side, half, dim)
+    state_into(
+        outs,
+        lambda j: k_ref[:, lanes(side, half, j, dim)],
+        lambda j: v_ref[:, lanes(side, half, j, dim)],
+        tail, side, half,
+    )
 
 
 def weights_of(cum_t, cum_r, h):
@@ -182,7 +213,7 @@
             gain_part_ref[j : j + 1, :] = jnp.sum(g * normed, axis=0, keepdims=True)
             kept[j] = d
             j += 1
-    state_into(outs, q_ref, lambda j: kept[j], lead, side, half, dim)
+    state_into(outs, lambda j: q_ref[:, lanes(side, half, j, dim)], lambda j: kept[j], lead, side, half)
 
 
 def local_grads(half, dim, chunks, place_ref, *refs):
@@ -215,25 +246,32 @@
                 j += 1
 
 
-def final_grads(half, dim, chunks, place_ref, *refs):
-    side = side_of(place_ref, False)
+def final_grads(half, dim, parts, skip, place_ref, *refs):
     k_ref, v_ref, cum_t_ref, kg_ref, vg_ref = refs[:5]
-    states = refs[5 : 5 + 2 * chunks]
-    key_ref, value_ref = refs[5 + 2 * chunks :]
+    states = refs[5 : 5 + len(parts)]
+    key_ref, value_ref, key_buf, value_buf, sems = refs[5 + len(parts) + skip :]
     cum_t = cum_t_ref[...]
     tail = jnp.exp(cum_t[cum_t.shape[0] - 1 :, :] - cum_t)
-    for s, group in enumerate((states[:chunks], states[chunks:])):
-        which = side if s == 0 else 1 - side
-        j = 0
-        for ref in group:
-            for i in range(ref.shape[0]):
-                at = lanes(which, half, j, dim)
-                tail_col = column(tail, which, half, j)
-                hi, lo = split(ref[i])
-                v, k = v_ref[:, at], k_ref[:, at]
-                key_ref[:, at] = (kg_ref[:, at] + (dot(v, hi, 1, 1) + dot(v, lo, 1, 1)) * tail_col).astype(bf16)
-                value_ref[:, at] = (vg_ref[:, at] + (dot(k, hi, 1, 0) + dot(k, lo, 1, 0)) * tail_col).astype(bf16)
-                j += 1
+    copies = []
+    at = 0
+    for n, (ref, (give, j)) in enumerate(zip(states, parts)):
+        side = side_of(place_ref, give)
+        size = ref.shape[0] * dim
+        target = pl.ds(pl.multiple_of((side * half + j) * dim, dim), size)
+        for i in range(ref.shape[0]):
+            here = lanes(side, half, j + i, dim)
+            to = slice(at + i * dim, at + (i + 1) * dim)
+            tail_col = column(tail, side, half, j + i)
+            hi, lo = split(ref[i])
+            v, k = v_ref[:, here], k_ref[:, here]
+            key_buf[:, to] = (kg_ref[:, here] + (dot(v, hi, 1, 1) + dot(v, lo, 1, 1)) * tail_col).astype(bf16)
+            value_buf[:, to] = (vg_ref[:, here] + (dot(k, hi, 1, 0) + dot(k, lo, 1, 0)) * tail_col).astype(bf16)
+        for m, (buf, out) in enumerate(((key_buf, key_ref), (value_buf, value_ref))):
+            copies.append(pltpu.make_async_copy(buf.at[:, at : at + size], out.at[:, target], sems.at[2 * n + m]))
+            copies[-1].start()
+        at += size
+    for copy in copies:
+        copy.wait()
 
 
 def carried(mine, theirs, total_mine, total_theirs, flags, n_seq, n_dp, reverse):
@@ -315,6 +353,13 @@
         functools.partial(first_states, half, dim, pairs),
         [((tok, heads), f32), ((heads, tok), f32), ((heads, dim), f32), ((rows, dim), f32)] + state,
         2 * half * pair_flops, 8 * row_bytes,
+        in_hbm=(0, 1, 2),
+        scratch=[
+            pltpu.VMEM((tok, half * dim), bf16),
+            pltpu.VMEM((tok, half * dim), bf16),
+            pltpu.VMEM((heads, tok), f32),
+            pltpu.SemaphoreType.DMA((1 + 2 * chunks,)),
+        ],
     )(place, keys, values, log_decay)
     swap = [(i, i ^ 1) for i in range(n_seq)]
     other = lax.ppermute(total, "seq", swap)
@@ -382,11 +427,28 @@
         gain_grad = gain_grad + lax.ppermute(gain_grad, "seq", [(i, i ^ step) for i in range(n_seq)])
         step *= 2
 
-    key_grad, value_grad = call(
-        functools.partial(final_grads, half, dim, chunks),
-        [((tok, width), bf16), ((tok, width), bf16)],
-        4 * heads * pair_flops, 32 * row_bytes,
-    )(place, keys, values, cum_t, key_part, value_part, *late_own, *late_give)
+    places = [sum(sizes[:c]) for c in range(chunks)]
+
+    def finish(parts, states, before):
+        count = sum(x.shape[0] for x in states)
+        return call(
+            functools.partial(final_grads, half, dim, parts, len(before)),
+            [((tok, width), bf16), ((tok, width), bf16)],
+            4 * count * pair_flops, 20 * tok * count * dim,
+            in_hbm=range(5 + len(parts), 7 + len(parts)),
+            outs_in_hbm=True,
+            scratch=[
+                pltpu.VMEM((tok, count * dim), bf16),
+                pltpu.VMEM((tok, count * dim), bf16),
+                pltpu.SemaphoreType.DMA((2 * len(parts),)),
+            ],
+            aliases={6 + len(parts): 0, 7 + len(parts): 1} if before else None,
+        )(place, keys, values, cum_t, key_part, value_part, *states, *before)
+
+    own_parts = [(False, p) for p in places]
+    give_parts = [(True, p) for p in places]
+    begun = finish(own_parts + give_parts[:-1], late_own + late_give[:-1], [])
+    key_grad, value_grad = finish(give_parts[-1:], late_give[-1:], list(begun))
     return query_grad, key_grad, value_grad, gain_grad.reshape(width)
 
 

time: 110 us -> 106 us (0.964)
  waiting for transfers between devices: 38.6 us -> 25.7 us
  starting transfers between devices: 51.8 us -> 60 us
  Pallas kernels: 12.6 us -> 14.9 us
  local copies, waits for them, and re-layouts: 3.71 us -> 1.98 us
    ppermute x24, starting transfers between devices: 23.4 us -> 30.2 us  [carried(): got = [lax.ppermute(x, ('seq', 'dp'), hop(a)) for x in outward]]
    ppermute x8, waiting for transfers between devices: 7.1 us -> 3.22 us  [carried(): received = [lax.ppermute(x, 'seq', swap) for x in theirs]]
    ppermute x24, waiting for transfers between devices: 12 us -> 8.89 us  [carried(): got = [lax.ppermute(x, ('seq', 'dp'), hop(a)) for x in outward]]
    ppermute x3, waiting for transfers between devices: 2.98 us -> 0.01 us  [on_device(): lax.ppermute(gain_grad, 'seq', [(i, i ^ step) for i in range(n_seq)])]
    ppermute x8, waiting for transfers between devices: 14.2 us -> 11.2 us  [carried(): return (kept, [lax.ppermute(x, 'seq', swap) for x in sent])]
    pallas_call x10 -> x11, Pallas kernels: 12.6 us -> 14.9 us  [run(): pl.pallas_call(body, out_shape=[jax.ShapeDtypeStruct(*o) for o in outs],...]
    unnamed x16 -> x12, local copies, waits for them, and re-layouts: 3.71 us -> 1.98 us
    ppermute x8, starting transfers between devices: 7.46 us -> 8.86 us  [carried(): return (kept, [lax.ppermute(x, 'seq', swap) for x in sent])]
  transfers between devices with their start and end apart: 47 -> 47, of which waited for: 19 -> 19; matrix products, arithmetic and copies ran while one was open for 2% -> 2% of each run, Pallas kernels for 7% -> 9%
where the time goes in v3:
time: 106 us; the launch traced here: 105 us
  starting transfers between devices  60 us (57%)
  waiting for transfers between devices  25.7 us (24%)
  Pallas kernels  14.9 us (14%)
  local copies, waits for them, and re-layouts  1.98 us (2%)
  other arithmetic  1.74 us (2%)
    ppermute x24, starting transfers between devices, carried(): got = [lax.ppermute(x, ('seq', 'dp'), hop(a)) for x in outward]  30.2 us
    pallas_call x11, Pallas kernels, run(): pl.pallas_call(body, out_shape=[jax.ShapeDtypeStruct(*o) for o in outs],...  14.9 us
    ppermute x8, waiting for transfers between devices, carried(): return (kept, [lax.ppermute(x, 'seq', swap) for x in sent])  11.2 us
    ppermute x24, waiting for transfers between devices, carried(): got = [lax.ppermute(x, ('seq', 'dp'), hop(a)) for x in outward]  8.89 us
    ppermute x8, starting transfers between devices, carried(): return (kept, [lax.ppermute(x, 'seq', swap) for x in sent])  8.86 us
    ppermute x8, starting transfers between devices, carried(): received = [lax.ppermute(x, 'seq', swap) for x in theirs]  8.1 us
    ppermute x3, starting transfers between devices, on_device(): lax.ppermute(gain_grad, 'seq', [(i, i ^ step) for i in range(n_seq)])  7.83 us
    ppermute x8, waiting for transfers between devices, carried(): received = [lax.ppermute(x, 'seq', swap) for x in theirs]  3.22 us
  transfers between devices with their start and end apart: 47, of which 19 were waited for; matrix products, arithmetic and copies ran while one was open for 2% of the time, Pallas kernels for 9%

profile of v3, /device:TPU:0, one launch (start us, length us, event | category | flops | bytes accessed | tf_op | source)
XLA Modules:
  0.0 105.4 jit_solution(1167308312132948455)
XLA Ops:
  0.7 2.6 %shard_map.93 = (f32[128,16]{1,0:T(8,128)S(1)}, f32[16,128]{1,0:T(8,128)S(1)}, f32[16,128]{1,0:T(8,128)S(1)}, f32[16,128]{1,0:T(8,128)S(1)}, f32[2,128,128]{2,1,...) custom-call(s32[1]{0:T(128)} %bitcast.place_ref, ...), custom_call_target="tpu_custom_call" | custom-call | flops 67108864 | bytes 1048576 | tf_op jit(solution)/shard_map/pallas_call | solution.py:24
  3.3 3.1 %collective-permute-start = (f32[16,128]{1,0:T(8,128)S(1)}, f32[16,128]{1,0:T(8,128)S(1)}, u32[]{:S(2)}, u32[]{:S(2)}) collective-permute-start(f32[16,128]{1,0:T(8,128)S(1)} %get-tuple-element.60), channel_id=1, source_target_pairs={{0,4},{4,0},{8,12},{12,8},{16,20},{20,16},{24,28},{28,24},{1,5},{5... | collective-permute-start | bytes 24584 | tf_op jit(solution)/shard_map/ppermute | solution.py:365
  6.4 1.9 %collective-permute-start.5 = (f32[2,128,128]{2,1,0:T(8,128)S(1)}, f32[2,128,128]{2,1,0:T(8,128)S(1)}, u32[]{:S(2)}, u32[]{:S(2)}) collective-permute-start(f32[2,128,128]{2,1,0:T(8,128)S(1)} %get-tuple-element.64), channel_id=1, source_target_pairs={{0,4},{4,0},{8,12},{12,8},{16,20},{20,16},{24,28},{28,24},{1,5},{5... | collective-permute-start | bytes 393224 | tf_op jit(solution)/shard_map/ppermute | solution.py:298
  8.5 1.9 %collective-permute-start.13 = (f32[2,128,128]{2,1,0:T(8,128)S(1)}, f32[2,128,128]{2,1,0:T(8,128)S(1)}, u32[]{:S(2)}, u32[]{:S(2)}) collective-permute-start(f32[2,128,128]{2,1,0:T(8,128)S(1)} %get-tuple-element.70), channel_id=1, source_target_pairs={{0,4},{4,0},{8,12},{12,8},{16,20},{20,16},{24,28},{28,24},{1,5},{5... | collective-permute-start | bytes 393224 | tf_op jit(solution)/shard_map/ppermute | solution.py:298
  11.5 2.6 %shard_map.94 = (bf16[16,128,128]{2,1,0:T(8,128)(2,1)S(1)}, f32[128,2048]{1,0:T(8,128)S(1)}) custom-call(s32[1]{0:T(128)} %bitcast.place_ref, bf16[128,2048]{1,0:T(8,128)(2,1)S(1)} %copy-done, bf16[128,2048]{1,0:T(8,128)(2,1)S(1)} %copy-done.1, bf16[128,2048]{1,0:T(8,128)(2,1)S(1)} %copy-done.2, ...), custom_call_target="tpu_custom_call" | custom-call | flops 134217728 | bytes 1572864 | tf_op jit(solution)/shard_map/pallas_call | solution.py:24
  14.9 1.6 %collective-permute-start.2 = (f32[2,128,128]{2,1,0:T(8,128)S(1)}, f32[2,128,128]{2,1,0:T(8,128)S(1)}, u32[]{:S(2)}, u32[]{:S(2)}) collective-permute-start(f32[2,128,128]{2,1,0:T(8,128)S(1)} %multiply_add_fusion.23), channel_id=1, source_target_pairs={{0,8},{1,9},{2,10},{3,11},{4,12},{5,13},{6,14},{7,15},{8,0},{9,1},... | collective-permute-start | bytes 393224 | tf_op jit(solution)/shard_map/ppermute | solution.py:314
  16.5 3.2 %collective-permute-done.13 = f32[2,128,128]{2,1,0:T(8,128)S(1)} collective-permute-done((f32[2,128,128]{2,1,0:T(8,128)S(1)}, f32[2,128,128]{2,1,0:T(8,128)S(1)}, u32[]{:S(2)}, u32[]{:S(2)}) %collective-permute-start.13) | collective-permute-done | bytes 131104 | tf_op jit(solution)/shard_map/ppermute | solution.py:298
  19.8 1.6 %collective-permute-start.14 = (f32[2,128,128]{2,1,0:T(8,128)S(1)}, f32[2,128,128]{2,1,0:T(8,128)S(1)}, u32[]{:S(2)}, u32[]{:S(2)}) collective-permute-start(f32[2,128,128]{2,1,0:T(8,128)S(1)} %multiply_add_fusion.14), channel_id=1, source_target_pairs={{0,8},{1,9},{2,10},{3,11},{4,12},{5,13},{6,14},{7,15},{8,0},{9,1},... | collective-permute-start | bytes 393224 | tf_op jit(solution)/shard_map/ppermute | solution.py:314
  22.0 1.6 %collective-permute-start.6 = (f32[2,128,128]{2,1,0:T(8,128)S(1)}, f32[2,128,128]{2,1,0:T(8,128)S(1)}, u32[]{:S(2)}, u32[]{:S(2)}) collective-permute-start(f32[2,128,128]{2,1,0:T(8,128)S(1)} %multiply_add_fusion.20), channel_id=1, source_target_pairs={{0,8},{1,9},{2,10},{3,11},{4,12},{5,13},{6,14},{7,15},{8,0},{9,1},... | collective-permute-start | bytes 393224 | tf_op jit(solution)/shard_map/ppermute | solution.py:314
  23.7 2.5 %collective-permute-done.14 = f32[2,128,128]{2,1,0:T(8,128)S(1)} collective-permute-done((f32[2,128,128]{2,1,0:T(8,128)S(1)}, f32[2,128,128]{2,1,0:T(8,128)S(1)}, u32[]{:S(2)}, u32[]{:S(2)}) %collective-permute-start.14) | collective-permute-done | bytes 131104 | tf_op jit(solution)/shard_map/ppermute | solution.py:314
  26.3 1.8 %collective-permute-done.10 = f32[2,128,128]{2,1,0:T(8,128)S(1)} collective-permute-done((f32[2,128,128]{2,1,0:T(8,128)S(1)}, f32[2,128,128]{2,1,0:T(8,128)S(1)}, u32[]{:S(2)}, u32[]{:S(2)}) %collective-permute-start.10) | collective-permute-done | bytes 131104 | tf_op jit(solution)/shard_map/ppermute | solution.py:314
  37.7 5.6 %collective-permute-done.19.refs_8_.refs_14_ = f32[2,128,128]{2,1,0:T(8,128)S(1)} collective-permute-done((f32[2,128,128]{2,1,0:T(8,128)S(1)}, f32[2,128,128]{2,1,0:T(8,128)S(1)}, u32[]{:S(2)}, u32[]{:S(2)}) %collective-permute-start.19) | collective-permute-done | bytes 131104 | tf_op jit(solution)/shard_map/ppermute | solution.py:328
  43.3 2.2 %collective-permute-done.18.refs_7_.refs_13_ = f32[2,128,128]{2,1,0:T(8,128)S(1)} collective-permute-done((f32[2,128,128]{2,1,0:T(8,128)S(1)}, f32[2,128,128]{2,1,0:T(8,128)S(1)}, u32[]{:S(2)}, u32[]{:S(2)}) %collective-permute-start.18) | collective-permute-done | bytes 131104 | tf_op jit(solution)/shard_map/ppermute | solution.py:328
  52.9 1.4 %collective-permute-start.24 = (f32[2,128,128]{2,1,0:T(8,128)S(1)}, f32[2,128,128]{2,1,0:T(8,128)S(1)}, u32[]{:S(2)}, u32[]{:S(2)}) collective-permute-start(f32[2,128,128]{2,1,0:T(8,128)S(1)} %get-tuple-element.87), channel_id=1, source_target_pairs={{0,4},{4,0},{8,12},{12,8},{16,20},{20,16},{24,28},{28,24},{1,5},{5... | collective-permute-start | bytes 393224 | tf_op jit(solution)/shard_map/ppermute | solution.py:298
  54.9 1.4 %collective-permute-start.32 = (f32[2,128,128]{2,1,0:T(8,128)S(1)}, f32[2,128,128]{2,1,0:T(8,128)S(1)}, u32[]{:S(2)}, u32[]{:S(2)}) collective-permute-start(f32[2,128,128]{2,1,0:T(8,128)S(1)} %get-tuple-element.91), channel_id=1, source_target_pairs={{0,4},{4,0},{8,12},{12,8},{16,20},{20,16},{24,28},{28,24},{1,5},{5... | collective-permute-start | bytes 393224 | tf_op jit(solution)/shard_map/ppermute | solution.py:298
  57.0 6.1 %collective-permute-start.45 = (f32[16,128]{1,0:T(8,128)S(1)}, f32[16,128]{1,0:T(8,128)S(1)}, u32[]{:S(2)}, u32[]{:S(2)}) collective-permute-start(f32[16,128]{1,0:T(8,128)S(1)} %fusion.16), channel_id=1, source_target_pairs={{0,8},{4,12},{8,0},{12,4},{16,24},{20,28},{24,16},{28,20},{1,9},{5... | collective-permute-start | bytes 24584 | tf_op jit(solution)/shard_map/ppermute | solution.py:427
  63.0 3.6 %shard_map.101 = (bf16[128,2048]{1,0:T(8,128)(2,1)}, f32[128,2048]{1,0:T(8,128)S(1)}, f32[128,2048]{1,0:T(8,128)S(1)}) custom-call(s32[1]{0:T(128)} %bitcast.place_ref, bf16[128,2048]{1,0:T(8,128)(2,1)S(1)} %copy-done, bf16[128,2048]{1,0:T(8,128)(2,1)S(1)} %copy-done.1, bf16[128,2048]{1,0:T(8,128)(2,1)S(1)} %copy-done.3, ...), custom_call_target="tpu_custom_call" | custom-call | flops 402653184 | bytes 5242880 | tf_op jit(solution)/shard_map/pallas_call | solution.py:24
  70.6 17.0 %collective-permute-start.39 = (f32[2,128,128]{2,1,0:T(8,128)S(1)}, f32[2,128,128]{2,1,0:T(8,128)S(1)}, u32[]{:S(2)}, u32[]{:S(2)}) collective-permute-start(f32[2,128,128]{2,1,0:T(8,128)S(1)} %multiply_add_fusion), channel_id=1, source_target_pairs={{0,8},{1,9},{2,10},{3,11},{4,12},{5,13},{6,14},{7,15},{8,0},{9,1},... | collective-permute-start | bytes 393224 | tf_op jit(solution)/shard_map/ppermute | solution.py:314
  87.7 2.1 %collective-permute-start.31 = (f32[2,128,128]{2,1,0:T(8,128)S(1)}, f32[2,128,128]{2,1,0:T(8,128)S(1)}, u32[]{:S(2)}, u32[]{:S(2)}) collective-permute-start(f32[2,128,128]{2,1,0:T(8,128)S(1)} %multiply_add_fusion.6), channel_id=1, source_target_pairs={{0,8},{1,9},{2,10},{3,11},{4,12},{5,13},{6,14},{7,15},{8,0},{9,1},... | collective-permute-start | bytes 393224 | tf_op jit(solution)/shard_map/ppermute | solution.py:314
  89.8 1.4 %collective-permute-start.27 = (f32[2,128,128]{2,1,0:T(8,128)S(1)}, f32[2,128,128]{2,1,0:T(8,128)S(1)}, u32[]{:S(2)}, u32[]{:S(2)}) collective-permute-start(f32[2,128,128]{2,1,0:T(8,128)S(1)} %multiply_add_fusion.9), channel_id=1, source_target_pairs={{0,8},{1,9},{2,10},{3,11},{4,12},{5,13},{6,14},{7,15},{8,0},{9,1},... | collective-permute-start | bytes 393224 | tf_op jit(solution)/shard_map/ppermute | solution.py:314
  92.0 1.3 %collective-permute-start.41 = (f32[2,128,128]{2,1,0:T(8,128)S(1)}, f32[2,128,128]{2,1,0:T(8,128)S(1)}, u32[]{:S(2)}, u32[]{:S(2)}) collective-permute-start(f32[2,128,128]{2,1,0:T(8,128)S(1)} %fusion.9), channel_id=1, source_target_pairs={{0,4},{4,0},{8,12},{12,8},{16,20},{20,16},{24,28},{28,24},{1,5},{5... | collective-permute-start | bytes 393224 | tf_op jit(solution)/shard_map/ppermute | solution.py:328
  93.3 1.4 %collective-permute-done.35 = f32[2,128,128]{2,1,0:T(8,128)S(1)} collective-permute-done((f32[2,128,128]{2,1,0:T(8,128)S(1)}, f32[2,128,128]{2,1,0:T(8,128)S(1)}, u32[]{:S(2)}, u32[]{:S(2)}) %collective-permute-start.35) | collective-permute-done | bytes 131104 | tf_op jit(solution)/shard_map/ppermute | solution.py:314
  101.1 1.5 %collective-permute-done.43.refs_11_ = f32[2,128,128]{2,1,0:T(8,128)S(1)} collective-permute-done((f32[2,128,128]{2,1,0:T(8,128)S(1)}, f32[2,128,128]{2,1,0:T(8,128)S(1)}, u32[]{:S(2)}, u32[]{:S(2)}) %collective-permute-start.43) | collective-permute-done | bytes 131104 | tf_op jit(solution)/shard_map/ppermute | solution.py:328
  102.6 1.8 %shard_map.102 = (bf16[128,2048]{1,0:T(8,128)(2,1)}, bf16[128,2048]{1,0:T(8,128)(2,1)}) custom-call(s32[1]{0:T(128)} %bitcast.place_ref, bf16[128,2048]{1,0:T(8,128)(2,1)S(1)} %copy-done.1, bf16[128,2048]{1,0:T(8,128)(2,1)S(1)} %copy-done.3, f32[128,16]{1,0:T(8,128)S(1)} %get-tuple-element.55.cum_t_ref.refs_4_.refs_3_.refs_2_, ...), custom_call_target="tpu_custom_call" | custom-call | flops 234881024 | bytes 4587520 | tf_op jit(solution)/shard_map/pallas_call | solution.py:24
  (140 shorter events, 33.0 us)
Async XLA Ops:
  3.3 11.5 %collective-permute-start = (f32[16,128]{1,0:T(8,128)S(1)}, f32[16,128]{1,0:T(8,128)S(1)}, u32[]{:S(2)}, u32[]{:S(2)}) collective-permute-start(f32[16,128]{1,0:T(8,128)S(1)} %get-tuple-element.60), channel_id=1, source_target_pairs={{0,4},{4,0},{8,12},{12,8},{16,20},{20,16},{24,28},{28,24},{1,5},{5... | collective-permute-start | bytes 24584 | tf_op jit(solution)/shard_map/ppermute | solution.py:365
  6.4 8.5 %collective-permute-start.1 = (f32[2,128,128]{2,1,0:T(8,128)S(1)}, f32[2,128,128]{2,1,0:T(8,128)S(1)}, u32[]{:S(2)}, u32[]{:S(2)}) collective-permute-start(f32[2,128,128]{2,1,0:T(8,128)S(1)} %get-tuple-element.62), channel_id=1, source_target_pairs={{0,4},{4,0},{8,12},{12,8},{16,20},{20,16},{24,28},{28,24},{1,5},{5... | collective-permute-start | bytes 393224 | tf_op jit(solution)/shard_map/ppermute | solution.py:298
  6.4 15.5 %collective-permute-start.5 = (f32[2,128,128]{2,1,0:T(8,128)S(1)}, f32[2,128,128]{2,1,0:T(8,128)S(1)}, u32[]{:S(2)}, u32[]{:S(2)}) collective-permute-start(f32[2,128,128]{2,1,0:T(8,128)S(1)} %get-tuple-element.64), channel_id=1, source_target_pairs={{0,4},{4,0},{8,12},{12,8},{16,20},{20,16},{24,28},{28,24},{1,5},{5... | collective-permute-start | bytes 393224 | tf_op jit(solution)/shard_map/ppermute | solution.py:298
  8.4 13.0 %collective-permute-start.9 = (f32[2,128,128]{2,1,0:T(8,128)S(1)}, f32[2,128,128]{2,1,0:T(8,128)S(1)}, u32[]{:S(2)}, u32[]{:S(2)}) collective-permute-start(f32[2,128,128]{2,1,0:T(8,128)S(1)} %get-tuple-element.67), channel_id=1, source_target_pairs={{0,4},{4,0},{8,12},{12,8},{16,20},{20,16},{24,28},{28,24},{1,5},{5... | collective-permute-start | bytes 393224 | tf_op jit(solution)/shard_map/ppermute | solution.py:298
  8.5 11.3 %collective-permute-start.13 = (f32[2,128,128]{2,1,0:T(8,128)S(1)}, f32[2,128,128]{2,1,0:T(8,128)S(1)}, u32[]{:S(2)}, u32[]{:S(2)}) collective-permute-start(f32[2,128,128]{2,1,0:T(8,128)S(1)} %get-tuple-element.70), channel_id=1, source_target_pairs={{0,4},{4,0},{8,12},{12,8},{16,20},{20,16},{24,28},{28,24},{1,5},{5... | collective-permute-start | bytes 393224 | tf_op jit(solution)/shard_map/ppermute | solution.py:298
  14.9 8.7 %collective-permute-start.2 = (f32[2,128,128]{2,1,0:T(8,128)S(1)}, f32[2,128,128]{2,1,0:T(8,128)S(1)}, u32[]{:S(2)}, u32[]{:S(2)}) collective-permute-start(f32[2,128,128]{2,1,0:T(8,128)S(1)} %multiply_add_fusion.23), channel_id=1, source_target_pairs={{0,8},{1,9},{2,10},{3,11},{4,12},{5,13},{6,14},{7,15},{8,0},{9,1},... | collective-permute-start | bytes 393224 | tf_op jit(solution)/shard_map/ppermute | solution.py:314
  22.0 7.6 %collective-permute-start.6 = (f32[2,128,128]{2,1,0:T(8,128)S(1)}, f32[2,128,128]{2,1,0:T(8,128)S(1)}, u32[]{:S(2)}, u32[]{:S(2)}) collective-permute-start(f32[2,128,128]{2,1,0:T(8,128)S(1)} %multiply_add_fusion.20), channel_id=1, source_target_pairs={{0,8},{1,9},{2,10},{3,11},{4,12},{5,13},{6,14},{7,15},{8,0},{9,1},... | collective-permute-start | bytes 393224 | tf_op jit(solution)/shard_map/ppermute | solution.py:314
  32.6 13.3 %collective-permute-start.20 = (f32[2,128,128]{2,1,0:T(8,128)S(1)}, f32[2,128,128]{2,1,0:T(8,128)S(1)}, u32[]{:S(2)}, u32[]{:S(2)}) collective-permute-start(f32[2,128,128]{2,1,0:T(8,128)S(1)} %get-tuple-element.114), channel_id=1, source_target_pairs={{0,4},{4,0},{8,12},{12,8},{16,20},{20,16},{24,28},{28,24},{1,5},{5... | collective-permute-start | bytes 393224 | tf_op jit(solution)/shard_map/ppermute | solution.py:328
  33.6 9.7 %collective-permute-start.19 = (f32[2,128,128]{2,1,0:T(8,128)S(1)}, f32[2,128,128]{2,1,0:T(8,128)S(1)}, u32[]{:S(2)}, u32[]{:S(2)}) collective-permute-start(f32[2,128,128]{2,1,0:T(8,128)S(1)} %get-tuple-element.75), channel_id=1, source_target_pairs={{0,4},{4,0},{8,12},{12,8},{16,20},{20,16},{24,28},{28,24},{1,5},{5... | collective-permute-start | bytes 393224 | tf_op jit(solution)/shard_map/ppermute | solution.py:328
  34.7 10.8 %collective-permute-start.18 = (f32[2,128,128]{2,1,0:T(8,128)S(1)}, f32[2,128,128]{2,1,0:T(8,128)S(1)}, u32[]{:S(2)}, u32[]{:S(2)}) collective-permute-start(f32[2,128,128]{2,1,0:T(8,128)S(1)} %get-tuple-element.74), channel_id=1, source_target_pairs={{0,4},{4,0},{8,12},{12,8},{16,20},{20,16},{24,28},{28,24},{1,5},{5... | collective-permute-start | bytes 393224 | tf_op jit(solution)/shard_map/ppermute | solution.py:328
  52.9 15.6 %collective-permute-start.24 = (f32[2,128,128]{2,1,0:T(8,128)S(1)}, f32[2,128,128]{2,1,0:T(8,128)S(1)}, u32[]{:S(2)}, u32[]{:S(2)}) collective-permute-start(f32[2,128,128]{2,1,0:T(8,128)S(1)} %get-tuple-element.87), channel_id=1, source_target_pairs={{0,4},{4,0},{8,12},{12,8},{16,20},{20,16},{24,28},{28,24},{1,5},{5... | collective-permute-start | bytes 393224 | tf_op jit(solution)/shard_map/ppermute | solution.py:298
  54.3 14.1 %collective-permute-start.28 = (f32[2,128,128]{2,1,0:T(8,128)S(1)}, f32[2,128,128]{2,1,0:T(8,128)S(1)}, u32[]{:S(2)}, u32[]{:S(2)}) collective-permute-start(f32[2,128,128]{2,1,0:T(8,128)S(1)} %get-tuple-element.89), channel_id=1, source_target_pairs={{0,4},{4,0},{8,12},{12,8},{16,20},{20,16},{24,28},{28,24},{1,5},{5... | collective-permute-start | bytes 393224 | tf_op jit(solution)/shard_map/ppermute | solution.py:298
  54.9 12.9 %collective-permute-start.32 = (f32[2,128,128]{2,1,0:T(8,128)S(1)}, f32[2,128,128]{2,1,0:T(8,128)S(1)}, u32[]{:S(2)}, u32[]{:S(2)}) collective-permute-start(f32[2,128,128]{2,1,0:T(8,128)S(1)} %get-tuple-element.91), channel_id=1, source_target_pairs={{0,4},{4,0},{8,12},{12,8},{16,20},{20,16},{24,28},{28,24},{1,5},{5... | collective-permute-start | bytes 393224 | tf_op jit(solution)/shard_map/ppermute | solution.py:298
  56.3 11.4 %collective-permute-start.36 = (f32[2,128,128]{2,1,0:T(8,128)S(1)}, f32[2,128,128]{2,1,0:T(8,128)S(1)}, u32[]{:S(2)}, u32[]{:S(2)}) collective-permute-start(f32[2,128,128]{2,1,0:T(8,128)S(1)} %get-tuple-element.93), channel_id=1, source_target_pairs={{0,4},{4,0},{8,12},{12,8},{16,20},{20,16},{24,28},{28,24},{1,5},{5... | collective-permute-start | bytes 393224 | tf_op jit(solution)/shard_map/ppermute | solution.py:298
  57.0 9.7 %collective-permute-start.45 = (f32[16,128]{1,0:T(8,128)S(1)}, f32[16,128]{1,0:T(8,128)S(1)}, u32[]{:S(2)}, u32[]{:S(2)}) collective-permute-start(f32[16,128]{1,0:T(8,128)S(1)} %fusion.16), channel_id=1, source_target_pairs={{0,8},{4,12},{8,0},{12,4},{16,24},{20,28},{24,16},{28,20},{1,9},{5... | collective-permute-start | bytes 24584 | tf_op jit(solution)/shard_map/ppermute | solution.py:427
  66.7 32.6 %collective-permute-start.46 = (f32[16,128]{1,0:T(8,128)S(1)}, f32[16,128]{1,0:T(8,128)S(1)}, u32[]{:S(2)}, u32[]{:S(2)}) collective-permute-start(f32[16,128]{1,0:T(8,128)S(1)} %add.138), channel_id=1, source_target_pairs={{0,16},{4,20},{8,24},{12,28},{16,0},{20,4},{24,8},{28,12},{1,17},{... | collective-permute-start | bytes 24584 | tf_op jit(solution)/shard_map/ppermute | solution.py:427
  69.4 18.2 %collective-permute-start.34 = (f32[2,128,128]{2,1,0:T(8,128)S(1)}, f32[2,128,128]{2,1,0:T(8,128)S(1)}, u32[]{:S(2)}, u32[]{:S(2)}) collective-permute-start(f32[2,128,128]{2,1,0:T(8,128)S(1)} %multiply_add_fusion.4), channel_id=1, source_target_pairs={{0,1},{1,0},{2,3},{3,2},{4,5},{5,4},{6,7},{7,6},{8,16},{9,17},{10,... | collective-permute-start | bytes 393224 | tf_op jit(solution)/shard_map/ppermute | solution.py:314
  69.8 17.8 %collective-permute-start.30 = (f32[2,128,128]{2,1,0:T(8,128)S(1)}, f32[2,128,128]{2,1,0:T(8,128)S(1)}, u32[]{:S(2)}, u32[]{:S(2)}) collective-permute-start(f32[2,128,128]{2,1,0:T(8,128)S(1)} %multiply_add_fusion.7), channel_id=1, source_target_pairs={{0,1},{1,0},{2,3},{3,2},{4,5},{5,4},{6,7},{7,6},{8,16},{9,17},{10,... | collective-permute-start | bytes 393224 | tf_op jit(solution)/shard_map/ppermute | solution.py:314
  70.1 19.7 %collective-permute-start.26 = (f32[2,128,128]{2,1,0:T(8,128)S(1)}, f32[2,128,128]{2,1,0:T(8,128)S(1)}, u32[]{:S(2)}, u32[]{:S(2)}) collective-permute-start(f32[2,128,128]{2,1,0:T(8,128)S(1)} %multiply_add_fusion.10), channel_id=1, source_target_pairs={{0,1},{1,0},{2,3},{3,2},{4,5},{5,4},{6,7},{7,6},{8,16},{9,17},{10,... | collective-permute-start | bytes 393224 | tf_op jit(solution)/shard_map/ppermute | solution.py:314
  70.6 21.3 %collective-permute-start.39 = (f32[2,128,128]{2,1,0:T(8,128)S(1)}, f32[2,128,128]{2,1,0:T(8,128)S(1)}, u32[]{:S(2)}, u32[]{:S(2)}) collective-permute-start(f32[2,128,128]{2,1,0:T(8,128)S(1)} %multiply_add_fusion), channel_id=1, source_target_pairs={{0,8},{1,9},{2,10},{3,11},{4,12},{5,13},{6,14},{7,15},{8,0},{9,1},... | collective-permute-start | bytes 393224 | tf_op jit(solution)/shard_map/ppermute | solution.py:314
  87.6 7.1 %collective-permute-start.35 = (f32[2,128,128]{2,1,0:T(8,128)S(1)}, f32[2,128,128]{2,1,0:T(8,128)S(1)}, u32[]{:S(2)}, u32[]{:S(2)}) collective-permute-start(f32[2,128,128]{2,1,0:T(8,128)S(1)} %multiply_add_fusion.3), channel_id=1, source_target_pairs={{0,8},{1,9},{2,10},{3,11},{4,12},{5,13},{6,14},{7,15},{8,0},{9,1},... | collective-permute-start | bytes 393224 | tf_op jit(solution)/shard_map/ppermute | solution.py:314
  87.7 8.9 %collective-permute-start.31 = (f32[2,128,128]{2,1,0:T(8,128)S(1)}, f32[2,128,128]{2,1,0:T(8,128)S(1)}, u32[]{:S(2)}, u32[]{:S(2)}) collective-permute-start(f32[2,128,128]{2,1,0:T(8,128)S(1)} %multiply_add_fusion.6), channel_id=1, source_target_pairs={{0,8},{1,9},{2,10},{3,11},{4,12},{5,13},{6,14},{7,15},{8,0},{9,1},... | collective-permute-start | bytes 393224 | tf_op jit(solution)/shard_map/ppermute | solution.py:314
  89.8 8.2 %collective-permute-start.27 = (f32[2,128,128]{2,1,0:T(8,128)S(1)}, f32[2,128,128]{2,1,0:T(8,128)S(1)}, u32[]{:S(2)}, u32[]{:S(2)}) collective-permute-start(f32[2,128,128]{2,1,0:T(8,128)S(1)} %multiply_add_fusion.9), channel_id=1, source_target_pairs={{0,8},{1,9},{2,10},{3,11},{4,12},{5,13},{6,14},{7,15},{8,0},{9,1},... | collective-permute-start | bytes 393224 | tf_op jit(solution)/shard_map/ppermute | solution.py:314
  92.0 7.9 %collective-permute-start.41 = (f32[2,128,128]{2,1,0:T(8,128)S(1)}, f32[2,128,128]{2,1,0:T(8,128)S(1)}, u32[]{:S(2)}, u32[]{:S(2)}) collective-permute-start(f32[2,128,128]{2,1,0:T(8,128)S(1)} %fusion.9), channel_id=1, source_target_pairs={{0,4},{4,0},{8,12},{12,8},{16,20},{20,16},{24,28},{28,24},{1,5},{5... | collective-permute-start | bytes 393224 | tf_op jit(solution)/shard_map/ppermute | solution.py:328
  (29 other events, 105.9 us)

commit v4 on v3

--- a/solution.py
+++ b/solution.py
@@ -18,14 +18,14 @@
 GRANT = 24 * 2**20
 
 
-def call(body, outs, flops, moved, in_hbm=(), outs_in_hbm=False, scratch=(), aliases=None):
+def call(body, outs, flops, moved, in_hbm=(), outs_in_hbm=(), scratch=(), aliases=None):
     def run(place, *arrays):
         arrays = [pltpu.with_memory_space_constraint(x, pltpu.HBM) if i in in_hbm and not aliases else x for i, x in enumerate(arrays)]
         return pl.pallas_call(
             body,
             out_shape=[jax.ShapeDtypeStruct(*o) for o in outs],
             in_specs=[SMEM] + [HBM if i in in_hbm else VMEM for i in range(len(arrays))],
-            out_specs=[HBM if outs_in_hbm else VMEM] * len(outs),
+            out_specs=[HBM if i in outs_in_hbm else VMEM for i in range(len(outs))],
             scratch_shapes=list(scratch),
             input_output_aliases=aliases or {},
             compiler_params=pltpu.CompilerParams(vmem_limit_bytes=GRANT),
@@ -134,29 +134,31 @@
     )
 
 
-def weights_of(cum_t, cum_r, h):
+def weights_of(cum_t, cum_r_ref, side, half, j):
     tok = cum_t.shape[0]
     row = lax.broadcasted_iota(jnp.int32, (tok, tok), 0)
     col = lax.broadcasted_iota(jnp.int32, (tok, tok), 1)
-    gap = cum_t[:, h : h + 1] - cum_r[h : h + 1, :]
+    gap = column(cum_t, side, half, j) - cum_r_ref[pl.ds(side * half + j, 1), :]
     return jnp.where(row >= col, jnp.exp(jnp.minimum(gap, 0.0)), 0.0)
 
 
-def within(heads, dim, place_ref, q_ref, k_ref, v_ref, cum_t_ref, cum_r_ref, mixed_ref, inner_ref):
-    cum_t, cum_r = cum_t_ref[...], cum_r_ref[...]
-    for h in range(heads):
-        at = slice(h * dim, (h + 1) * dim)
+def within(half, dim, give, start, place_ref, q_ref, k_ref, v_ref, cum_t_ref, cum_r_ref, mixed_ref, inner_ref):
+    side = side_of(place_ref, give)
+    cum_t = cum_t_ref[...]
+    for i in range(mixed_ref.shape[0]):
+        at = lanes(side, half, start + i, dim)
         scores = dot(q_ref[:, at], k_ref[:, at], 1, 1)
-        mixed = (scores * weights_of(cum_t, cum_r, h)).astype(bf16)
-        mixed_ref[h] = mixed
-        inner_ref[:, at] = dot(mixed, v_ref[:, at], 1, 0)
-
-
-def across(half, dim, give, start, have, last, place_ref, *refs):
+        mixed = (scores * weights_of(cum_t, cum_r_ref, side, half, start + i)).astype(bf16)
+        mixed_ref[i] = mixed
+        inner_ref[:, i * dim : (i + 1) * dim] = dot(mixed, v_ref[:, at], 1, 0)
+
+
+def across(half, dim, give, start, inners, have, last, place_ref, *refs):
     side = side_of(place_ref, give)
-    q_ref, inner_ref, g_ref, gain_ref, cum_t_ref = refs[:5]
-    before = refs[5 : 5 + have]
-    states = refs[5 + have : -2]
+    q_ref, g_ref, gain_ref, cum_t_ref = refs[:4]
+    inner = [ref[:, i * dim : (i + 1) * dim] for ref in refs[4 : 4 + inners] for i in range(ref.shape[1] // dim)]
+    before = refs[4 + inners : 4 + inners + have]
+    states = refs[4 + inners + have : -2]
     attn_ref, sums_ref = refs[-2:]
     lead = jnp.exp(cum_t_ref[...])
     squares = cross = jnp.zeros((lead.shape[0], dim), f32)
@@ -167,7 +169,7 @@
             hi, lo = split(ref[i])
             q = q_ref[:, at]
             outer = (dot(q, hi, 1, 0) + dot(q, lo, 1, 0)) * column(lead, side, half, j)
-            attn = inner_ref[:, at] + outer
+            attn = inner[j] + outer
             attn_ref[:, (j - start) * dim : (j - start + 1) * dim] = attn
             scaled = g_ref[:, at].astype(f32) * gain_ref[:, at]
             squares += attn * attn
@@ -216,59 +218,67 @@
     state_into(outs, lambda j: q_ref[:, lanes(side, half, j, dim)], lambda j: kept[j], lead, side, half)
 
 
-def local_grads(half, dim, chunks, place_ref, *refs):
-    side = side_of(place_ref, False)
-    q_ref, k_ref, v_ref, cum_t_ref, cum_r_ref, mixed_ref, d_own_ref, d_give_ref = refs[:8]
-    states = refs[8 : 8 + 2 * chunks]
-    qg_ref, kg_ref, vg_ref = refs[8 + 2 * chunks :]
+def local_grads(half, dim, give, start, place_ref, *refs):
+    side = side_of(place_ref, give)
+    q_ref, k_ref, v_ref, cum_t_ref, cum_r_ref, mixed_ref, d_ref = refs[:7]
+    query_ref, kg_ref, vg_ref = refs[-3:]
     cum_t = cum_t_ref[...]
     lead = jnp.exp(cum_t)
-    tok = cum_t.shape[0]
-    row = lax.broadcasted_iota(jnp.int32, (tok, tok), 0)
-    col = lax.broadcasted_iota(jnp.int32, (tok, tok), 1)
-    for s, (d_ref, group) in enumerate(((d_own_ref, states[:chunks]), (d_give_ref, states[chunks:]))):
-        which = side if s == 0 else 1 - side
-        j = 0
-        for ref in group:
-            for i in range(ref.shape[0]):
-                at = lanes(which, half, j, dim)
-                h = which * half + j
-                d = d_ref[:, j * dim : (j + 1) * dim]
-                cum_col = column(cum_t, which, half, j)
-                gap = cum_col - cum_r_ref[pl.ds(h, 1), :]
-                weights = jnp.where(row >= col, jnp.exp(jnp.minimum(gap, 0.0)), 0.0)
-                graded = (dot(d, v_ref[:, at], 1, 1) * weights).astype(bf16)
-                hi, lo = split(ref[i])
-                outer = (dot(d, hi, 1, 1) + dot(d, lo, 1, 1)) * column(lead, which, half, j)
-                qg_ref[:, at] = (dot(graded, k_ref[:, at], 1, 0) + outer).astype(bf16)
-                kg_ref[:, at] = dot(graded, q_ref[:, at], 0, 0)
-                vg_ref[:, at] = dot(mixed_ref[h], d, 0, 0)
-                j += 1
-
-
-def final_grads(half, dim, parts, skip, place_ref, *refs):
-    k_ref, v_ref, cum_t_ref, kg_ref, vg_ref = refs[:5]
-    states = refs[5 : 5 + len(parts)]
-    key_ref, value_ref, key_buf, value_buf, sems = refs[5 + len(parts) + skip :]
+    count = 0
+    for ref in refs[7:-3]:
+        for n in range(ref.shape[0]):
+            j = start + count
+            at = lanes(side, half, j, dim)
+            to = slice(count * dim, (count + 1) * dim)
+            d = d_ref[:, j * dim : (j + 1) * dim]
+            graded = (dot(d, v_ref[:, at], 1, 1) * weights_of(cum_t, cum_r_ref, side, half, j)).astype(bf16)
+            hi, lo = split(ref[n])
+            outer = (dot(d, hi, 1, 1) + dot(d, lo, 1, 1)) * column(lead, side, half, j)
+            query_ref[:, to] = (dot(graded, k_ref[:, at], 1, 0) + outer).astype(bf16)
+            kg_ref[:, to] = dot(graded, q_ref[:, at], 0, 0)
+            vg_ref[:, to] = dot(mixed_ref[count], d, 0, 0)
+            count += 1
+
+
+def final_grads(half, dim, parts, pieces, queries, skip, place_ref, *refs):
+    k_ref, v_ref, cum_t_ref = refs[:3]
+    refs = refs[3:]
+    local = {}
+    for (give, first), kg_ref, vg_ref in zip(pieces, refs[::2], refs[1::2]):
+        for i in range(kg_ref.shape[1] // dim):
+            local[give, first + i] = (kg_ref, vg_ref, slice(i * dim, (i + 1) * dim))
+    refs = refs[2 * len(pieces) :]
+    states, query_pieces = refs[: len(parts)], refs[len(parts) : len(parts) + len(queries)]
+    outs = refs[len(parts) + len(queries) + skip :]
+    key_ref, value_ref = outs[:2]
+    key_buf, value_buf, sems = outs[-3:]
     cum_t = cum_t_ref[...]
     tail = jnp.exp(cum_t[cum_t.shape[0] - 1 :, :] - cum_t)
     copies = []
+
+    def put(source, out, give, j):
+        side = side_of(place_ref, give)
+        target = pl.ds(pl.multiple_of((side * half + j) * dim, dim), source.shape[1])
+        copies.append(pltpu.make_async_copy(source, out.at[:, target], sems.at[len(copies)]))
+        copies[-1].start()
+
+    for ref, (give, j) in zip(query_pieces, queries):
+        put(ref, outs[2], give, j)
     at = 0
-    for n, (ref, (give, j)) in enumerate(zip(states, parts)):
+    for ref, (give, j) in zip(states, parts):
         side = side_of(place_ref, give)
         size = ref.shape[0] * dim
-        target = pl.ds(pl.multiple_of((side * half + j) * dim, dim), size)
         for i in range(ref.shape[0]):
             here = lanes(side, half, j + i, dim)
             to = slice(at + i * dim, at + (i + 1) * dim)
             tail_col = column(tail, side, half, j + i)
             hi, lo = split(ref[i])
             v, k = v_ref[:, here], k_ref[:, here]
-            key_buf[:, to] = (kg_ref[:, here] + (dot(v, hi, 1, 1) + dot(v, lo, 1, 1)) * tail_col).astype(bf16)
-            value_buf[:, to] = (vg_ref[:, here] + (dot(k, hi, 1, 0) + dot(k, lo, 1, 0)) * tail_col).astype(bf16)
-        for m, (buf, out) in enumerate(((key_buf, key_ref), (value_buf, value_ref))):
-            copies.append(pltpu.make_async_copy(buf.at[:, at : at + size], out.at[:, target], sems.at[2 * n + m]))
-            copies[-1].start()
+            kg_ref, vg_ref, part = local[give, j + i]
+            key_buf[:, to] = (kg_ref[:, part] + (dot(v, hi, 1, 1) + dot(v, lo, 1, 1)) * tail_col).astype(bf16)
+            value_buf[:, to] = (vg_ref[:, part] + (dot(k, hi, 1, 0) + dot(k, lo, 1, 0)) * tail_col).astype(bf16)
+        put(key_buf.at[:, at : at + size], key_ref, give, j)
+        put(value_buf.at[:, at : at + size], value_ref, give, j)
         at += size
     for copy in copies:
         copy.wait()
@@ -366,11 +376,24 @@
     own_states = call(
         functools.partial(more_states, half, dim), state, 2 * half * pair_flops, 8 * row_bytes
     )(place, keys, values, cum_t)
-    mixed, inner = call(
-        functools.partial(within, heads, dim),
-        [((heads, tok, tok), bf16), ((tok, width), f32)],
-        2 * heads * pair_flops, 12 * row_bytes,
-    )(place, queries, keys, values, cum_t, cum_r)
+    places = [sum(sizes[:c]) for c in range(chunks)]
+    middle = (chunks + 1) // 2
+    pieces = [
+        (give_piece, run)
+        for give_piece in (False, True)
+        for run in (list(range(middle)), list(range(middle, chunks)))
+        if run
+    ]
+    mixed, inner = [], {False: [], True: []}
+    for is_give, run in pieces:
+        count = sum(sizes[c] for c in run)
+        mix, inn = call(
+            functools.partial(within, half, dim, is_give, places[run[0]]),
+            [((count, tok, tok), bf16), ((tok, count * dim), f32)],
+            2 * count * pair_flops, 12 * tok * count * dim,
+        )(place, queries, keys, values, cum_t, cum_r)
+        mixed.append(mix)
+        inner[is_give].append(inn)
 
     upper = flags[0] > 0.5
     total_mine = jnp.where(upper, total[half:], total[:half])
@@ -380,10 +403,10 @@
     def outer(is_give, states, start, before, last):
         count = sum(x.shape[0] for x in states)
         return call(
-            functools.partial(across, half, dim, is_give, start, len(before), last),
+            functools.partial(across, half, dim, is_give, start, len(inner[is_give]), len(before), last),
             [((tok, count * dim), f32), ((8, tok), f32) if last else ((2, tok, dim), f32)],
             2 * count * pair_flops, 14 * tok * count * dim,
-        )(place, queries, inner, output_gradient, gain_row, cum_t, *before, *states)
+        )(place, queries, output_gradient, gain_row, cum_t, *inner[is_give], *before, *states)
 
     attn_own, part = outer(False, in_own, 0, [], False)
     early = sum(sizes[:-1])
@@ -411,11 +434,17 @@
 
     d_give, gain_give, *back_give = grads(True, attn_give)
     d_own, gain_own, *back_own = grads(False, [attn_own])
-    query_grad, key_part, value_part = call(
-        functools.partial(local_grads, half, dim, chunks),
-        [((tok, width), bf16), ((tok, width), f32), ((tok, width), f32)],
-        6 * heads * pair_flops, 40 * row_bytes,
-    )(place, queries, keys, values, cum_t, cum_r, mixed, d_own, d_give, *in_own, *in_give)
+    query_pieces, local = [], []
+    for n, (is_give, run) in enumerate(pieces):
+        count = sum(sizes[c] for c in run)
+        states = [(in_give if is_give else in_own)[c] for c in run]
+        query, key_part, value_part = call(
+            functools.partial(local_grads, half, dim, is_give, places[run[0]]),
+            [((tok, count * dim), bf16), ((tok, count * dim), f32), ((tok, count * dim), f32)],
+            6 * count * pair_flops, 40 * tok * count * dim,
+        )(place, queries, keys, values, cum_t, cum_r, mixed[n], d_give if is_give else d_own, *states)
+        query_pieces.append(((is_give, places[run[0]]), query))
+        local.append(((is_give, places[run[0]]), key_part, value_part))
 
     late_own, late_give = carried(back_own, back_give, total_mine, total_theirs, flags, n_seq, n_dp, True)
 
@@ -427,28 +456,42 @@
         gain_grad = gain_grad + lax.ppermute(gain_grad, "seq", [(i, i ^ step) for i in range(n_seq)])
         step *= 2
 
-    places = [sum(sizes[:c]) for c in range(chunks)]
-
-    def finish(parts, states, before):
+    def finish(parts, states, query_parts, before):
         count = sum(x.shape[0] for x in states)
+        used = [
+            (mark, key_part, value_part)
+            for mark, key_part, value_part in local
+            if any(mark[0] == g and mark[1] <= p < mark[1] + key_part.shape[1] // dim for g, p in parts)
+        ]
+        base = 3 + 2 * len(used) + len(parts) + len(query_parts)
+        outs = 3 if query_parts else 2
         return call(
-            functools.partial(final_grads, half, dim, parts, len(before)),
-            [((tok, width), bf16), ((tok, width), bf16)],
+            functools.partial(
+                final_grads, half, dim, parts, [u[0] for u in used], [q for q, _ in query_parts], len(before)
+            ),
+            [((tok, width), bf16)] * outs,
             4 * count * pair_flops, 20 * tok * count * dim,
-            in_hbm=range(5 + len(parts), 7 + len(parts)),
-            outs_in_hbm=True,
+            in_hbm=(base, base + 1),
+            outs_in_hbm=range(outs),
             scratch=[
                 pltpu.VMEM((tok, count * dim), bf16),
                 pltpu.VMEM((tok, count * dim), bf16),
-                pltpu.SemaphoreType.DMA((2 * len(parts),)),
+                pltpu.SemaphoreType.DMA((2 * len(parts) + len(query_parts),)),
             ],
-            aliases={6 + len(parts): 0, 7 + len(parts): 1} if before else None,
-        )(place, keys, values, cum_t, key_part, value_part, *states, *before)
+            aliases={base + 1: 0, base + 2: 1} if before else None,
+        )(
+            place, keys, values, cum_t, *[x for _, a, b in used for x in (a, b)], *states,
+            *[q for _, q in query_parts], *before,
+        )
 
     own_parts = [(False, p) for p in places]
     give_parts = [(True, p) for p in places]
-    begun = finish(own_parts + give_parts[:-1], late_own + late_give[:-1], [])
-    key_grad, value_grad = finish(give_parts[-1:], late_give[-1:], list(begun))
+    begun = finish(own_parts, late_own, [], [])
+    if chunks > 1:
+        *begun, query_grad = finish(give_parts[:-1], late_give[:-1], query_pieces, begun)
+        key_grad, value_grad = finish(give_parts[-1:], late_give[-1:], [], begun)
+    else:
+        key_grad, value_grad, query_grad = finish(give_parts, late_give, query_pieces, begun)
     return query_grad, key_grad, value_grad, gain_grad.reshape(width)
 
 

time: 106 us -> 103 us (0.972)
  the two profiles are of different devices: /device:TPU:0 before, /device:TPU:16 now
where the time goes in v4:
time: 103 us; the launch traced here: 102 us
  waiting for transfers between devices  41 us (40%)
  starting transfers between devices  40.4 us (39%)
  Pallas kernels  15.9 us (15%)
  local copies, waits for them, and re-layouts  2.26 us (2%)
  other arithmetic  1.72 us (2%)
  between operations  1.11 us (1%)
    ppermute x24, starting transfers between devices, carried(): got = [lax.ppermute(x, ('seq', 'dp'), hop(a)) for x in outward]  19.1 us
    ppermute x24, waiting for transfers between devices, carried(): got = [lax.ppermute(x, ('seq', 'dp'), hop(a)) for x in outward]  18.1 us
    pallas_call x18, Pallas kernels, run(): pl.pallas_call(body, out_shape=[jax.ShapeDtypeStruct(*o) for o in outs],...  15.9 us
    ppermute x8, waiting for transfers between devices, carried(): return (kept, [lax.ppermute(x, 'seq', swap) for x in sent])  11.3 us
    ppermute x8, starting transfers between devices, carried(): received = [lax.ppermute(x, 'seq', swap) for x in theirs]  8.1 us
    ppermute x8, starting transfers between devices, carried(): return (kept, [lax.ppermute(x, 'seq', swap) for x in sent])  8.07 us
    ppermute x3, waiting for transfers between devices, on_device(): lax.ppermute(gain_grad, 'seq', [(i, i ^ step) for i in range(n_seq)])  5.64 us
    ppermute x8, waiting for transfers between devices, carried(): received = [lax.ppermute(x, 'seq', swap) for x in theirs]  4.12 us
  transfers between devices with their start and end apart: 47, of which 24 were waited for; matrix products, arithmetic and copies ran while one was open for 2% of the time, Pallas kernels for 10%

profile of v4, /device:TPU:16, one launch (start us, length us, event | category | flops | bytes accessed | tf_op | source)
XLA Modules:
  0.0 102.3 jit_solution(8925261250572336027)
XLA Ops:
  0.7 2.6 %shard_map.93 = (f32[128,16]{1,0:T(8,128)S(1)}, f32[16,128]{1,0:T(8,128)S(1)}, f32[16,128]{1,0:T(8,128)S(1)}, f32[16,128]{1,0:T(8,128)S(1)}, f32[2,128,128]{2,1,...) custom-call(s32[1]{0:T(128)} %bitcast.place_ref, ...), custom_call_target="tpu_custom_call" | custom-call | flops 67108864 | bytes 1048576 | tf_op jit(solution)/shard_map/pallas_call | solution.py:24
  3.3 1.6 %collective-permute-start = (f32[16,128]{1,0:T(8,128)S(1)}, f32[16,128]{1,0:T(8,128)S(1)}, u32[]{:S(2)}, u32[]{:S(2)}) collective-permute-start(f32[16,128]{1,0:T(8,128)S(1)} %get-tuple-element.81), channel_id=1, source_target_pairs={{0,4},{4,0},{8,12},{12,8},{16,20},{20,16},{24,28},{28,24},{1,5},{5... | collective-permute-start | bytes 24584 | tf_op jit(solution)/shard_map/ppermute | solution.py:375
  5.4 1.5 %collective-permute-start.5 = (f32[2,128,128]{2,1,0:T(8,128)S(1)}, f32[2,128,128]{2,1,0:T(8,128)S(1)}, u32[]{:S(2)}, u32[]{:S(2)}) collective-permute-start(f32[2,128,128]{2,1,0:T(8,128)S(1)} %get-tuple-element.85), channel_id=1, source_target_pairs={{0,4},{4,0},{8,12},{12,8},{16,20},{20,16},{24,28},{28,24},{1,5},{5... | collective-permute-start | bytes 393224 | tf_op jit(solution)/shard_map/ppermute | solution.py:308
  7.4 1.5 %collective-permute-start.13 = (f32[2,128,128]{2,1,0:T(8,128)S(1)}, f32[2,128,128]{2,1,0:T(8,128)S(1)}, u32[]{:S(2)}, u32[]{:S(2)}) collective-permute-start(f32[2,128,128]{2,1,0:T(8,128)S(1)} %get-tuple-element.91), channel_id=1, source_target_pairs={{0,4},{4,0},{8,12},{12,8},{16,20},{20,16},{24,28},{28,24},{1,5},{5... | collective-permute-start | bytes 393224 | tf_op jit(solution)/shard_map/ppermute | solution.py:308
  14.2 4.1 %collective-permute-done.13 = f32[2,128,128]{2,1,0:T(8,128)S(1)} collective-permute-done((f32[2,128,128]{2,1,0:T(8,128)S(1)}, f32[2,128,128]{2,1,0:T(8,128)S(1)}, u32[]{:S(2)}, u32[]{:S(2)}) %collective-permute-start.13) | collective-permute-done | bytes 131104 | tf_op jit(solution)/shard_map/ppermute | solution.py:308
  19.1 2.5 %collective-permute-start.3 = (f32[2,128,128]{2,1,0:T(8,128)S(1)}, f32[2,128,128]{2,1,0:T(8,128)S(1)}, u32[]{:S(2)}, u32[]{:S(2)}) collective-permute-start(f32[2,128,128]{2,1,0:T(8,128)S(1)} %multiply_add_fusion.22), channel_id=1, source_target_pairs={{0,1},{1,0},{2,3},{3,2},{4,5},{5,4},{6,7},{7,6},{8,16},{9,17},{10,... | collective-permute-start | bytes 393224 | tf_op jit(solution)/shard_map/ppermute | solution.py:324
  21.6 3.7 %collective-permute-start.15 = (f32[2,128,128]{2,1,0:T(8,128)S(1)}, f32[2,128,128]{2,1,0:T(8,128)S(1)}, u32[]{:S(2)}, u32[]{:S(2)}) collective-permute-start(f32[2,128,128]{2,1,0:T(8,128)S(1)} %multiply_add_fusion.13), channel_id=1, source_target_pairs={{0,1},{1,0},{2,3},{3,2},{4,5},{5,4},{6,7},{7,6},{8,16},{9,17},{10,... | collective-permute-start | bytes 393224 | tf_op jit(solution)/shard_map/ppermute | solution.py:324
  25.3 1.9 %collective-permute-start.11 = (f32[2,128,128]{2,1,0:T(8,128)S(1)}, f32[2,128,128]{2,1,0:T(8,128)S(1)}, u32[]{:S(2)}, u32[]{:S(2)}) collective-permute-start(f32[2,128,128]{2,1,0:T(8,128)S(1)} %multiply_add_fusion.16), channel_id=1, source_target_pairs={{0,1},{1,0},{2,3},{3,2},{4,5},{5,4},{6,7},{7,6},{8,16},{9,17},{10,... | collective-permute-start | bytes 393224 | tf_op jit(solution)/shard_map/ppermute | solution.py:324
  35.5 4.6 %collective-permute-done.8 = f32[2,128,128]{2,1,0:T(8,128)S(1)} collective-permute-done((f32[2,128,128]{2,1,0:T(8,128)S(1)}, f32[2,128,128]{2,1,0:T(8,128)S(1)}, u32[]{:S(2)}, u32[]{:S(2)}) %collective-permute-start.8) | collective-permute-done | bytes 131104 | tf_op jit(solution)/shard_map/ppermute | solution.py:324
  44.5 2.7 %collective-permute-done.19.refs_9_.refs_7_ = f32[2,128,128]{2,1,0:T(8,128)S(1)} collective-permute-done((f32[2,128,128]{2,1,0:T(8,128)S(1)}, f32[2,128,128]{2,1,0:T(8,128)S(1)}, u32[]{:S(2)}, u32[]{:S(2)}) %collective-permute-start.19) | collective-permute-done | bytes 131104 | tf_op jit(solution)/shard_map/ppermute | solution.py:338
  47.3 1.4 %collective-permute-done.18.refs_8_ = f32[2,128,128]{2,1,0:T(8,128)S(1)} collective-permute-done((f32[2,128,128]{2,1,0:T(8,128)S(1)}, f32[2,128,128]{2,1,0:T(8,128)S(1)}, u32[]{:S(2)}, u32[]{:S(2)}) %collective-permute-start.18) | collective-permute-done | bytes 131104 | tf_op jit(solution)/shard_map/ppermute | solution.py:338
  49.4 1.6 %collective-permute-start.22 = (f32[8,128]{1,0:T(8,128)S(1)}, f32[8,128]{1,0:T(8,128)S(1)}, u32[]{:S(2)}, u32[]{:S(2)}) collective-permute-start(f32[8,128]{1,0:T(8,128)S(1)} %get-tuple-element.98.refs_4_), channel_id=1, source_target_pairs={{0,2},{1,3},{2,0},{3,1},{4,6},{5,7},{6,4},{7,5},{8,10},{9,11},{10,... | collective-permute-start | bytes 12296 | tf_op jit(solution)/shard_map/ppermute | solution.py:423
  55.4 1.4 %collective-permute-start.24 = (f32[2,128,128]{2,1,0:T(8,128)S(1)}, f32[2,128,128]{2,1,0:T(8,128)S(1)}, u32[]{:S(2)}, u32[]{:S(2)}) collective-permute-start(f32[2,128,128]{2,1,0:T(8,128)S(1)} %get-tuple-element.110), channel_id=1, source_target_pairs={{0,4},{4,0},{8,12},{12,8},{16,20},{20,16},{24,28},{28,24},{1,5},{5... | collective-permute-start | bytes 393224 | tf_op jit(solution)/shard_map/ppermute | solution.py:308
  57.5 1.4 %collective-permute-start.34 = (f32[2,128,128]{2,1,0:T(8,128)S(1)}, f32[2,128,128]{2,1,0:T(8,128)S(1)}, u32[]{:S(2)}, u32[]{:S(2)}) collective-permute-start(f32[2,128,128]{2,1,0:T(8,128)S(1)} %get-tuple-element.117), channel_id=1, source_target_pairs={{0,4},{4,0},{8,12},{12,8},{16,20},{20,16},{24,28},{28,24},{1,5},{5... | collective-permute-start | bytes 393224 | tf_op jit(solution)/shard_map/ppermute | solution.py:308
  62.6 2.3 %collective-permute-done.45 = f32[16,128]{1,0:T(8,128)S(1)} collective-permute-done((f32[16,128]{1,0:T(8,128)S(1)}, f32[16,128]{1,0:T(8,128)S(1)}, u32[]{:S(2)}, u32[]{:S(2)}) %collective-permute-start.45) | collective-permute-done | bytes 8224 | tf_op jit(solution)/shard_map/ppermute | solution.py:456
  66.2 3.3 %collective-permute-done.46 = f32[16,128]{1,0:T(8,128)S(1)} collective-permute-done((f32[16,128]{1,0:T(8,128)S(1)}, f32[16,128]{1,0:T(8,128)S(1)}, u32[]{:S(2)}, u32[]{:S(2)}) %collective-permute-start.46) | collective-permute-done | bytes 8224 | tf_op jit(solution)/shard_map/ppermute | solution.py:456
  70.7 1.6 %collective-permute-start.30 = (f32[2,128,128]{2,1,0:T(8,128)S(1)}, f32[2,128,128]{2,1,0:T(8,128)S(1)}, u32[]{:S(2)}, u32[]{:S(2)}) collective-permute-start(f32[2,128,128]{2,1,0:T(8,128)S(1)} %multiply_add_fusion.8), channel_id=1, source_target_pairs={{0,1},{1,0},{2,3},{3,2},{4,5},{5,4},{6,7},{7,6},{8,9},{9,8},{10,11... | collective-permute-start | bytes 393224 | tf_op jit(solution)/shard_map/ppermute | solution.py:324
  72.9 1.6 %collective-permute-start.40 = (f32[2,128,128]{2,1,0:T(8,128)S(1)}, f32[2,128,128]{2,1,0:T(8,128)S(1)}, u32[]{:S(2)}, u32[]{:S(2)}) collective-permute-start(f32[2,128,128]{2,1,0:T(8,128)S(1)} %multiply_add_fusion.2), channel_id=1, source_target_pairs={{0,1},{1,0},{2,3},{3,2},{4,5},{5,4},{6,7},{7,6},{8,9},{9,8},{10,11... | collective-permute-start | bytes 393224 | tf_op jit(solution)/shard_map/ppermute | solution.py:324
  74.5 2.0 %collective-permute-done.25 = f32[2,128,128]{2,1,0:T(8,128)S(1)} collective-permute-done((f32[2,128,128]{2,1,0:T(8,128)S(1)}, f32[2,128,128]{2,1,0:T(8,128)S(1)}, u32[]{:S(2)}, u32[]{:S(2)}) %collective-permute-start.25) | collective-permute-done | bytes 131104 | tf_op jit(solution)/shard_map/ppermute | solution.py:324
  76.7 1.5 %collective-permute-done.30 = f32[2,128,128]{2,1,0:T(8,128)S(1)} collective-permute-done((f32[2,128,128]{2,1,0:T(8,128)S(1)}, f32[2,128,128]{2,1,0:T(8,128)S(1)}, u32[]{:S(2)}, u32[]{:S(2)}) %collective-permute-start.30) | collective-permute-done | bytes 131104 | tf_op jit(solution)/shard_map/ppermute | solution.py:324
  87.0 1.5 %collective-permute-start.28 = (f32[2,128,128]{2,1,0:T(8,128)S(1)}, f32[2,128,128]{2,1,0:T(8,128)S(1)}, u32[]{:S(2)}, u32[]{:S(2)}) collective-permute-start(f32[2,128,128]{2,1,0:T(8,128)S(1)} %fusion.9), channel_id=1, source_target_pairs={{0,4},{4,0},{8,12},{12,8},{16,20},{20,16},{24,28},{28,24},{1,5},{5... | collective-permute-start | bytes 393224 | tf_op jit(solution)/shard_map/ppermute | solution.py:338
  89.3 1.5 %collective-permute-start.38 = (f32[2,128,128]{2,1,0:T(8,128)S(1)}, f32[2,128,128]{2,1,0:T(8,128)S(1)}, u32[]{:S(2)}, u32[]{:S(2)}) collective-permute-start(f32[2,128,128]{2,1,0:T(8,128)S(1)} %fusion.13), channel_id=1, source_target_pairs={{0,4},{4,0},{8,12},{12,8},{16,20},{20,16},{24,28},{28,24},{1,5},{5... | collective-permute-start | bytes 393224 | tf_op jit(solution)/shard_map/ppermute | solution.py:338
  93.5 2.8 %collective-permute-done.33.refs_8_ = f32[2,128,128]{2,1,0:T(8,128)S(1)} collective-permute-done((f32[2,128,128]{2,1,0:T(8,128)S(1)}, f32[2,128,128]{2,1,0:T(8,128)S(1)}, u32[]{:S(2)}, u32[]{:S(2)}) %collective-permute-start.33) | collective-permute-done | bytes 131104 | tf_op jit(solution)/shard_map/ppermute | solution.py:338
  96.3 2.8 %collective-permute-done.38.refs_9_ = f32[2,128,128]{2,1,0:T(8,128)S(1)} collective-permute-done((f32[2,128,128]{2,1,0:T(8,128)S(1)}, f32[2,128,128]{2,1,0:T(8,128)S(1)}, u32[]{:S(2)}, u32[]{:S(2)}) %collective-permute-start.38) | collective-permute-done | bytes 131104 | tf_op jit(solution)/shard_map/ppermute | solution.py:338
  (147 shorter events, 47.6 us)
Async XLA Ops:
  3.3 10.7 %collective-permute-start = (f32[16,128]{1,0:T(8,128)S(1)}, f32[16,128]{1,0:T(8,128)S(1)}, u32[]{:S(2)}, u32[]{:S(2)}) collective-permute-start(f32[16,128]{1,0:T(8,128)S(1)} %get-tuple-element.81), channel_id=1, source_target_pairs={{0,4},{4,0},{8,12},{12,8},{16,20},{20,16},{24,28},{28,24},{1,5},{5... | collective-permute-start | bytes 24584 | tf_op jit(solution)/shard_map/ppermute | solution.py:375
  4.9 9.2 %collective-permute-start.1 = (f32[2,128,128]{2,1,0:T(8,128)S(1)}, f32[2,128,128]{2,1,0:T(8,128)S(1)}, u32[]{:S(2)}, u32[]{:S(2)}) collective-permute-start(f32[2,128,128]{2,1,0:T(8,128)S(1)} %get-tuple-element.83), channel_id=1, source_target_pairs={{0,4},{4,0},{8,12},{12,8},{16,20},{20,16},{24,28},{28,24},{1,5},{5... | collective-permute-start | bytes 393224 | tf_op jit(solution)/shard_map/ppermute | solution.py:308
  5.4 13.6 %collective-permute-start.5 = (f32[2,128,128]{2,1,0:T(8,128)S(1)}, f32[2,128,128]{2,1,0:T(8,128)S(1)}, u32[]{:S(2)}, u32[]{:S(2)}) collective-permute-start(f32[2,128,128]{2,1,0:T(8,128)S(1)} %get-tuple-element.85), channel_id=1, source_target_pairs={{0,4},{4,0},{8,12},{12,8},{16,20},{20,16},{24,28},{28,24},{1,5},{5... | collective-permute-start | bytes 393224 | tf_op jit(solution)/shard_map/ppermute | solution.py:308
  6.9 11.5 %collective-permute-start.9 = (f32[2,128,128]{2,1,0:T(8,128)S(1)}, f32[2,128,128]{2,1,0:T(8,128)S(1)}, u32[]{:S(2)}, u32[]{:S(2)}) collective-permute-start(f32[2,128,128]{2,1,0:T(8,128)S(1)} %get-tuple-element.88), channel_id=1, source_target_pairs={{0,4},{4,0},{8,12},{12,8},{16,20},{20,16},{24,28},{28,24},{1,5},{5... | collective-permute-start | bytes 393224 | tf_op jit(solution)/shard_map/ppermute | solution.py:308
  7.4 10.9 %collective-permute-start.13 = (f32[2,128,128]{2,1,0:T(8,128)S(1)}, f32[2,128,128]{2,1,0:T(8,128)S(1)}, u32[]{:S(2)}, u32[]{:S(2)}) collective-permute-start(f32[2,128,128]{2,1,0:T(8,128)S(1)} %get-tuple-element.91), channel_id=1, source_target_pairs={{0,4},{4,0},{8,12},{12,8},{16,20},{20,16},{24,28},{28,24},{1,5},{5... | collective-permute-start | bytes 393224 | tf_op jit(solution)/shard_map/ppermute | solution.py:308
  18.4 6.9 %collective-permute-start.10 = (f32[2,128,128]{2,1,0:T(8,128)S(1)}, f32[2,128,128]{2,1,0:T(8,128)S(1)}, u32[]{:S(2)}, u32[]{:S(2)}) collective-permute-start(f32[2,128,128]{2,1,0:T(8,128)S(1)} %multiply_add_fusion.17), channel_id=1, source_target_pairs={{0,8},{1,9},{2,10},{3,11},{4,12},{5,13},{6,14},{7,15},{8,0},{9,1},... | collective-permute-start | bytes 393224 | tf_op jit(solution)/shard_map/ppermute | solution.py:324
  19.0 8.2 %collective-permute-start.6 = (f32[2,128,128]{2,1,0:T(8,128)S(1)}, f32[2,128,128]{2,1,0:T(8,128)S(1)}, u32[]{:S(2)}, u32[]{:S(2)}) collective-permute-start(f32[2,128,128]{2,1,0:T(8,128)S(1)} %multiply_add_fusion.20), channel_id=1, source_target_pairs={{0,8},{1,9},{2,10},{3,11},{4,12},{5,13},{6,14},{7,15},{8,0},{9,1},... | collective-permute-start | bytes 393224 | tf_op jit(solution)/shard_map/ppermute | solution.py:324
  19.1 9.5 %collective-permute-start.3 = (f32[2,128,128]{2,1,0:T(8,128)S(1)}, f32[2,128,128]{2,1,0:T(8,128)S(1)}, u32[]{:S(2)}, u32[]{:S(2)}) collective-permute-start(f32[2,128,128]{2,1,0:T(8,128)S(1)} %multiply_add_fusion.22), channel_id=1, source_target_pairs={{0,1},{1,0},{2,3},{3,2},{4,5},{5,4},{6,7},{7,6},{8,16},{9,17},{10,... | collective-permute-start | bytes 393224 | tf_op jit(solution)/shard_map/ppermute | solution.py:324
  21.6 8.0 %collective-permute-start.15 = (f32[2,128,128]{2,1,0:T(8,128)S(1)}, f32[2,128,128]{2,1,0:T(8,128)S(1)}, u32[]{:S(2)}, u32[]{:S(2)}) collective-permute-start(f32[2,128,128]{2,1,0:T(8,128)S(1)} %multiply_add_fusion.13), channel_id=1, source_target_pairs={{0,1},{1,0},{2,3},{3,2},{4,5},{5,4},{6,7},{7,6},{8,16},{9,17},{10,... | collective-permute-start | bytes 393224 | tf_op jit(solution)/shard_map/ppermute | solution.py:324
  25.3 6.8 %collective-permute-start.11 = (f32[2,128,128]{2,1,0:T(8,128)S(1)}, f32[2,128,128]{2,1,0:T(8,128)S(1)}, u32[]{:S(2)}, u32[]{:S(2)}) collective-permute-start(f32[2,128,128]{2,1,0:T(8,128)S(1)} %multiply_add_fusion.16), channel_id=1, source_target_pairs={{0,1},{1,0},{2,3},{3,2},{4,5},{5,4},{6,7},{7,6},{8,16},{9,17},{10,... | collective-permute-start | bytes 393224 | tf_op jit(solution)/shard_map/ppermute | solution.py:324
  29.6 10.6 %collective-permute-start.16 = (f32[2,128,128]{2,1,0:T(8,128)S(1)}, f32[2,128,128]{2,1,0:T(8,128)S(1)}, u32[]{:S(2)}, u32[]{:S(2)}) collective-permute-start(f32[2,128,128]{2,1,0:T(8,128)S(1)} %multiply_add_fusion.12), channel_id=1, source_target_pairs={{0,1},{1,0},{2,3},{3,2},{4,5},{5,4},{6,7},{7,6},{8,9},{9,8},{10,11... | collective-permute-start | bytes 393224 | tf_op jit(solution)/shard_map/ppermute | solution.py:324
  32.1 8.1 %collective-permute-start.12 = (f32[2,128,128]{2,1,0:T(8,128)S(1)}, f32[2,128,128]{2,1,0:T(8,128)S(1)}, u32[]{:S(2)}, u32[]{:S(2)}) collective-permute-start(f32[2,128,128]{2,1,0:T(8,128)S(1)} %multiply_add_fusion.15), channel_id=1, source_target_pairs={{0,1},{1,0},{2,3},{3,2},{4,5},{5,4},{6,7},{7,6},{8,9},{9,8},{10,11... | collective-permute-start | bytes 393224 | tf_op jit(solution)/shard_map/ppermute | solution.py:324
  34.6 10.0 %collective-permute-start.17 = (f32[2,128,128]{2,1,0:T(8,128)S(1)}, f32[2,128,128]{2,1,0:T(8,128)S(1)}, u32[]{:S(2)}, u32[]{:S(2)}) collective-permute-start(f32[2,128,128]{2,1,0:T(8,128)S(1)} %get-tuple-element.94), channel_id=1, source_target_pairs={{0,4},{4,0},{8,12},{12,8},{16,20},{20,16},{24,28},{28,24},{1,5},{5... | collective-permute-start | bytes 393224 | tf_op jit(solution)/shard_map/ppermute | solution.py:338
  40.3 8.7 %collective-permute-start.20 = (f32[2,128,128]{2,1,0:T(8,128)S(1)}, f32[2,128,128]{2,1,0:T(8,128)S(1)}, u32[]{:S(2)}, u32[]{:S(2)}) collective-permute-start(f32[2,128,128]{2,1,0:T(8,128)S(1)} %get-tuple-element.150), channel_id=1, source_target_pairs={{0,4},{4,0},{8,12},{12,8},{16,20},{20,16},{24,28},{28,24},{1,5},{5... | collective-permute-start | bytes 393224 | tf_op jit(solution)/shard_map/ppermute | solution.py:338
  55.4 14.7 %collective-permute-start.24 = (f32[2,128,128]{2,1,0:T(8,128)S(1)}, f32[2,128,128]{2,1,0:T(8,128)S(1)}, u32[]{:S(2)}, u32[]{:S(2)}) collective-permute-start(f32[2,128,128]{2,1,0:T(8,128)S(1)} %get-tuple-element.110), channel_id=1, source_target_pairs={{0,4},{4,0},{8,12},{12,8},{16,20},{20,16},{24,28},{28,24},{1,5},{5... | collective-permute-start | bytes 393224 | tf_op jit(solution)/shard_map/ppermute | solution.py:308
  56.9 13.8 %collective-permute-start.29 = (f32[2,128,128]{2,1,0:T(8,128)S(1)}, f32[2,128,128]{2,1,0:T(8,128)S(1)}, u32[]{:S(2)}, u32[]{:S(2)}) collective-permute-start(f32[2,128,128]{2,1,0:T(8,128)S(1)} %get-tuple-element.113), channel_id=1, source_target_pairs={{0,4},{4,0},{8,12},{12,8},{16,20},{20,16},{24,28},{28,24},{1,5},{5... | collective-permute-start | bytes 393224 | tf_op jit(solution)/shard_map/ppermute | solution.py:308
  57.5 14.8 %collective-permute-start.34 = (f32[2,128,128]{2,1,0:T(8,128)S(1)}, f32[2,128,128]{2,1,0:T(8,128)S(1)}, u32[]{:S(2)}, u32[]{:S(2)}) collective-permute-start(f32[2,128,128]{2,1,0:T(8,128)S(1)} %get-tuple-element.117), channel_id=1, source_target_pairs={{0,4},{4,0},{8,12},{12,8},{16,20},{20,16},{24,28},{28,24},{1,5},{5... | collective-permute-start | bytes 393224 | tf_op jit(solution)/shard_map/ppermute | solution.py:308
  58.9 14.0 %collective-permute-start.39 = (f32[2,128,128]{2,1,0:T(8,128)S(1)}, f32[2,128,128]{2,1,0:T(8,128)S(1)}, u32[]{:S(2)}, u32[]{:S(2)}) collective-permute-start(f32[2,128,128]{2,1,0:T(8,128)S(1)} %get-tuple-element.131), channel_id=1, source_target_pairs={{0,4},{4,0},{8,12},{12,8},{16,20},{20,16},{24,28},{28,24},{1,5},{5... | collective-permute-start | bytes 393224 | tf_op jit(solution)/shard_map/ppermute | solution.py:308
  70.7 7.5 %collective-permute-start.30 = (f32[2,128,128]{2,1,0:T(8,128)S(1)}, f32[2,128,128]{2,1,0:T(8,128)S(1)}, u32[]{:S(2)}, u32[]{:S(2)}) collective-permute-start(f32[2,128,128]{2,1,0:T(8,128)S(1)} %multiply_add_fusion.8), channel_id=1, source_target_pairs={{0,1},{1,0},{2,3},{3,2},{4,5},{5,4},{6,7},{7,6},{8,9},{9,8},{10,11... | collective-permute-start | bytes 393224 | tf_op jit(solution)/shard_map/ppermute | solution.py:324
  72.3 7.3 %collective-permute-start.35 = (f32[2,128,128]{2,1,0:T(8,128)S(1)}, f32[2,128,128]{2,1,0:T(8,128)S(1)}, u32[]{:S(2)}, u32[]{:S(2)}) collective-permute-start(f32[2,128,128]{2,1,0:T(8,128)S(1)} %multiply_add_fusion.5), channel_id=1, source_target_pairs={{0,1},{1,0},{2,3},{3,2},{4,5},{5,4},{6,7},{7,6},{8,9},{9,8},{10,11... | collective-permute-start | bytes 393224 | tf_op jit(solution)/shard_map/ppermute | solution.py:324
  72.9 8.1 %collective-permute-start.40 = (f32[2,128,128]{2,1,0:T(8,128)S(1)}, f32[2,128,128]{2,1,0:T(8,128)S(1)}, u32[]{:S(2)}, u32[]{:S(2)}) collective-permute-start(f32[2,128,128]{2,1,0:T(8,128)S(1)} %multiply_add_fusion.2), channel_id=1, source_target_pairs={{0,1},{1,0},{2,3},{3,2},{4,5},{5,4},{6,7},{7,6},{8,9},{9,8},{10,11... | collective-permute-start | bytes 393224 | tf_op jit(solution)/shard_map/ppermute | solution.py:324
  88.6 7.7 %collective-permute-start.33 = (f32[2,128,128]{2,1,0:T(8,128)S(1)}, f32[2,128,128]{2,1,0:T(8,128)S(1)}, u32[]{:S(2)}, u32[]{:S(2)}) collective-permute-start(f32[2,128,128]{2,1,0:T(8,128)S(1)} %fusion.11), channel_id=1, source_target_pairs={{0,4},{4,0},{8,12},{12,8},{16,20},{20,16},{24,28},{28,24},{1,5},{5... | collective-permute-start | bytes 393224 | tf_op jit(solution)/shard_map/ppermute | solution.py:338
  89.3 9.7 %collective-permute-start.38 = (f32[2,128,128]{2,1,0:T(8,128)S(1)}, f32[2,128,128]{2,1,0:T(8,128)S(1)}, u32[]{:S(2)}, u32[]{:S(2)}) collective-permute-start(f32[2,128,128]{2,1,0:T(8,128)S(1)} %fusion.13), channel_id=1, source_target_pairs={{0,4},{4,0},{8,12},{12,8},{16,20},{20,16},{24,28},{28,24},{1,5},{5... | collective-permute-start | bytes 393224 | tf_op jit(solution)/shard_map/ppermute | solution.py:338
  90.9 10.5 %collective-permute-start.43 = (f32[2,128,128]{2,1,0:T(8,128)S(1)}, f32[2,128,128]{2,1,0:T(8,128)S(1)}, u32[]{:S(2)}, u32[]{:S(2)}) collective-permute-start(f32[2,128,128]{2,1,0:T(8,128)S(1)} %get-tuple-element.142), channel_id=1, source_target_pairs={{0,4},{4,0},{8,12},{12,8},{16,20},{20,16},{24,28},{28,24},{1,5},{5... | collective-permute-start | bytes 393224 | tf_op jit(solution)/shard_map/ppermute | solution.py:338
  (29 other events, 136.6 us)

commit v5 on v4

--- a/solution.py
+++ b/solution.py
@@ -313,10 +313,9 @@
         n = x.shape[0]
         cuts.append((total_mine[at : at + n, None, :], total_theirs[at : at + n, None, :]))
         at += n
-    sums = [
-        jnp.where(first > 0.5, their_decay, 1.0) * x + jnp.where(first > 0.5, 1.0, my_decay) * r
-        for x, r, (my_decay, their_decay) in zip(mine, received, cuts)
-    ]
+    sums = []
+    for x, r, (my_decay, their_decay) in zip(mine, received, cuts):
+        sums.append(jnp.where(first > 0.5, their_decay, 1.0) * x + jnp.where(first > 0.5, 1.0, my_decay) * r)
     both = [a * b for a, b in cuts]
     inward = [None] * len(mine)
     outward = sums
@@ -326,7 +325,9 @@
         inward = [
             jnp.where(here > 0.5, g, 0.0 if e is None else e) for g, e in zip(got, inward)
         ]
-        outward = [s + d * g for s, d, g in zip(sums, both, got)]
+        outward = []
+        for total, decay, g in zip(sums, both, got):
+            outward.append(total + decay * g)
     for x, r, e, (my_decay, their_decay) in zip(mine, received, inward, cuts):
         if e is None:
             e = jnp.zeros_like(x)
@@ -453,7 +454,10 @@
     )
     step = 1
     while step < n_seq:
-        gain_grad = gain_grad + lax.ppermute(gain_grad, "seq", [(i, i ^ step) for i in range(n_seq)])
+        moved = lax.ppermute(gain_grad, "seq", [(i, i ^ step) for i in range(n_seq)])
+        gain_grad = gain_grad + moved
+        if 2 * step >= n_seq:
+            gain_grad = gain_grad.reshape(width)
         step *= 2
 
     def finish(parts, states, query_parts, before):
@@ -492,7 +496,7 @@
         key_grad, value_grad = finish(give_parts[-1:], late_give[-1:], [], begun)
     else:
         key_grad, value_grad, query_grad = finish(give_parts, late_give, query_pieces, begun)
-    return query_grad, key_grad, value_grad, gain_grad.reshape(width)
+    return query_grad, key_grad, value_grad, gain_grad
 
 
 def solution(mesh):

time: 103 us -> 103 us (level)
  no operation moved by 1% of the time
where the time goes in v5:
time: 103 us; the launch traced here: 102 us
  waiting for transfers between devices  41 us (40%)
  starting transfers between devices  40.4 us (39%)
  Pallas kernels  15.9 us (15%)
  local copies, waits for them, and re-layouts  2.26 us (2%)
  other arithmetic  1.72 us (2%)
  between operations  1.11 us (1%)
    ppermute x24, starting transfers between devices, carried(): got = [lax.ppermute(x, ('seq', 'dp'), hop(a)) for x in outward]  19.1 us
    ppermute x24, waiting for transfers between devices, carried(): got = [lax.ppermute(x, ('seq', 'dp'), hop(a)) for x in outward]  18.1 us
    pallas_call x18, Pallas kernels, run(): pl.pallas_call(body, out_shape=[jax.ShapeDtypeStruct(*o) for o in outs],...  15.9 us
    ppermute x8, waiting for transfers between devices, carried(): return (kept, [lax.ppermute(x, 'seq', swap) for x in sent])  11.3 us
    ppermute x8, starting transfers between devices, carried(): received = [lax.ppermute(x, 'seq', swap) for x in theirs]  8.1 us
    ppermute x8, starting transfers between devices, carried(): return (kept, [lax.ppermute(x, 'seq', swap) for x in sent])  8.07 us
    ppermute x3, waiting for transfers between devices, on_device(): lax.ppermute(gain_grad, 'seq', [(i, i ^ step) for i in range(n_seq)])  5.64 us
    ppermute x8, waiting for transfers between devices, carried(): received = [lax.ppermute(x, 'seq', swap) for x in theirs]  4.12 us
  transfers between devices with their start and end apart: 47, of which 24 were waited for; matrix products, arithmetic and copies ran while one was open for 2% of the time, Pallas kernels for 10%

profile of v5, /device:TPU:16, one launch (start us, length us, event | category | flops | bytes accessed | tf_op | source)
XLA Modules:
  0.0 102.3 jit_solution(8925261250572336027)
XLA Ops:
  0.7 2.6 %shard_map.93 = (f32[128,16]{1,0:T(8,128)S(1)}, f32[16,128]{1,0:T(8,128)S(1)}, f32[16,128]{1,0:T(8,128)S(1)}, f32[16,128]{1,0:T(8,128)S(1)}, f32[2,128,128]{2,1,...) custom-call(s32[1]{0:T(128)} %bitcast.place_ref, ...), custom_call_target="tpu_custom_call" | custom-call | flops 67108864 | bytes 1048576 | tf_op jit(solution)/shard_map/pallas_call | solution.py:24
  3.3 1.6 %collective-permute-start = (f32[16,128]{1,0:T(8,128)S(1)}, f32[16,128]{1,0:T(8,128)S(1)}, u32[]{:S(2)}, u32[]{:S(2)}) collective-permute-start(f32[16,128]{1,0:T(8,128)S(1)} %get-tuple-element.81), channel_id=1, source_target_pairs={{0,4},{4,0},{8,12},{12,8},{16,20},{20,16},{24,28},{28,24},{1,5},{5... | collective-permute-start | bytes 24584 | tf_op jit(solution)/shard_map/ppermute | solution.py:376
  5.4 1.5 %collective-permute-start.5 = (f32[2,128,128]{2,1,0:T(8,128)S(1)}, f32[2,128,128]{2,1,0:T(8,128)S(1)}, u32[]{:S(2)}, u32[]{:S(2)}) collective-permute-start(f32[2,128,128]{2,1,0:T(8,128)S(1)} %get-tuple-element.85), channel_id=1, source_target_pairs={{0,4},{4,0},{8,12},{12,8},{16,20},{20,16},{24,28},{28,24},{1,5},{5... | collective-permute-start | bytes 393224 | tf_op jit(solution)/shard_map/ppermute | solution.py:308
  7.4 1.5 %collective-permute-start.13 = (f32[2,128,128]{2,1,0:T(8,128)S(1)}, f32[2,128,128]{2,1,0:T(8,128)S(1)}, u32[]{:S(2)}, u32[]{:S(2)}) collective-permute-start(f32[2,128,128]{2,1,0:T(8,128)S(1)} %get-tuple-element.91), channel_id=1, source_target_pairs={{0,4},{4,0},{8,12},{12,8},{16,20},{20,16},{24,28},{28,24},{1,5},{5... | collective-permute-start | bytes 393224 | tf_op jit(solution)/shard_map/ppermute | solution.py:308
  14.2 4.1 %collective-permute-done.13 = f32[2,128,128]{2,1,0:T(8,128)S(1)} collective-permute-done((f32[2,128,128]{2,1,0:T(8,128)S(1)}, f32[2,128,128]{2,1,0:T(8,128)S(1)}, u32[]{:S(2)}, u32[]{:S(2)}) %collective-permute-start.13) | collective-permute-done | bytes 131104 | tf_op jit(solution)/shard_map/ppermute | solution.py:308
  19.1 2.5 %collective-permute-start.3 = (f32[2,128,128]{2,1,0:T(8,128)S(1)}, f32[2,128,128]{2,1,0:T(8,128)S(1)}, u32[]{:S(2)}, u32[]{:S(2)}) collective-permute-start(f32[2,128,128]{2,1,0:T(8,128)S(1)} %multiply_add_fusion.22), channel_id=1, source_target_pairs={{0,1},{1,0},{2,3},{3,2},{4,5},{5,4},{6,7},{7,6},{8,16},{9,17},{10,... | collective-permute-start | bytes 393224 | tf_op jit(solution)/shard_map/ppermute | solution.py:323
  21.6 3.7 %collective-permute-start.15 = (f32[2,128,128]{2,1,0:T(8,128)S(1)}, f32[2,128,128]{2,1,0:T(8,128)S(1)}, u32[]{:S(2)}, u32[]{:S(2)}) collective-permute-start(f32[2,128,128]{2,1,0:T(8,128)S(1)} %multiply_add_fusion.13), channel_id=1, source_target_pairs={{0,1},{1,0},{2,3},{3,2},{4,5},{5,4},{6,7},{7,6},{8,16},{9,17},{10,... | collective-permute-start | bytes 393224 | tf_op jit(solution)/shard_map/ppermute | solution.py:323
  25.3 1.9 %collective-permute-start.11 = (f32[2,128,128]{2,1,0:T(8,128)S(1)}, f32[2,128,128]{2,1,0:T(8,128)S(1)}, u32[]{:S(2)}, u32[]{:S(2)}) collective-permute-start(f32[2,128,128]{2,1,0:T(8,128)S(1)} %multiply_add_fusion.16), channel_id=1, source_target_pairs={{0,1},{1,0},{2,3},{3,2},{4,5},{5,4},{6,7},{7,6},{8,16},{9,17},{10,... | collective-permute-start | bytes 393224 | tf_op jit(solution)/shard_map/ppermute | solution.py:323
  35.5 4.6 %collective-permute-done.8 = f32[2,128,128]{2,1,0:T(8,128)S(1)} collective-permute-done((f32[2,128,128]{2,1,0:T(8,128)S(1)}, f32[2,128,128]{2,1,0:T(8,128)S(1)}, u32[]{:S(2)}, u32[]{:S(2)}) %collective-permute-start.8) | collective-permute-done | bytes 131104 | tf_op jit(solution)/shard_map/ppermute | solution.py:323
  44.5 2.7 %collective-permute-done.19.refs_9_.refs_7_ = f32[2,128,128]{2,1,0:T(8,128)S(1)} collective-permute-done((f32[2,128,128]{2,1,0:T(8,128)S(1)}, f32[2,128,128]{2,1,0:T(8,128)S(1)}, u32[]{:S(2)}, u32[]{:S(2)}) %collective-permute-start.19) | collective-permute-done | bytes 131104 | tf_op jit(solution)/shard_map/ppermute | solution.py:339
  47.3 1.4 %collective-permute-done.18.refs_8_ = f32[2,128,128]{2,1,0:T(8,128)S(1)} collective-permute-done((f32[2,128,128]{2,1,0:T(8,128)S(1)}, f32[2,128,128]{2,1,0:T(8,128)S(1)}, u32[]{:S(2)}, u32[]{:S(2)}) %collective-permute-start.18) | collective-permute-done | bytes 131104 | tf_op jit(solution)/shard_map/ppermute | solution.py:339
  49.4 1.6 %collective-permute-start.22 = (f32[8,128]{1,0:T(8,128)S(1)}, f32[8,128]{1,0:T(8,128)S(1)}, u32[]{:S(2)}, u32[]{:S(2)}) collective-permute-start(f32[8,128]{1,0:T(8,128)S(1)} %get-tuple-element.98.refs_4_), channel_id=1, source_target_pairs={{0,2},{1,3},{2,0},{3,1},{4,6},{5,7},{6,4},{7,5},{8,10},{9,11},{10,... | collective-permute-start | bytes 12296 | tf_op jit(solution)/shard_map/ppermute | solution.py:424
  55.4 1.4 %collective-permute-start.24 = (f32[2,128,128]{2,1,0:T(8,128)S(1)}, f32[2,128,128]{2,1,0:T(8,128)S(1)}, u32[]{:S(2)}, u32[]{:S(2)}) collective-permute-start(f32[2,128,128]{2,1,0:T(8,128)S(1)} %get-tuple-element.110), channel_id=1, source_target_pairs={{0,4},{4,0},{8,12},{12,8},{16,20},{20,16},{24,28},{28,24},{1,5},{5... | collective-permute-start | bytes 393224 | tf_op jit(solution)/shard_map/ppermute | solution.py:308
  57.5 1.4 %collective-permute-start.34 = (f32[2,128,128]{2,1,0:T(8,128)S(1)}, f32[2,128,128]{2,1,0:T(8,128)S(1)}, u32[]{:S(2)}, u32[]{:S(2)}) collective-permute-start(f32[2,128,128]{2,1,0:T(8,128)S(1)} %get-tuple-element.117), channel_id=1, source_target_pairs={{0,4},{4,0},{8,12},{12,8},{16,20},{20,16},{24,28},{28,24},{1,5},{5... | collective-permute-start | bytes 393224 | tf_op jit(solution)/shard_map/ppermute | solution.py:308
  62.6 2.3 %collective-permute-done.45 = f32[16,128]{1,0:T(8,128)S(1)} collective-permute-done((f32[16,128]{1,0:T(8,128)S(1)}, f32[16,128]{1,0:T(8,128)S(1)}, u32[]{:S(2)}, u32[]{:S(2)}) %collective-permute-start.45) | collective-permute-done | bytes 8224 | tf_op jit(solution)/shard_map/ppermute | solution.py:457
  66.2 3.3 %collective-permute-done.46 = f32[16,128]{1,0:T(8,128)S(1)} collective-permute-done((f32[16,128]{1,0:T(8,128)S(1)}, f32[16,128]{1,0:T(8,128)S(1)}, u32[]{:S(2)}, u32[]{:S(2)}) %collective-permute-start.46) | collective-permute-done | bytes 8224 | tf_op jit(solution)/shard_map/ppermute | solution.py:457
  70.7 1.6 %collective-permute-start.30 = (f32[2,128,128]{2,1,0:T(8,128)S(1)}, f32[2,128,128]{2,1,0:T(8,128)S(1)}, u32[]{:S(2)}, u32[]{:S(2)}) collective-permute-start(f32[2,128,128]{2,1,0:T(8,128)S(1)} %multiply_add_fusion.8), channel_id=1, source_target_pairs={{0,1},{1,0},{2,3},{3,2},{4,5},{5,4},{6,7},{7,6},{8,9},{9,8},{10,11... | collective-permute-start | bytes 393224 | tf_op jit(solution)/shard_map/ppermute | solution.py:323
  72.9 1.6 %collective-permute-start.40 = (f32[2,128,128]{2,1,0:T(8,128)S(1)}, f32[2,128,128]{2,1,0:T(8,128)S(1)}, u32[]{:S(2)}, u32[]{:S(2)}) collective-permute-start(f32[2,128,128]{2,1,0:T(8,128)S(1)} %multiply_add_fusion.2), channel_id=1, source_target_pairs={{0,1},{1,0},{2,3},{3,2},{4,5},{5,4},{6,7},{7,6},{8,9},{9,8},{10,11... | collective-permute-start | bytes 393224 | tf_op jit(solution)/shard_map/ppermute | solution.py:323
  74.5 2.0 %collective-permute-done.25 = f32[2,128,128]{2,1,0:T(8,128)S(1)} collective-permute-done((f32[2,128,128]{2,1,0:T(8,128)S(1)}, f32[2,128,128]{2,1,0:T(8,128)S(1)}, u32[]{:S(2)}, u32[]{:S(2)}) %collective-permute-start.25) | collective-permute-done | bytes 131104 | tf_op jit(solution)/shard_map/ppermute | solution.py:323
  76.7 1.5 %collective-permute-done.30 = f32[2,128,128]{2,1,0:T(8,128)S(1)} collective-permute-done((f32[2,128,128]{2,1,0:T(8,128)S(1)}, f32[2,128,128]{2,1,0:T(8,128)S(1)}, u32[]{:S(2)}, u32[]{:S(2)}) %collective-permute-start.30) | collective-permute-done | bytes 131104 | tf_op jit(solution)/shard_map/ppermute | solution.py:323
  87.0 1.5 %collective-permute-start.28 = (f32[2,128,128]{2,1,0:T(8,128)S(1)}, f32[2,128,128]{2,1,0:T(8,128)S(1)}, u32[]{:S(2)}, u32[]{:S(2)}) collective-permute-start(f32[2,128,128]{2,1,0:T(8,128)S(1)} %fusion.9), channel_id=1, source_target_pairs={{0,4},{4,0},{8,12},{12,8},{16,20},{20,16},{24,28},{28,24},{1,5},{5... | collective-permute-start | bytes 393224 | tf_op jit(solution)/shard_map/ppermute | solution.py:339
  89.3 1.5 %collective-permute-start.38 = (f32[2,128,128]{2,1,0:T(8,128)S(1)}, f32[2,128,128]{2,1,0:T(8,128)S(1)}, u32[]{:S(2)}, u32[]{:S(2)}) collective-permute-start(f32[2,128,128]{2,1,0:T(8,128)S(1)} %fusion.13), channel_id=1, source_target_pairs={{0,4},{4,0},{8,12},{12,8},{16,20},{20,16},{24,28},{28,24},{1,5},{5... | collective-permute-start | bytes 393224 | tf_op jit(solution)/shard_map/ppermute | solution.py:339
  93.5 2.8 %collective-permute-done.33.refs_8_ = f32[2,128,128]{2,1,0:T(8,128)S(1)} collective-permute-done((f32[2,128,128]{2,1,0:T(8,128)S(1)}, f32[2,128,128]{2,1,0:T(8,128)S(1)}, u32[]{:S(2)}, u32[]{:S(2)}) %collective-permute-start.33) | collective-permute-done | bytes 131104 | tf_op jit(solution)/shard_map/ppermute | solution.py:339
  96.3 2.8 %collective-permute-done.38.refs_9_ = f32[2,128,128]{2,1,0:T(8,128)S(1)} collective-permute-done((f32[2,128,128]{2,1,0:T(8,128)S(1)}, f32[2,128,128]{2,1,0:T(8,128)S(1)}, u32[]{:S(2)}, u32[]{:S(2)}) %collective-permute-start.38) | collective-permute-done | bytes 131104 | tf_op jit(solution)/shard_map/ppermute | solution.py:339
  (147 shorter events, 47.6 us)
Async XLA Ops:
  3.3 10.7 %collective-permute-start = (f32[16,128]{1,0:T(8,128)S(1)}, f32[16,128]{1,0:T(8,128)S(1)}, u32[]{:S(2)}, u32[]{:S(2)}) collective-permute-start(f32[16,128]{1,0:T(8,128)S(1)} %get-tuple-element.81), channel_id=1, source_target_pairs={{0,4},{4,0},{8,12},{12,8},{16,20},{20,16},{24,28},{28,24},{1,5},{5... | collective-permute-start | bytes 24584 | tf_op jit(solution)/shard_map/ppermute | solution.py:376
  4.9 9.2 %collective-permute-start.1 = (f32[2,128,128]{2,1,0:T(8,128)S(1)}, f32[2,128,128]{2,1,0:T(8,128)S(1)}, u32[]{:S(2)}, u32[]{:S(2)}) collective-permute-start(f32[2,128,128]{2,1,0:T(8,128)S(1)} %get-tuple-element.83), channel_id=1, source_target_pairs={{0,4},{4,0},{8,12},{12,8},{16,20},{20,16},{24,28},{28,24},{1,5},{5... | collective-permute-start | bytes 393224 | tf_op jit(solution)/shard_map/ppermute | solution.py:308
  5.4 13.6 %collective-permute-start.5 = (f32[2,128,128]{2,1,0:T(8,128)S(1)}, f32[2,128,128]{2,1,0:T(8,128)S(1)}, u32[]{:S(2)}, u32[]{:S(2)}) collective-permute-start(f32[2,128,128]{2,1,0:T(8,128)S(1)} %get-tuple-element.85), channel_id=1, source_target_pairs={{0,4},{4,0},{8,12},{12,8},{16,20},{20,16},{24,28},{28,24},{1,5},{5... | collective-permute-start | bytes 393224 | tf_op jit(solution)/shard_map/ppermute | solution.py:308
  6.9 11.5 %collective-permute-start.9 = (f32[2,128,128]{2,1,0:T(8,128)S(1)}, f32[2,128,128]{2,1,0:T(8,128)S(1)}, u32[]{:S(2)}, u32[]{:S(2)}) collective-permute-start(f32[2,128,128]{2,1,0:T(8,128)S(1)} %get-tuple-element.88), channel_id=1, source_target_pairs={{0,4},{4,0},{8,12},{12,8},{16,20},{20,16},{24,28},{28,24},{1,5},{5... | collective-permute-start | bytes 393224 | tf_op jit(solution)/shard_map/ppermute | solution.py:308
  7.4 10.9 %collective-permute-start.13 = (f32[2,128,128]{2,1,0:T(8,128)S(1)}, f32[2,128,128]{2,1,0:T(8,128)S(1)}, u32[]{:S(2)}, u32[]{:S(2)}) collective-permute-start(f32[2,128,128]{2,1,0:T(8,128)S(1)} %get-tuple-element.91), channel_id=1, source_target_pairs={{0,4},{4,0},{8,12},{12,8},{16,20},{20,16},{24,28},{28,24},{1,5},{5... | collective-permute-start | bytes 393224 | tf_op jit(solution)/shard_map/ppermute | solution.py:308
  18.4 6.9 %collective-permute-start.10 = (f32[2,128,128]{2,1,0:T(8,128)S(1)}, f32[2,128,128]{2,1,0:T(8,128)S(1)}, u32[]{:S(2)}, u32[]{:S(2)}) collective-permute-start(f32[2,128,128]{2,1,0:T(8,128)S(1)} %multiply_add_fusion.17), channel_id=1, source_target_pairs={{0,8},{1,9},{2,10},{3,11},{4,12},{5,13},{6,14},{7,15},{8,0},{9,1},... | collective-permute-start | bytes 393224 | tf_op jit(solution)/shard_map/ppermute | solution.py:323
  19.0 8.2 %collective-permute-start.6 = (f32[2,128,128]{2,1,0:T(8,128)S(1)}, f32[2,128,128]{2,1,0:T(8,128)S(1)}, u32[]{:S(2)}, u32[]{:S(2)}) collective-permute-start(f32[2,128,128]{2,1,0:T(8,128)S(1)} %multiply_add_fusion.20), channel_id=1, source_target_pairs={{0,8},{1,9},{2,10},{3,11},{4,12},{5,13},{6,14},{7,15},{8,0},{9,1},... | collective-permute-start | bytes 393224 | tf_op jit(solution)/shard_map/ppermute | solution.py:323
  19.1 9.5 %collective-permute-start.3 = (f32[2,128,128]{2,1,0:T(8,128)S(1)}, f32[2,128,128]{2,1,0:T(8,128)S(1)}, u32[]{:S(2)}, u32[]{:S(2)}) collective-permute-start(f32[2,128,128]{2,1,0:T(8,128)S(1)} %multiply_add_fusion.22), channel_id=1, source_target_pairs={{0,1},{1,0},{2,3},{3,2},{4,5},{5,4},{6,7},{7,6},{8,16},{9,17},{10,... | collective-permute-start | bytes 393224 | tf_op jit(solution)/shard_map/ppermute | solution.py:323
  21.6 8.0 %collective-permute-start.15 = (f32[2,128,128]{2,1,0:T(8,128)S(1)}, f32[2,128,128]{2,1,0:T(8,128)S(1)}, u32[]{:S(2)}, u32[]{:S(2)}) collective-permute-start(f32[2,128,128]{2,1,0:T(8,128)S(1)} %multiply_add_fusion.13), channel_id=1, source_target_pairs={{0,1},{1,0},{2,3},{3,2},{4,5},{5,4},{6,7},{7,6},{8,16},{9,17},{10,... | collective-permute-start | bytes 393224 | tf_op jit(solution)/shard_map/ppermute | solution.py:323
  25.3 6.8 %collective-permute-start.11 = (f32[2,128,128]{2,1,0:T(8,128)S(1)}, f32[2,128,128]{2,1,0:T(8,128)S(1)}, u32[]{:S(2)}, u32[]{:S(2)}) collective-permute-start(f32[2,128,128]{2,1,0:T(8,128)S(1)} %multiply_add_fusion.16), channel_id=1, source_target_pairs={{0,1},{1,0},{2,3},{3,2},{4,5},{5,4},{6,7},{7,6},{8,16},{9,17},{10,... | collective-permute-start | bytes 393224 | tf_op jit(solution)/shard_map/ppermute | solution.py:323
  29.6 10.6 %collective-permute-start.16 = (f32[2,128,128]{2,1,0:T(8,128)S(1)}, f32[2,128,128]{2,1,0:T(8,128)S(1)}, u32[]{:S(2)}, u32[]{:S(2)}) collective-permute-start(f32[2,128,128]{2,1,0:T(8,128)S(1)} %multiply_add_fusion.12), channel_id=1, source_target_pairs={{0,1},{1,0},{2,3},{3,2},{4,5},{5,4},{6,7},{7,6},{8,9},{9,8},{10,11... | collective-permute-start | bytes 393224 | tf_op jit(solution)/shard_map/ppermute | solution.py:323
  32.1 8.1 %collective-permute-start.12 = (f32[2,128,128]{2,1,0:T(8,128)S(1)}, f32[2,128,128]{2,1,0:T(8,128)S(1)}, u32[]{:S(2)}, u32[]{:S(2)}) collective-permute-start(f32[2,128,128]{2,1,0:T(8,128)S(1)} %multiply_add_fusion.15), channel_id=1, source_target_pairs={{0,1},{1,0},{2,3},{3,2},{4,5},{5,4},{6,7},{7,6},{8,9},{9,8},{10,11... | collective-permute-start | bytes 393224 | tf_op jit(solution)/shard_map/ppermute | solution.py:323
  34.6 10.0 %collective-permute-start.17 = (f32[2,128,128]{2,1,0:T(8,128)S(1)}, f32[2,128,128]{2,1,0:T(8,128)S(1)}, u32[]{:S(2)}, u32[]{:S(2)}) collective-permute-start(f32[2,128,128]{2,1,0:T(8,128)S(1)} %get-tuple-element.94), channel_id=1, source_target_pairs={{0,4},{4,0},{8,12},{12,8},{16,20},{20,16},{24,28},{28,24},{1,5},{5... | collective-permute-start | bytes 393224 | tf_op jit(solution)/shard_map/ppermute | solution.py:339
  40.3 8.7 %collective-permute-start.20 = (f32[2,128,128]{2,1,0:T(8,128)S(1)}, f32[2,128,128]{2,1,0:T(8,128)S(1)}, u32[]{:S(2)}, u32[]{:S(2)}) collective-permute-start(f32[2,128,128]{2,1,0:T(8,128)S(1)} %get-tuple-element.150), channel_id=1, source_target_pairs={{0,4},{4,0},{8,12},{12,8},{16,20},{20,16},{24,28},{28,24},{1,5},{5... | collective-permute-start | bytes 393224 | tf_op jit(solution)/shard_map/ppermute | solution.py:339
  55.4 14.7 %collective-permute-start.24 = (f32[2,128,128]{2,1,0:T(8,128)S(1)}, f32[2,128,128]{2,1,0:T(8,128)S(1)}, u32[]{:S(2)}, u32[]{:S(2)}) collective-permute-start(f32[2,128,128]{2,1,0:T(8,128)S(1)} %get-tuple-element.110), channel_id=1, source_target_pairs={{0,4},{4,0},{8,12},{12,8},{16,20},{20,16},{24,28},{28,24},{1,5},{5... | collective-permute-start | bytes 393224 | tf_op jit(solution)/shard_map/ppermute | solution.py:308
  56.9 13.8 %collective-permute-start.29 = (f32[2,128,128]{2,1,0:T(8,128)S(1)}, f32[2,128,128]{2,1,0:T(8,128)S(1)}, u32[]{:S(2)}, u32[]{:S(2)}) collective-permute-start(f32[2,128,128]{2,1,0:T(8,128)S(1)} %get-tuple-element.113), channel_id=1, source_target_pairs={{0,4},{4,0},{8,12},{12,8},{16,20},{20,16},{24,28},{28,24},{1,5},{5... | collective-permute-start | bytes 393224 | tf_op jit(solution)/shard_map/ppermute | solution.py:308
  57.5 14.8 %collective-permute-start.34 = (f32[2,128,128]{2,1,0:T(8,128)S(1)}, f32[2,128,128]{2,1,0:T(8,128)S(1)}, u32[]{:S(2)}, u32[]{:S(2)}) collective-permute-start(f32[2,128,128]{2,1,0:T(8,128)S(1)} %get-tuple-element.117), channel_id=1, source_target_pairs={{0,4},{4,0},{8,12},{12,8},{16,20},{20,16},{24,28},{28,24},{1,5},{5... | collective-permute-start | bytes 393224 | tf_op jit(solution)/shard_map/ppermute | solution.py:308
  58.9 14.0 %collective-permute-start.39 = (f32[2,128,128]{2,1,0:T(8,128)S(1)}, f32[2,128,128]{2,1,0:T(8,128)S(1)}, u32[]{:S(2)}, u32[]{:S(2)}) collective-permute-start(f32[2,128,128]{2,1,0:T(8,128)S(1)} %get-tuple-element.131), channel_id=1, source_target_pairs={{0,4},{4,0},{8,12},{12,8},{16,20},{20,16},{24,28},{28,24},{1,5},{5... | collective-permute-start | bytes 393224 | tf_op jit(solution)/shard_map/ppermute | solution.py:308
  70.7 7.5 %collective-permute-start.30 = (f32[2,128,128]{2,1,0:T(8,128)S(1)}, f32[2,128,128]{2,1,0:T(8,128)S(1)}, u32[]{:S(2)}, u32[]{:S(2)}) collective-permute-start(f32[2,128,128]{2,1,0:T(8,128)S(1)} %multiply_add_fusion.8), channel_id=1, source_target_pairs={{0,1},{1,0},{2,3},{3,2},{4,5},{5,4},{6,7},{7,6},{8,9},{9,8},{10,11... | collective-permute-start | bytes 393224 | tf_op jit(solution)/shard_map/ppermute | solution.py:323
  72.3 7.3 %collective-permute-start.35 = (f32[2,128,128]{2,1,0:T(8,128)S(1)}, f32[2,128,128]{2,1,0:T(8,128)S(1)}, u32[]{:S(2)}, u32[]{:S(2)}) collective-permute-start(f32[2,128,128]{2,1,0:T(8,128)S(1)} %multiply_add_fusion.5), channel_id=1, source_target_pairs={{0,1},{1,0},{2,3},{3,2},{4,5},{5,4},{6,7},{7,6},{8,9},{9,8},{10,11... | collective-permute-start | bytes 393224 | tf_op jit(solution)/shard_map/ppermute | solution.py:323
  72.9 8.1 %collective-permute-start.40 = (f32[2,128,128]{2,1,0:T(8,128)S(1)}, f32[2,128,128]{2,1,0:T(8,128)S(1)}, u32[]{:S(2)}, u32[]{:S(2)}) collective-permute-start(f32[2,128,128]{2,1,0:T(8,128)S(1)} %multiply_add_fusion.2), channel_id=1, source_target_pairs={{0,1},{1,0},{2,3},{3,2},{4,5},{5,4},{6,7},{7,6},{8,9},{9,8},{10,11... | collective-permute-start | bytes 393224 | tf_op jit(solution)/shard_map/ppermute | solution.py:323
  88.6 7.7 %collective-permute-start.33 = (f32[2,128,128]{2,1,0:T(8,128)S(1)}, f32[2,128,128]{2,1,0:T(8,128)S(1)}, u32[]{:S(2)}, u32[]{:S(2)}) collective-permute-start(f32[2,128,128]{2,1,0:T(8,128)S(1)} %fusion.11), channel_id=1, source_target_pairs={{0,4},{4,0},{8,12},{12,8},{16,20},{20,16},{24,28},{28,24},{1,5},{5... | collective-permute-start | bytes 393224 | tf_op jit(solution)/shard_map/ppermute | solution.py:339
  89.3 9.7 %collective-permute-start.38 = (f32[2,128,128]{2,1,0:T(8,128)S(1)}, f32[2,128,128]{2,1,0:T(8,128)S(1)}, u32[]{:S(2)}, u32[]{:S(2)}) collective-permute-start(f32[2,128,128]{2,1,0:T(8,128)S(1)} %fusion.13), channel_id=1, source_target_pairs={{0,4},{4,0},{8,12},{12,8},{16,20},{20,16},{24,28},{28,24},{1,5},{5... | collective-permute-start | bytes 393224 | tf_op jit(solution)/shard_map/ppermute | solution.py:339
  90.9 10.5 %collective-permute-start.43 = (f32[2,128,128]{2,1,0:T(8,128)S(1)}, f32[2,128,128]{2,1,0:T(8,128)S(1)}, u32[]{:S(2)}, u32[]{:S(2)}) collective-permute-start(f32[2,128,128]{2,1,0:T(8,128)S(1)} %get-tuple-element.142), channel_id=1, source_target_pairs={{0,4},{4,0},{8,12},{12,8},{16,20},{20,16},{24,28},{28,24},{1,5},{5... | collective-permute-start | bytes 393224 | tf_op jit(solution)/shard_map/ppermute | solution.py:339
  (29 other events, 136.6 us)

commit v6 on v5

--- a/solution.py
+++ b/solution.py
@@ -122,15 +122,15 @@
         start += out.shape[0]
 
 
-def more_states(half, dim, place_ref, k_ref, v_ref, cum_t_ref, *outs):
-    side = side_of(place_ref, False)
+def more_states(half, dim, give, start, place_ref, k_ref, v_ref, cum_t_ref, *outs):
+    side = side_of(place_ref, give)
     cum_t = cum_t_ref[...]
     tail = jnp.exp(cum_t[cum_t.shape[0] - 1 :, :] - cum_t)
     state_into(
         outs,
         lambda j: k_ref[:, lanes(side, half, j, dim)],
         lambda j: v_ref[:, lanes(side, half, j, dim)],
-        tail, side, half,
+        tail, side, half, start,
     )
 
 
@@ -187,7 +187,7 @@
         sums_ref[1] = cross
 
 
-def gradient(half, dim, give, full_width, n_sums, n_attn, place_ref, *refs):
+def gradient(half, dim, give, start, full_width, n_sums, n_attn, place_ref, *refs):
     side = side_of(place_ref, give)
     q_ref, g_ref, gain_ref, cum_t_ref = refs[:4]
     sums = refs[4 : 4 + n_sums]
@@ -203,34 +203,34 @@
     inv = jnp.broadcast_to(inv_row, (tok, tok)).T
     mean = jnp.broadcast_to(mean_row, (tok, tok)).T
     lead = jnp.exp(cum_t_ref[...])
+    attn = [ref[:, i * dim : (i + 1) * dim] for ref in attns for i in range(ref.shape[1] // dim)]
     kept = {}
-    j = 0
-    for ref in attns:
-        for i in range(ref.shape[1] // dim):
-            at = lanes(side, half, j, dim)
-            normed = ref[:, i * dim : (i + 1) * dim] * inv
-            g = g_ref[:, at].astype(f32)
-            d = (inv * (g * gain_ref[:, at] - normed * mean)).astype(bf16)
-            d_ref[:, j * dim : (j + 1) * dim] = d
-            gain_part_ref[j : j + 1, :] = jnp.sum(g * normed, axis=0, keepdims=True)
-            kept[j] = d
-            j += 1
-    state_into(outs, lambda j: q_ref[:, lanes(side, half, j, dim)], lambda j: kept[j], lead, side, half)
-
-
-def local_grads(half, dim, give, start, place_ref, *refs):
+    for i in range(d_ref.shape[1] // dim):
+        j = start + i
+        at = lanes(side, half, j, dim)
+        normed = attn[j] * inv
+        g = g_ref[:, at].astype(f32)
+        d = (inv * (g * gain_ref[:, at] - normed * mean)).astype(bf16)
+        d_ref[:, i * dim : (i + 1) * dim] = d
+        gain_part_ref[i : i + 1, :] = jnp.sum(g * normed, axis=0, keepdims=True)
+        kept[j] = d
+    state_into(outs, lambda j: q_ref[:, lanes(side, half, j, dim)], lambda j: kept[j], lead, side, half, start)
+
+
+def local_grads(half, dim, give, start, n_d, place_ref, *refs):
     side = side_of(place_ref, give)
-    q_ref, k_ref, v_ref, cum_t_ref, cum_r_ref, mixed_ref, d_ref = refs[:7]
+    q_ref, k_ref, v_ref, cum_t_ref, cum_r_ref, mixed_ref = refs[:6]
+    d_all = [ref[:, i * dim : (i + 1) * dim] for ref in refs[6 : 6 + n_d] for i in range(ref.shape[1] // dim)]
     query_ref, kg_ref, vg_ref = refs[-3:]
     cum_t = cum_t_ref[...]
     lead = jnp.exp(cum_t)
     count = 0
-    for ref in refs[7:-3]:
+    for ref in refs[6 + n_d : -3]:
         for n in range(ref.shape[0]):
             j = start + count
             at = lanes(side, half, j, dim)
             to = slice(count * dim, (count + 1) * dim)
-            d = d_ref[:, j * dim : (j + 1) * dim]
+            d = d_all[j]
             graded = (dot(d, v_ref[:, at], 1, 1) * weights_of(cum_t, cum_r_ref, side, half, j)).astype(bf16)
             hi, lo = split(ref[n])
             outer = (dot(d, hi, 1, 1) + dot(d, lo, 1, 1)) * column(lead, side, half, j)
@@ -360,23 +360,31 @@
     state = [((n, dim, dim), f32) for n in sizes]
     row_bytes = tok * half * dim
 
+    first = sizes[0]
     cum_t, cum_r, total, flags, *give = call(
         functools.partial(first_states, half, dim, pairs),
-        [((tok, heads), f32), ((heads, tok), f32), ((heads, dim), f32), ((rows, dim), f32)] + state,
-        2 * half * pair_flops, 8 * row_bytes,
+        [((tok, heads), f32), ((heads, tok), f32), ((heads, dim), f32), ((rows, dim), f32)] + state[:1],
+        2 * first * pair_flops, 8 * tok * first * dim,
         in_hbm=(0, 1, 2),
         scratch=[
-            pltpu.VMEM((tok, half * dim), bf16),
-            pltpu.VMEM((tok, half * dim), bf16),
+            pltpu.VMEM((tok, first * dim), bf16),
+            pltpu.VMEM((tok, first * dim), bf16),
             pltpu.VMEM((heads, tok), f32),
-            pltpu.SemaphoreType.DMA((1 + 2 * chunks,)),
+            pltpu.SemaphoreType.DMA((3,)),
         ],
     )(place, keys, values, log_decay)
+
+    def states_of(is_give, start, outs):
+        return call(
+            functools.partial(more_states, half, dim, is_give, start),
+            outs, 2 * half * pair_flops, 8 * row_bytes,
+        )(place, keys, values, cum_t)
+
+    if chunks > 1:
+        give += states_of(True, first, state[1:])
     swap = [(i, i ^ 1) for i in range(n_seq)]
     other = lax.ppermute(total, "seq", swap)
-    own_states = call(
-        functools.partial(more_states, half, dim), state, 2 * half * pair_flops, 8 * row_bytes
-    )(place, keys, values, cum_t)
+    own_states = states_of(False, 0, state)
     places = [sum(sizes[:c]) for c in range(chunks)]
     middle = (chunks + 1) // 2
     pieces = [
@@ -426,24 +434,36 @@
     else:
         all_sums = [lax.psum(sums, "dp")]
 
-    def grads(is_give, attns):
+    def grads(is_give, attns, run):
+        count = sum(sizes[c] for c in run)
         return call(
-            functools.partial(gradient, half, dim, is_give, full_width, len(all_sums), len(attns)),
-            [((tok, half * dim), bf16), ((half, dim), f32)] + state,
-            2 * half * pair_flops, 14 * row_bytes,
+            functools.partial(
+                gradient, half, dim, is_give, places[run[0]], full_width, len(all_sums), len(attns)
+            ),
+            [((tok, count * dim), bf16), ((count, dim), f32)] + [state[c] for c in run],
+            2 * count * pair_flops, 14 * tok * count * dim,
         )(place, queries, output_gradient, gain_row, cum_t, *all_sums, *attns)
 
-    d_give, gain_give, *back_give = grads(True, attn_give)
-    d_own, gain_own, *back_own = grads(False, [attn_own])
+    d_first, gain_first, *back_give = grads(True, attn_give, [0])
+    d_give, gain_give = [d_first], [gain_first]
+    if chunks > 1:
+        d_rest, gain_rest, *back_rest = grads(True, attn_give, list(range(1, chunks)))
+        d_give.append(d_rest)
+        gain_give.append(gain_rest)
+        back_give += back_rest
+    gain_give = jnp.concatenate(gain_give, axis=0)
+    d_own, gain_own, *back_own = grads(False, [attn_own], list(range(chunks)))
+    d_own = [d_own]
     query_pieces, local = [], []
     for n, (is_give, run) in enumerate(pieces):
         count = sum(sizes[c] for c in run)
         states = [(in_give if is_give else in_own)[c] for c in run]
+        d_side = d_give if is_give else d_own
         query, key_part, value_part = call(
-            functools.partial(local_grads, half, dim, is_give, places[run[0]]),
+            functools.partial(local_grads, half, dim, is_give, places[run[0]], len(d_side)),
             [((tok, count * dim), bf16), ((tok, count * dim), f32), ((tok, count * dim), f32)],
             6 * count * pair_flops, 40 * tok * count * dim,
-        )(place, queries, keys, values, cum_t, cum_r, mixed[n], d_give if is_give else d_own, *states)
+        )(place, queries, keys, values, cum_t, cum_r, mixed[n], *d_side, *states)
         query_pieces.append(((is_give, places[run[0]]), query))
         local.append(((is_give, places[run[0]]), key_part, value_part))
 

time: 103 us -> 111 us (1.078)
  the two profiles are of different devices: /device:TPU:16 before, /device:TPU:0 now
where the time goes in v6:
time: 111 us
  starting transfers between devices  57.1 us (51%)
  waiting for transfers between devices  34.3 us (31%)
  Pallas kernels  15.6 us (14%)
  other arithmetic  1.76 us (2%)
    ppermute x24, starting transfers between devices, carried(): got = [lax.ppermute(x, ('seq', 'dp'), hop(a)) for x in outward]  25.4 us
    pallas_call x20, Pallas kernels, run(): pl.pallas_call(body, out_shape=[jax.ShapeDtypeStruct(*o) for o in outs],...  15.6 us
    ppermute x8, waiting for transfers between devices, carried(): return (kept, [lax.ppermute(x, 'seq', swap) for x in sent])  12 us
    ppermute x3, starting transfers between devices, on_device(): lax.ppermute(gain_grad, 'seq', [(i, i ^ step) for i in range(n_seq)])  10 us
    ppermute x24, waiting for transfers between devices, carried(): got = [lax.ppermute(x, ('seq', 'dp'), hop(a)) for x in outward]  9.14 us
    ppermute x8, starting transfers between devices, carried(): return (kept, [lax.ppermute(x, 'seq', swap) for x in sent])  8.44 us
    ppermute x8, starting transfers between devices, carried(): received = [lax.ppermute(x, 'seq', swap) for x in theirs]  8.3 us
    ppermute x3, waiting for transfers between devices, on_device(): lax.ppermute(gain_grad, 'seq', [(i, i ^ step) for i in range(n_seq)])  7.54 us
  transfers between devices with their start and end apart: 47, of which 20 were waited for; matrix products, arithmetic and copies ran while one was open for 2% of the time, Pallas kernels for 11%

profile of v6, /device:TPU:0, one launch (start us, length us, event | category | flops | bytes accessed | tf_op | source)
XLA Modules:
  0.0 110.8 jit_solution(15072623819211058483)
XLA Ops:
  0.7 1.6 %shard_map.93 = (f32[128,16]{1,0:T(8,128)S(1)}, f32[16,128]{1,0:T(8,128)S(1)}, f32[16,128]{1,0:T(8,128)S(1)}, f32[16,128]{1,0:T(8,128)S(1)}, f32[2,128,128]{2,1,0:T(8,128)S(1)}) custom-call(s32[1]{0:T(128)} %bitcast.place_ref, bf16[128,2048]{1,0:T(8,128)(2,1)} %refs_0_.25, bf16[128,2048]{1,0:T(8,128)(2,1)} %refs_1_.25, f32[16,128]{1,0:T(8,128)} %ld_ref.1), custom_call_target="tpu_custom_call" | custom-call | flops 16777216 | bytes 262144 | tf_op jit(solution)/shard_map/pallas_call | solution.py:24
  2.3 3.1 %collective-permute-start = (f32[16,128]{1,0:T(8,128)S(1)}, f32[16,128]{1,0:T(8,128)S(1)}, u32[]{:S(2)}, u32[]{:S(2)}) collective-permute-start(f32[16,128]{1,0:T(8,128)S(1)} %get-tuple-element.83), channel_id=1, source_target_pairs={{0,4},{4,0},{8,12},{12,8},{16,20},{20,16},{24,28},{28,24},{1,5},{5... | collective-permute-start | bytes 24584 | tf_op jit(solution)/shard_map/ppermute | solution.py:386
  6.0 2.0 %collective-permute-start.5 = (f32[2,128,128]{2,1,0:T(8,128)S(1)}, f32[2,128,128]{2,1,0:T(8,128)S(1)}, u32[]{:S(2)}, u32[]{:S(2)}) collective-permute-start(f32[2,128,128]{2,1,0:T(8,128)S(1)} %get-tuple-element.87), channel_id=1, source_target_pairs={{0,4},{4,0},{8,12},{12,8},{16,20},{20,16},{24,28},{28,24},{1,5},{5... | collective-permute-start | bytes 393224 | tf_op jit(solution)/shard_map/ppermute | solution.py:308
  8.0 1.9 %collective-permute-start.13 = (f32[2,128,128]{2,1,0:T(8,128)S(1)}, f32[2,128,128]{2,1,0:T(8,128)S(1)}, u32[]{:S(2)}, u32[]{:S(2)}) collective-permute-start(f32[2,128,128]{2,1,0:T(8,128)S(1)} %get-tuple-element.93), channel_id=1, source_target_pairs={{0,4},{4,0},{8,12},{12,8},{16,20},{20,16},{24,28},{28,24},{1,5},{5... | collective-permute-start | bytes 393224 | tf_op jit(solution)/shard_map/ppermute | solution.py:308
  13.8 1.6 %collective-permute-start.2 = (f32[2,128,128]{2,1,0:T(8,128)S(1)}, f32[2,128,128]{2,1,0:T(8,128)S(1)}, u32[]{:S(2)}, u32[]{:S(2)}) collective-permute-start(f32[2,128,128]{2,1,0:T(8,128)S(1)} %multiply_add_fusion.23), channel_id=1, source_target_pairs={{0,8},{1,9},{2,10},{3,11},{4,12},{5,13},{6,14},{7,15},{8,0},{9,1},... | collective-permute-start | bytes 393224 | tf_op jit(solution)/shard_map/ppermute | solution.py:323
  15.4 3.3 %collective-permute-done.13 = f32[2,128,128]{2,1,0:T(8,128)S(1)} collective-permute-done((f32[2,128,128]{2,1,0:T(8,128)S(1)}, f32[2,128,128]{2,1,0:T(8,128)S(1)}, u32[]{:S(2)}, u32[]{:S(2)}) %collective-permute-start.13) | collective-permute-done | bytes 131104 | tf_op jit(solution)/shard_map/ppermute | solution.py:308
  18.7 1.6 %collective-permute-start.14 = (f32[2,128,128]{2,1,0:T(8,128)S(1)}, f32[2,128,128]{2,1,0:T(8,128)S(1)}, u32[]{:S(2)}, u32[]{:S(2)}) collective-permute-start(f32[2,128,128]{2,1,0:T(8,128)S(1)} %multiply_add_fusion.14), channel_id=1, source_target_pairs={{0,8},{1,9},{2,10},{3,11},{4,12},{5,13},{6,14},{7,15},{8,0},{9,1},... | collective-permute-start | bytes 393224 | tf_op jit(solution)/shard_map/ppermute | solution.py:323
  20.9 1.6 %collective-permute-start.6 = (f32[2,128,128]{2,1,0:T(8,128)S(1)}, f32[2,128,128]{2,1,0:T(8,128)S(1)}, u32[]{:S(2)}, u32[]{:S(2)}) collective-permute-start(f32[2,128,128]{2,1,0:T(8,128)S(1)} %multiply_add_fusion.20), channel_id=1, source_target_pairs={{0,8},{1,9},{2,10},{3,11},{4,12},{5,13},{6,14},{7,15},{8,0},{9,1},... | collective-permute-start | bytes 393224 | tf_op jit(solution)/shard_map/ppermute | solution.py:323
  22.7 2.5 %collective-permute-done.14 = f32[2,128,128]{2,1,0:T(8,128)S(1)} collective-permute-done((f32[2,128,128]{2,1,0:T(8,128)S(1)}, f32[2,128,128]{2,1,0:T(8,128)S(1)}, u32[]{:S(2)}, u32[]{:S(2)}) %collective-permute-start.14) | collective-permute-done | bytes 131104 | tf_op jit(solution)/shard_map/ppermute | solution.py:323
  25.3 1.8 %collective-permute-done.10 = f32[2,128,128]{2,1,0:T(8,128)S(1)} collective-permute-done((f32[2,128,128]{2,1,0:T(8,128)S(1)}, f32[2,128,128]{2,1,0:T(8,128)S(1)}, u32[]{:S(2)}, u32[]{:S(2)}) %collective-permute-start.10) | collective-permute-done | bytes 131104 | tf_op jit(solution)/shard_map/ppermute | solution.py:323
  27.2 1.3 %collective-permute-done.6 = f32[2,128,128]{2,1,0:T(8,128)S(1)} collective-permute-done((f32[2,128,128]{2,1,0:T(8,128)S(1)}, f32[2,128,128]{2,1,0:T(8,128)S(1)}, u32[]{:S(2)}, u32[]{:S(2)}) %collective-permute-start.6) | collective-permute-done | bytes 131104 | tf_op jit(solution)/shard_map/ppermute | solution.py:323
  36.7 5.6 %collective-permute-done.19.refs_9_.refs_8_ = f32[2,128,128]{2,1,0:T(8,128)S(1)} collective-permute-done((f32[2,128,128]{2,1,0:T(8,128)S(1)}, f32[2,128,128]{2,1,0:T(8,128)S(1)}, u32[]{:S(2)}, u32[]{:S(2)}) %collective-permute-start.19) | collective-permute-done | bytes 131104 | tf_op jit(solution)/shard_map/ppermute | solution.py:339
  42.3 2.2 %collective-permute-done.18.refs_8_.refs_9_ = f32[2,128,128]{2,1,0:T(8,128)S(1)} collective-permute-done((f32[2,128,128]{2,1,0:T(8,128)S(1)}, f32[2,128,128]{2,1,0:T(8,128)S(1)}, u32[]{:S(2)}, u32[]{:S(2)}) %collective-permute-start.18) | collective-permute-done | bytes 131104 | tf_op jit(solution)/shard_map/ppermute | solution.py:339
  58.3 6.0 %collective-permute-done.44 = f32[16,128]{1,0:T(8,128)S(1)} collective-permute-done((f32[16,128]{1,0:T(8,128)S(1)}, f32[16,128]{1,0:T(8,128)S(1)}, u32[]{:S(2)}, u32[]{:S(2)}) %collective-permute-start.44) | collective-permute-done | bytes 8224 | tf_op jit(solution)/shard_map/ppermute | solution.py:477
  64.3 5.8 %collective-permute-start.45 = (f32[16,128]{1,0:T(8,128)S(1)}, f32[16,128]{1,0:T(8,128)S(1)}, u32[]{:S(2)}, u32[]{:S(2)}) collective-permute-start(f32[16,128]{1,0:T(8,128)S(1)} %fusion.18), channel_id=1, source_target_pairs={{0,8},{4,12},{8,0},{12,4},{16,24},{20,28},{24,16},{28,20},{1,9},{5... | collective-permute-start | bytes 24584 | tf_op jit(solution)/shard_map/ppermute | solution.py:477
  71.7 3.2 %collective-permute-start.46 = (f32[16,128]{1,0:T(8,128)S(1)}, f32[16,128]{1,0:T(8,128)S(1)}, u32[]{:S(2)}, u32[]{:S(2)}) collective-permute-start(f32[16,128]{1,0:T(8,128)S(1)} %add.138), channel_id=1, source_target_pairs={{0,16},{4,20},{8,24},{12,28},{16,0},{20,4},{24,8},{28,12},{1,17},{... | collective-permute-start | bytes 24584 | tf_op jit(solution)/shard_map/ppermute | solution.py:477
  80.0 11.9 %collective-permute-start.27 = (f32[2,128,128]{2,1,0:T(8,128)S(1)}, f32[2,128,128]{2,1,0:T(8,128)S(1)}, u32[]{:S(2)}, u32[]{:S(2)}) collective-permute-start(f32[2,128,128]{2,1,0:T(8,128)S(1)} %multiply_add_fusion.9), channel_id=1, source_target_pairs={{0,8},{1,9},{2,10},{3,11},{4,12},{5,13},{6,14},{7,15},{8,0},{9,1},... | collective-permute-start | bytes 393224 | tf_op jit(solution)/shard_map/ppermute | solution.py:323
  93.0 1.4 %collective-permute-start.37 = (f32[2,128,128]{2,1,0:T(8,128)S(1)}, f32[2,128,128]{2,1,0:T(8,128)S(1)}, u32[]{:S(2)}, u32[]{:S(2)}) collective-permute-start(f32[2,128,128]{2,1,0:T(8,128)S(1)} %multiply_add_fusion.3), channel_id=1, source_target_pairs={{0,8},{1,9},{2,10},{3,11},{4,12},{5,13},{6,14},{7,15},{8,0},{9,1},... | collective-permute-start | bytes 393224 | tf_op jit(solution)/shard_map/ppermute | solution.py:323
  94.4 1.4 %collective-permute-start.32 = (f32[2,128,128]{2,1,0:T(8,128)S(1)}, f32[2,128,128]{2,1,0:T(8,128)S(1)}, u32[]{:S(2)}, u32[]{:S(2)}) collective-permute-start(f32[2,128,128]{2,1,0:T(8,128)S(1)} %multiply_add_fusion.6), channel_id=1, source_target_pairs={{0,8},{1,9},{2,10},{3,11},{4,12},{5,13},{6,14},{7,15},{8,0},{9,1},... | collective-permute-start | bytes 393224 | tf_op jit(solution)/shard_map/ppermute | solution.py:323
  97.3 3.0 %collective-permute-done.32 = f32[2,128,128]{2,1,0:T(8,128)S(1)} collective-permute-done((f32[2,128,128]{2,1,0:T(8,128)S(1)}, f32[2,128,128]{2,1,0:T(8,128)S(1)}, u32[]{:S(2)}, u32[]{:S(2)}) %collective-permute-start.32) | collective-permute-done | bytes 131104 | tf_op jit(solution)/shard_map/ppermute | solution.py:323
  103.7 1.4 %shard_map.110 = (bf16[128,2048]{1,0:T(8,128)(2,1)}, bf16[128,2048]{1,0:T(8,128)(2,1)}) custom-call(s32[1]{0:T(128)} %bitcast.place_ref, bf16[128,2048]{1,0:T(8,128)(2,1)S(1)} %copy-done.1, bf16[128,2048]{1,0:T(8,128)(2,1)S(1)} %copy-done.2, f32[128,16]{1,0:T(8,128)S(1)} %get-tuple-element.75.cum_t_ref.refs_3_.refs_2_, ...), custom_call_target="tpu_custom_call" | custom-call | flops 134217728 | bytes 2621440 | tf_op jit(solution)/shard_map/pallas_call | solution.py:24
  105.1 2.1 %collective-permute-done.38.refs_9_ = f32[2,128,128]{2,1,0:T(8,128)S(1)} collective-permute-done((f32[2,128,128]{2,1,0:T(8,128)S(1)}, f32[2,128,128]{2,1,0:T(8,128)S(1)}, u32[]{:S(2)}, u32[]{:S(2)}) %collective-permute-start.38) | collective-permute-done | bytes 131104 | tf_op jit(solution)/shard_map/ppermute | solution.py:339
  107.2 1.4 %collective-permute-done.33.refs_8_ = f32[2,128,128]{2,1,0:T(8,128)S(1)} collective-permute-done((f32[2,128,128]{2,1,0:T(8,128)S(1)}, f32[2,128,128]{2,1,0:T(8,128)S(1)}, u32[]{:S(2)}, u32[]{:S(2)}) %collective-permute-start.33) | collective-permute-done | bytes 131104 | tf_op jit(solution)/shard_map/ppermute | solution.py:339
  108.6 1.3 %shard_map.111 = (bf16[128,2048]{1,0:T(8,128)(2,1)}, bf16[128,2048]{1,0:T(8,128)(2,1)}, bf16[128,2048]{1,0:T(8,128)(2,1)}) custom-call(s32[1]{0:T(128)} %bitcast.place_ref, bf16[128,2048]{1,0:T(8,128)(2,1)S(1)} %copy-done.1, bf16[128,2048]{1,0:T(8,128)(2,1)S(1)} %copy-done.2, ...), custom_call_target="tpu_custom_call", output_to_operand_aliasing={{0}: (15, {}), {1}: (16, {})} | custom-call | flops 100663296 | bytes 1966080 | tf_op jit(solution)/shard_map/pallas_call | solution.py:24
  (147 shorter events, 40.8 us)
Async XLA Ops:
  2.3 11.4 %collective-permute-start = (f32[16,128]{1,0:T(8,128)S(1)}, f32[16,128]{1,0:T(8,128)S(1)}, u32[]{:S(2)}, u32[]{:S(2)}) collective-permute-start(f32[16,128]{1,0:T(8,128)S(1)} %get-tuple-element.83), channel_id=1, source_target_pairs={{0,4},{4,0},{8,12},{12,8},{16,20},{20,16},{24,28},{28,24},{1,5},{5... | collective-permute-start | bytes 24584 | tf_op jit(solution)/shard_map/ppermute | solution.py:386
  5.3 8.4 %collective-permute-start.1 = (f32[2,128,128]{2,1,0:T(8,128)S(1)}, f32[2,128,128]{2,1,0:T(8,128)S(1)}, u32[]{:S(2)}, u32[]{:S(2)}) collective-permute-start(f32[2,128,128]{2,1,0:T(8,128)S(1)} %get-tuple-element.85), channel_id=1, source_target_pairs={{0,4},{4,0},{8,12},{12,8},{16,20},{20,16},{24,28},{28,24},{1,5},{5... | collective-permute-start | bytes 393224 | tf_op jit(solution)/shard_map/ppermute | solution.py:308
  6.0 15.0 %collective-permute-start.5 = (f32[2,128,128]{2,1,0:T(8,128)S(1)}, f32[2,128,128]{2,1,0:T(8,128)S(1)}, u32[]{:S(2)}, u32[]{:S(2)}) collective-permute-start(f32[2,128,128]{2,1,0:T(8,128)S(1)} %get-tuple-element.87), channel_id=1, source_target_pairs={{0,4},{4,0},{8,12},{12,8},{16,20},{20,16},{24,28},{28,24},{1,5},{5... | collective-permute-start | bytes 393224 | tf_op jit(solution)/shard_map/ppermute | solution.py:308
  8.0 12.4 %collective-permute-start.9 = (f32[2,128,128]{2,1,0:T(8,128)S(1)}, f32[2,128,128]{2,1,0:T(8,128)S(1)}, u32[]{:S(2)}, u32[]{:S(2)}) collective-permute-start(f32[2,128,128]{2,1,0:T(8,128)S(1)} %get-tuple-element.90), channel_id=1, source_target_pairs={{0,4},{4,0},{8,12},{12,8},{16,20},{20,16},{24,28},{28,24},{1,5},{5... | collective-permute-start | bytes 393224 | tf_op jit(solution)/shard_map/ppermute | solution.py:308
  8.0 10.7 %collective-permute-start.13 = (f32[2,128,128]{2,1,0:T(8,128)S(1)}, f32[2,128,128]{2,1,0:T(8,128)S(1)}, u32[]{:S(2)}, u32[]{:S(2)}) collective-permute-start(f32[2,128,128]{2,1,0:T(8,128)S(1)} %get-tuple-element.93), channel_id=1, source_target_pairs={{0,4},{4,0},{8,12},{12,8},{16,20},{20,16},{24,28},{28,24},{1,5},{5... | collective-permute-start | bytes 393224 | tf_op jit(solution)/shard_map/ppermute | solution.py:308
  13.8 8.8 %collective-permute-start.2 = (f32[2,128,128]{2,1,0:T(8,128)S(1)}, f32[2,128,128]{2,1,0:T(8,128)S(1)}, u32[]{:S(2)}, u32[]{:S(2)}) collective-permute-start(f32[2,128,128]{2,1,0:T(8,128)S(1)} %multiply_add_fusion.23), channel_id=1, source_target_pairs={{0,8},{1,9},{2,10},{3,11},{4,12},{5,13},{6,14},{7,15},{8,0},{9,1},... | collective-permute-start | bytes 393224 | tf_op jit(solution)/shard_map/ppermute | solution.py:323
  20.9 7.6 %collective-permute-start.6 = (f32[2,128,128]{2,1,0:T(8,128)S(1)}, f32[2,128,128]{2,1,0:T(8,128)S(1)}, u32[]{:S(2)}, u32[]{:S(2)}) collective-permute-start(f32[2,128,128]{2,1,0:T(8,128)S(1)} %multiply_add_fusion.20), channel_id=1, source_target_pairs={{0,8},{1,9},{2,10},{3,11},{4,12},{5,13},{6,14},{7,15},{8,0},{9,1},... | collective-permute-start | bytes 393224 | tf_op jit(solution)/shard_map/ppermute | solution.py:323
  31.6 13.2 %collective-permute-start.20 = (f32[2,128,128]{2,1,0:T(8,128)S(1)}, f32[2,128,128]{2,1,0:T(8,128)S(1)}, u32[]{:S(2)}, u32[]{:S(2)}) collective-permute-start(f32[2,128,128]{2,1,0:T(8,128)S(1)} %get-tuple-element.154), channel_id=1, source_target_pairs={{0,4},{4,0},{8,12},{12,8},{16,20},{20,16},{24,28},{28,24},{1,5},{5... | collective-permute-start | bytes 393224 | tf_op jit(solution)/shard_map/ppermute | solution.py:339
  32.6 9.7 %collective-permute-start.19 = (f32[2,128,128]{2,1,0:T(8,128)S(1)}, f32[2,128,128]{2,1,0:T(8,128)S(1)}, u32[]{:S(2)}, u32[]{:S(2)}) collective-permute-start(f32[2,128,128]{2,1,0:T(8,128)S(1)} %get-tuple-element.98), channel_id=1, source_target_pairs={{0,4},{4,0},{8,12},{12,8},{16,20},{20,16},{24,28},{28,24},{1,5},{5... | collective-permute-start | bytes 393224 | tf_op jit(solution)/shard_map/ppermute | solution.py:339
  33.7 10.8 %collective-permute-start.18 = (f32[2,128,128]{2,1,0:T(8,128)S(1)}, f32[2,128,128]{2,1,0:T(8,128)S(1)}, u32[]{:S(2)}, u32[]{:S(2)}) collective-permute-start(f32[2,128,128]{2,1,0:T(8,128)S(1)} %get-tuple-element.97), channel_id=1, source_target_pairs={{0,4},{4,0},{8,12},{12,8},{16,20},{20,16},{24,28},{28,24},{1,5},{5... | collective-permute-start | bytes 393224 | tf_op jit(solution)/shard_map/ppermute | solution.py:339
  50.1 27.9 %collective-permute-start.29 = (f32[2,128,128]{2,1,0:T(8,128)S(1)}, f32[2,128,128]{2,1,0:T(8,128)S(1)}, u32[]{:S(2)}, u32[]{:S(2)}) collective-permute-start(f32[2,128,128]{2,1,0:T(8,128)S(1)} %get-tuple-element.116), channel_id=1, source_target_pairs={{0,4},{4,0},{8,12},{12,8},{16,20},{20,16},{24,28},{28,24},{1,5},{5... | collective-permute-start | bytes 393224 | tf_op jit(solution)/shard_map/ppermute | solution.py:308
  51.1 26.7 %collective-permute-start.34 = (f32[2,128,128]{2,1,0:T(8,128)S(1)}, f32[2,128,128]{2,1,0:T(8,128)S(1)}, u32[]{:S(2)}, u32[]{:S(2)}) collective-permute-start(f32[2,128,128]{2,1,0:T(8,128)S(1)} %get-tuple-element.120), channel_id=1, source_target_pairs={{0,4},{4,0},{8,12},{12,8},{16,20},{20,16},{24,28},{28,24},{1,5},{5... | collective-permute-start | bytes 393224 | tf_op jit(solution)/shard_map/ppermute | solution.py:308
  52.2 25.1 %collective-permute-start.39 = (f32[2,128,128]{2,1,0:T(8,128)S(1)}, f32[2,128,128]{2,1,0:T(8,128)S(1)}, u32[]{:S(2)}, u32[]{:S(2)}) collective-permute-start(f32[2,128,128]{2,1,0:T(8,128)S(1)} %get-tuple-element.134), channel_id=1, source_target_pairs={{0,4},{4,0},{8,12},{12,8},{16,20},{20,16},{24,28},{28,24},{1,5},{5... | collective-permute-start | bytes 393224 | tf_op jit(solution)/shard_map/ppermute | solution.py:308
  53.5 23.6 %collective-permute-start.24 = (f32[2,128,128]{2,1,0:T(8,128)S(1)}, f32[2,128,128]{2,1,0:T(8,128)S(1)}, u32[]{:S(2)}, u32[]{:S(2)}) collective-permute-start(f32[2,128,128]{2,1,0:T(8,128)S(1)} %get-tuple-element.113), channel_id=1, source_target_pairs={{0,4},{4,0},{8,12},{12,8},{16,20},{20,16},{24,28},{28,24},{1,5},{5... | collective-permute-start | bytes 393224 | tf_op jit(solution)/shard_map/ppermute | solution.py:308
  55.6 8.7 %collective-permute-start.44 = (f32[16,128]{1,0:T(8,128)S(1)}, f32[16,128]{1,0:T(8,128)S(1)}, u32[]{:S(2)}, u32[]{:S(2)}) collective-permute-start(f32[16,128]{1,0:T(8,128)S(1)} %pad_maximum_fusion), channel_id=1, source_target_pairs={{0,4},{4,0},{8,12},{12,8},{16,20},{20,16},{24,28},{28,24},{1,5},{5... | collective-permute-start | bytes 24584 | tf_op jit(solution)/shard_map/ppermute | solution.py:477
  64.3 7.4 %collective-permute-start.45 = (f32[16,128]{1,0:T(8,128)S(1)}, f32[16,128]{1,0:T(8,128)S(1)}, u32[]{:S(2)}, u32[]{:S(2)}) collective-permute-start(f32[16,128]{1,0:T(8,128)S(1)} %fusion.18), channel_id=1, source_target_pairs={{0,8},{4,12},{8,0},{12,4},{16,24},{20,28},{24,16},{28,20},{1,9},{5... | collective-permute-start | bytes 24584 | tf_op jit(solution)/shard_map/ppermute | solution.py:477
  78.8 13.1 %collective-permute-start.41 = (f32[2,128,128]{2,1,0:T(8,128)S(1)}, f32[2,128,128]{2,1,0:T(8,128)S(1)}, u32[]{:S(2)}, u32[]{:S(2)}) collective-permute-start(f32[2,128,128]{2,1,0:T(8,128)S(1)} %multiply_add_fusion.1), channel_id=1, source_target_pairs={{0,1},{1,0},{2,3},{3,2},{4,5},{5,4},{6,7},{7,6},{8,16},{9,17},{10,... | collective-permute-start | bytes 393224 | tf_op jit(solution)/shard_map/ppermute | solution.py:323
  79.3 13.7 %collective-permute-start.36 = (f32[2,128,128]{2,1,0:T(8,128)S(1)}, f32[2,128,128]{2,1,0:T(8,128)S(1)}, u32[]{:S(2)}, u32[]{:S(2)}) collective-permute-start(f32[2,128,128]{2,1,0:T(8,128)S(1)} %multiply_add_fusion.4), channel_id=1, source_target_pairs={{0,1},{1,0},{2,3},{3,2},{4,5},{5,4},{6,7},{7,6},{8,16},{9,17},{10,... | collective-permute-start | bytes 393224 | tf_op jit(solution)/shard_map/ppermute | solution.py:323
  79.5 14.9 %collective-permute-start.31 = (f32[2,128,128]{2,1,0:T(8,128)S(1)}, f32[2,128,128]{2,1,0:T(8,128)S(1)}, u32[]{:S(2)}, u32[]{:S(2)}) collective-permute-start(f32[2,128,128]{2,1,0:T(8,128)S(1)} %multiply_add_fusion.7), channel_id=1, source_target_pairs={{0,1},{1,0},{2,3},{3,2},{4,5},{5,4},{6,7},{7,6},{8,16},{9,17},{10,... | collective-permute-start | bytes 393224 | tf_op jit(solution)/shard_map/ppermute | solution.py:323
  80.0 16.0 %collective-permute-start.27 = (f32[2,128,128]{2,1,0:T(8,128)S(1)}, f32[2,128,128]{2,1,0:T(8,128)S(1)}, u32[]{:S(2)}, u32[]{:S(2)}) collective-permute-start(f32[2,128,128]{2,1,0:T(8,128)S(1)} %multiply_add_fusion.9), channel_id=1, source_target_pairs={{0,8},{1,9},{2,10},{3,11},{4,12},{5,13},{6,14},{7,15},{8,0},{9,1},... | collective-permute-start | bytes 393224 | tf_op jit(solution)/shard_map/ppermute | solution.py:323
  91.9 8.5 %collective-permute-start.42 = (f32[2,128,128]{2,1,0:T(8,128)S(1)}, f32[2,128,128]{2,1,0:T(8,128)S(1)}, u32[]{:S(2)}, u32[]{:S(2)}) collective-permute-start(f32[2,128,128]{2,1,0:T(8,128)S(1)} %multiply_add_fusion), channel_id=1, source_target_pairs={{0,8},{1,9},{2,10},{3,11},{4,12},{5,13},{6,14},{7,15},{8,0},{9,1},... | collective-permute-start | bytes 393224 | tf_op jit(solution)/shard_map/ppermute | solution.py:323
  93.0 7.3 %collective-permute-start.37 = (f32[2,128,128]{2,1,0:T(8,128)S(1)}, f32[2,128,128]{2,1,0:T(8,128)S(1)}, u32[]{:S(2)}, u32[]{:S(2)}) collective-permute-start(f32[2,128,128]{2,1,0:T(8,128)S(1)} %multiply_add_fusion.3), channel_id=1, source_target_pairs={{0,8},{1,9},{2,10},{3,11},{4,12},{5,13},{6,14},{7,15},{8,0},{9,1},... | collective-permute-start | bytes 393224 | tf_op jit(solution)/shard_map/ppermute | solution.py:323
  96.1 9.0 %collective-permute-start.28 = (f32[2,128,128]{2,1,0:T(8,128)S(1)}, f32[2,128,128]{2,1,0:T(8,128)S(1)}, u32[]{:S(2)}, u32[]{:S(2)}) collective-permute-start(f32[2,128,128]{2,1,0:T(8,128)S(1)} %fusion.9), channel_id=1, source_target_pairs={{0,4},{4,0},{8,12},{12,8},{16,20},{20,16},{24,28},{28,24},{1,5},{5... | collective-permute-start | bytes 393224 | tf_op jit(solution)/shard_map/ppermute | solution.py:339
  100.5 9.4 %collective-permute-start.43 = (f32[2,128,128]{2,1,0:T(8,128)S(1)}, f32[2,128,128]{2,1,0:T(8,128)S(1)}, u32[]{:S(2)}, u32[]{:S(2)}) collective-permute-start(f32[2,128,128]{2,1,0:T(8,128)S(1)} %get-tuple-element.146), channel_id=1, source_target_pairs={{0,4},{4,0},{8,12},{12,8},{16,20},{20,16},{24,28},{28,24},{1,5},{5... | collective-permute-start | bytes 393224 | tf_op jit(solution)/shard_map/ppermute | solution.py:339
  (28 other events, 95.6 us)
